TPU v7x, 128 devices: a whole 4x4x4 slice. The times are simulated.
128 devices in a mesh: slab: 64 (over y, z, x), blk: 2 (over core).
Axes of the slice: x: 4, y: 4, z: 4, core: 2. Of those that a mesh axis runs over, the one named last changes fastest.
Arguments:
- p_blocks: bfloat16 [2, 2048, 64, 64], P('blk', 'slab'), may hold values from -0.75 to 0.75
- basis_vals: bfloat16 [512, 8, 64, 128], P('slab'), may hold values from -0.75 to 0.75
- need_list: int32 [2, 64, 64, 4], P('blk', 'slab'), may hold values from 0 to 31, as said below
- tasks: int32 [2, 64, 4, 1536], P('blk', 'slab'), may hold values from 0 to 255, as said below
- task_counts: int32 [2, 64], P('blk', 'slab'), may hold values from 1 to 1536, as said below
Outputs:
- density: float32 [512, 128], P('slab')
- potential_blocks: float32 [2, 2048, 64, 64], P('blk', 'slab')
Inputs may be any that keep to these rules, and one draw needn't show every extreme that they name: The 4 entries of one need_list[c, s, o, :] are distinct. `tasks`: field 0 is below 8, fields 1 and 2 below 8, field 3 below 256. `task_counts`: some device has 1536 live tasks.
All inputs are finite; a program needn't handle non-finite values.
Results may differ from a plain program's by a relative error of at most 0.0029.
Values may be sent and summed in bfloat16 or wider, within the bound.
No kernel may reach another device: no remote copies, remote signals or barrier semaphores. Data moves between devices by JAX's collectives and lax.ppermute only.
A program may use at most 128 MiB of HBM per device.

v0:
```python
import jax
import jax.numpy as jnp
from jax import lax
from jax.sharding import PartitionSpec as P


def body(p_blocks, basis_vals, need_list, tasks, task_counts):
    slabs = lax.axis_size("slab")
    owned_blocks = p_blocks[0]
    blk_dev = owned_blocks.shape[0]
    block_size = owned_blocks.shape[1]
    wanted_ids = need_list[0, 0]
    capacity = wanted_ids.shape[1]
    requested = lax.all_to_all(wanted_ids, "slab", split_axis=0, concat_axis=0, tiled=True)
    column_all = lax.all_gather(owned_blocks, "slab", axis=0, tiled=True)
    offsets = jnp.arange(slabs, dtype=jnp.int32)[:, None] * blk_dev
    global_ids = (offsets + wanted_ids).reshape(-1)
    received = column_all[global_ids]
    task_fields = tasks[0, 0]
    live_count = task_counts[0, 0]
    nbat_local = basis_vals.shape[0]
    grid_coordinates = basis_vals.shape[3]
    task_slots = task_fields.shape[1]
    tile_rows = min(256, task_slots)
    tile_count = task_slots // tile_rows
    batch_range = jnp.arange(nbat_local, dtype=jnp.int32)

    def tile_terms(tile_index):
        fields_tile = lax.dynamic_slice_in_dim(task_fields, tile_index * tile_rows, tile_rows, 1)
        grid_batch_index = fields_tile[0]
        live_mask = (
            tile_index * tile_rows + jnp.arange(tile_rows, dtype=jnp.int32) < live_count
        ).astype(jnp.float32)
        left_vals = basis_vals[grid_batch_index, fields_tile[1]]
        right_side_values = basis_vals[grid_batch_index, fields_tile[2]]
        return (grid_batch_index, fields_tile[3], live_mask, left_vals, right_side_values)

    def density_tile(total, tile_index):
        grid_batch_index, slot_ids, live_mask, left_vals, right_side_values = tile_terms(tile_index)
        selected_entries = received[slot_ids]
        mapped_result = jnp.einsum(
            "zhf,zfx->zhx", selected_entries, right_side_values, preferred_element_type=jnp.float32
        )
        contrib = (
            jnp.sum(left_vals.astype(jnp.float32) * mapped_result, axis=1) * live_mask[:, None]
        )
        one_hot = (grid_batch_index[:, None] == batch_range[None, :]).astype(jnp.float32)
        added = jnp.dot(
            one_hot.T, contrib, precision=lax.Precision.HIGHEST, preferred_element_type=jnp.float32
        )
        return (total + added, None)

    tile_ids = jnp.arange(tile_count, dtype=jnp.int32)
    partial_density, _ = lax.scan(
        density_tile, jnp.zeros((nbat_local, grid_coordinates), jnp.float32), tile_ids
    )
    density = lax.psum(partial_density, "blk")
    potential = density / jnp.sqrt(1.0 + density * density)

    def potential_tile(slot_sums, tile_index):
        grid_batch_index, slot_ids, live_mask, left_vals, right_side_values = tile_terms(tile_index)
        weight_applied = (
            left_vals.astype(jnp.float32) * potential[grid_batch_index][:, None, :]
        ).astype(jnp.bfloat16)
        incomplete_sum_terms = jnp.einsum(
            "lkf,lgf->lkg", weight_applied, right_side_values, preferred_element_type=jnp.float32
        )
        incomplete_sum_terms = incomplete_sum_terms * live_mask[:, None, None]
        return (slot_sums.at[slot_ids].add(incomplete_sum_terms), None)

    slot_start = jnp.zeros((slabs * capacity, block_size, block_size), jnp.float32)
    slot_sums, _ = lax.scan(potential_tile, slot_start, tile_ids)
    returned = lax.all_to_all(
        slot_sums.reshape(slabs, capacity, block_size, block_size),
        "slab",
        split_axis=0,
        concat_axis=0,
        tiled=True,
    )
    owner_sums = jnp.zeros((blk_dev, block_size, block_size), jnp.float32)
    owner_sums = owner_sums.at[requested.reshape(-1)].add(
        returned.reshape(slabs * capacity, block_size, block_size)
    )
    return (density, owner_sums[None])


def solution(mesh):
    in_specs = (
        P("blk", "slab", None, None),
        P("slab", None, None, None),
        P("blk", "slab", None, None),
        P("blk", "slab", None, None),
        P("blk", "slab"),
    )
    out_specs = (P("slab", None), P("blk", "slab", None, None))
    return jax.shard_map(body, mesh=mesh, in_specs=in_specs, out_specs=out_specs, check_vma=False)
```

profile of v0, /device:TPU:0, one launch (start us, length us, event | category | flops | bytes accessed | tf_op | source)
XLA Modules:
  0.0 798.4 jit_solution(16260203998572006986)
XLA Ops:
  9.3 11.5 %all-to-all-start = ((s32[64,1,4]{2,1,0:T(1,128)}), s32[64,1,4]{2,1,0:T(1,128)S(1)}, u32[]{:S(2)}, u32[]{:S(2)}) async-start(s32[64,1,4]{2,1,0:T(1,128)} %bitcast.14), calls=%async_computation | async-start | bytes 65536 | tf_op jit(solution)/shard_map/all_to_all | solution.py:14
  21.9 152.0 %all-gather.3.cloned.1.call-done = bf16[1,2048,64,64]{3,2,0,1:T(8,128)(2,1)} async-done(((bf16[1,32,64,64]{3,2,0,1:T(8,128)(2,1)}), bf16[1,2048,64,64]{3,2,0,1:T(8,128)(2,1)}) %all-gather.3.cloned.1.call-update) | async-done | bytes 16777232 | tf_op jit(solution)/shard_map/all_gather | solution.py:15
  179.0 130.2 %while.22 = (s32[]{:T(128)}, f32[8,128]{1,0:T(8,128)S(1)}, s32[6]{0:T(128)S(1)}, s32[4,1536]{1,0:T(4,128)}, bf16[8,8,64,128]{3,2,1,0:T(8,128)(2,1)S(1)}, /*index...) while((s32[]{:T(128)}, f32[8,128]{1,0:T(8,128)S(1)}, ...), condition=%wide.region_2.3_spmd.clone, body=%wide.region_0.2_spmd.clone.sunk | while | flops 277883648 | bytes 31750408 | solution.py:54
  193.1 5.9 multiply_reduce_fusion.2
  279.9 5.9 multiply_reduce_fusion.2
  316.0 352.7 %while.21 = (s32[]{:T(128)}, f32[256,64,64]{2,1,0:T(8,128)}, s32[6]{0:T(128)S(1)}, s32[4,1536]{1,0:T(4,128)}, bf16[8,8,64,128]{3,2,1,0:T(8,128)(2,1)S(1)}, /*ind...) while((s32[]{:T(128)}, f32[256,64,64]{2,1,0:T(8,128)}, ...), condition=%wide.region_6.7_spmd, body=%wide.region_4.6_spmd.sunk | while | flops 276830976 | bytes 42358008 | solution.py:72
  326.3 9.0 %broadcast_multiply_fusion.2 = f32[256,64,64]{2,1,0:T(8,128)} fusion(f32[256]{0:T(256)S(1)} %compare_convert_fusion.4, bf16[256,64,128]{2,1,0:T(8,128)(2,1)} %gather_fusion, bf16[256,64,128]{2,1,0:T(8,128)(2,1)} %gather_fusion.1, f32[256,128]{1,0:T(8,128)S(1)} %gather_fusion.2), kind=kOutput, calls=%fused_computation.12.clone.1 | convolution fusion | flops 275775488 | bytes 12715008 | tf_op jit(solution)/shard_map/while/body/eval_jaxpr/lkf,lgf->lkg/dot_general | solution.py:65
  335.4 39.4 %scatter_fusion = f32[256,64,64]{2,1,0:T(8,128)} fusion(f32[256,64,64]{2,1,0:T(8,128)} %get-tuple-element.301, s32[256]{0:T(256)S(1)} %bitcast.104, f32[256,64,64]{2,1,0:T(8,128)} %broadcast_multiply_fusion.2), kind=kCustom, calls=%fused_computation.7.clone.1 | custom fusion | flops 1048576 | bytes 12583936 | tf_op jit(solution)/shard_map/while/body/eval_jaxpr/scatter-add | solution.py:69
  385.1 9.0 %broadcast_multiply_fusion.2 = f32[256,64,64]{2,1,0:T(8,128)} fusion(f32[256]{0:T(256)S(1)} %compare_convert_fusion.4, bf16[256,64,128]{2,1,0:T(8,128)(2,1)} %gather_fusion, bf16[256,64,128]{2,1,0:T(8,128)(2,1)} %gather_fusion.1, f32[256,128]{1,0:T(8,128)S(1)} %gather_fusion.2), kind=kOutput, calls=%fused_computation.12.clone.1 | convolution fusion | flops 275775488 | bytes 12715008 | tf_op jit(solution)/shard_map/while/body/eval_jaxpr/lkf,lgf->lkg/dot_general | solution.py:65
  394.2 39.4 %scatter_fusion = f32[256,64,64]{2,1,0:T(8,128)} fusion(f32[256,64,64]{2,1,0:T(8,128)} %get-tuple-element.301, s32[256]{0:T(256)S(1)} %bitcast.104, f32[256,64,64]{2,1,0:T(8,128)} %broadcast_multiply_fusion.2), kind=kCustom, calls=%fused_computation.7.clone.1 | custom fusion | flops 1048576 | bytes 12583936 | tf_op jit(solution)/shard_map/while/body/eval_jaxpr/scatter-add | solution.py:69
  443.9 9.0 %broadcast_multiply_fusion.2 = f32[256,64,64]{2,1,0:T(8,128)} fusion(f32[256]{0:T(256)S(1)} %compare_convert_fusion.4, bf16[256,64,128]{2,1,0:T(8,128)(2,1)} %gather_fusion, bf16[256,64,128]{2,1,0:T(8,128)(2,1)} %gather_fusion.1, f32[256,128]{1,0:T(8,128)S(1)} %gather_fusion.2), kind=kOutput, calls=%fused_computation.12.clone.1 | convolution fusion | flops 275775488 | bytes 12715008 | tf_op jit(solution)/shard_map/while/body/eval_jaxpr/lkf,lgf->lkg/dot_general | solution.py:65
  452.9 39.4 %scatter_fusion = f32[256,64,64]{2,1,0:T(8,128)} fusion(f32[256,64,64]{2,1,0:T(8,128)} %get-tuple-element.301, s32[256]{0:T(256)S(1)} %bitcast.104, f32[256,64,64]{2,1,0:T(8,128)} %broadcast_multiply_fusion.2), kind=kCustom, calls=%fused_computation.7.clone.1 | custom fusion | flops 1048576 | bytes 12583936 | tf_op jit(solution)/shard_map/while/body/eval_jaxpr/scatter-add | solution.py:69
  502.7 9.0 %broadcast_multiply_fusion.2 = f32[256,64,64]{2,1,0:T(8,128)} fusion(f32[256]{0:T(256)S(1)} %compare_convert_fusion.4, bf16[256,64,128]{2,1,0:T(8,128)(2,1)} %gather_fusion, bf16[256,64,128]{2,1,0:T(8,128)(2,1)} %gather_fusion.1, f32[256,128]{1,0:T(8,128)S(1)} %gather_fusion.2), kind=kOutput, calls=%fused_computation.12.clone.1 | convolution fusion | flops 275775488 | bytes 12715008 | tf_op jit(solution)/shard_map/while/body/eval_jaxpr/lkf,lgf->lkg/dot_general | solution.py:65
  511.7 39.5 %scatter_fusion = f32[256,64,64]{2,1,0:T(8,128)} fusion(f32[256,64,64]{2,1,0:T(8,128)} %get-tuple-element.301, s32[256]{0:T(256)S(1)} %bitcast.104, f32[256,64,64]{2,1,0:T(8,128)} %broadcast_multiply_fusion.2), kind=kCustom, calls=%fused_computation.7.clone.1 | custom fusion | flops 1048576 | bytes 12583936 | tf_op jit(solution)/shard_map/while/body/eval_jaxpr/scatter-add | solution.py:69
  561.5 9.0 %broadcast_multiply_fusion.2 = f32[256,64,64]{2,1,0:T(8,128)} fusion(f32[256]{0:T(256)S(1)} %compare_convert_fusion.4, bf16[256,64,128]{2,1,0:T(8,128)(2,1)} %gather_fusion, bf16[256,64,128]{2,1,0:T(8,128)(2,1)} %gather_fusion.1, f32[256,128]{1,0:T(8,128)S(1)} %gather_fusion.2), kind=kOutput, calls=%fused_computation.12.clone.1 | convolution fusion | flops 275775488 | bytes 12715008 | tf_op jit(solution)/shard_map/while/body/eval_jaxpr/lkf,lgf->lkg/dot_general | solution.py:65
  570.5 39.5 %scatter_fusion = f32[256,64,64]{2,1,0:T(8,128)} fusion(f32[256,64,64]{2,1,0:T(8,128)} %get-tuple-element.301, s32[256]{0:T(256)S(1)} %bitcast.104, f32[256,64,64]{2,1,0:T(8,128)} %broadcast_multiply_fusion.2), kind=kCustom, calls=%fused_computation.7.clone.1 | custom fusion | flops 1048576 | bytes 12583936 | tf_op jit(solution)/shard_map/while/body/eval_jaxpr/scatter-add | solution.py:69
  620.4 9.0 %broadcast_multiply_fusion.2 = f32[256,64,64]{2,1,0:T(8,128)} fusion(f32[256]{0:T(256)S(1)} %compare_convert_fusion.4, bf16[256,64,128]{2,1,0:T(8,128)(2,1)} %gather_fusion, bf16[256,64,128]{2,1,0:T(8,128)(2,1)} %gather_fusion.1, f32[256,128]{1,0:T(8,128)S(1)} %gather_fusion.2), kind=kOutput, calls=%fused_computation.12.clone.1 | convolution fusion | flops 275775488 | bytes 12715008 | tf_op jit(solution)/shard_map/while/body/eval_jaxpr/lkf,lgf->lkg/dot_general | solution.py:65
  629.4 39.4 %scatter_fusion = f32[256,64,64]{2,1,0:T(8,128)} fusion(f32[256,64,64]{2,1,0:T(8,128)} %get-tuple-element.301, s32[256]{0:T(256)S(1)} %bitcast.104, f32[256,64,64]{2,1,0:T(8,128)} %broadcast_multiply_fusion.2), kind=kCustom, calls=%fused_computation.7.clone.1 | custom fusion | flops 1048576 | bytes 12583936 | tf_op jit(solution)/shard_map/while/body/eval_jaxpr/scatter-add | solution.py:69
  668.7 9.7 %reshape.408 = f32[64,1,16384]{2,1,0:T(1,128)} reshape(f32[64,4,64,64]{3,2,1,0:T(8,128)} %bitcast.99) | data formatting | bytes 8388608
  678.4 8.8 %all-to-all-start.1 = ((f32[64,1,16384]{2,1,0:T(1,128)}), f32[64,1,16384]{2,1,0:T(1,128)}, u32[]{:S(2)}, u32[]{:S(2)}) async-start(f32[64,1,16384]{2,1,0:T(1,128)} %reshape.408), calls=%async_computation.1 | async-start | bytes 8388608 | tf_op jit(solution)/shard_map/all_to_all | solution.py:73
  688.6 54.1 %all-to-all-done.1 = f32[64,1,16384]{2,1,0:T(1,128)} async-done(((f32[64,1,16384]{2,1,0:T(1,128)}), f32[64,1,16384]{2,1,0:T(1,128)}, u32[]{:S(2)}, u32[]{:S(2)}) %all-to-all-start.1) | async-done | bytes 4194336 | tf_op jit(solution)/shard_map/all_to_all | solution.py:73
  743.2 13.7 %reduce.4 = f32[64,16384]{1,0:T(8,128)} reduce(f32[64,1,16384]{2,1,0:T(1,128)} %all-to-all-done.1, f32[]{:T(128)} %broadcast.330), dimensions={1}, to_apply=%all_to_all.11.reduce_sub_computation | reduce | bytes 8388612 | tf_op jit(solution)/shard_map/all_to_all | solution.py:73
  757.0 7.4 reshape.409
  764.4 26.1 %scatter_fusion.1 = f32[32,64,64]{2,1,0:T(8,128)S(1)} fusion(f32[32,64,64]{2,1,0:T(8,128)S(1)} %broadcast_in_dim.9, s32[256]{0:T(256)S(1)} %bitcast.109, f32[256,64,64]{2,1,0:T(8,128)} %bitcast.101), kind=kCustom, calls=%fused_computation.8 | custom fusion | flops 1048576 | bytes 12583936 | tf_op jit(solution)/shard_map/scatter-add | solution.py:81
  (129 shorter events, 190.3 us)
Async XLA Ops:
  7.2 166.8 %all-gather.3.cloned.1.call-start = ((), (), s32[]{:S(2)}) async-start(), calls=%async_computation.2 | async-start | bytes 34078720 | tf_op jit(solution)/shard_map/all_gather | solution.py:15
  9.3 669.2 %all-to-all-start = ((s32[64,1,4]{2,1,0:T(1,128)}), s32[64,1,4]{2,1,0:T(1,128)S(1)}, u32[]{:S(2)}, u32[]{:S(2)}) async-start(s32[64,1,4]{2,1,0:T(1,128)} %bitcast.14), calls=%async_computation | async-start | bytes 65536 | tf_op jit(solution)/shard_map/all_to_all | solution.py:14
  174.0 5.0 copy-start
  311.7 4.3 copy-start.2
  678.4 64.3 %all-to-all-start.1 = ((f32[64,1,16384]{2,1,0:T(1,128)}), f32[64,1,16384]{2,1,0:T(1,128)}, u32[]{:S(2)}, u32[]{:S(2)}) async-start(f32[64,1,16384]{2,1,0:T(1,128)} %reshape.408), calls=%async_computation.1 | async-start | bytes 8388608 | tf_op jit(solution)/shard_map/all_to_all | solution.py:73
  790.6 1.0 copy-start.1
Sparse Core Ops, SparseCore 0:
  10.9 163.0 all-gather.2
where the time goes:
time: 804 us; the launch traced here: 798 us
  other arithmetic  296 us (37%)
  waiting for transfers between devices  207 us (26%)
  local copies, waits for them, and re-layouts  159 us (20%)
  matrix products  91.6 us (11%)
  starting transfers between devices  20.4 us (3%)
  between operations  14.1 us (2%)
  loops' own time  8.14 us (1%)
    scatter-add x6, other arithmetic, potential_tile(): return (slot_sums.at[slot_ids].add(incomplete_sum_terms), None)  237 us
    all_gather x1, waiting for transfers between devices, body(): column_all = lax.all_gather(owned_blocks, 'slab', axis=0, tiled=True)  152 us
    all_to_all x1, waiting for transfers between devices, body(): lax.all_to_all(slot_sums.reshape(slabs, capacity, block_size, block_size)...  54.1 us
    dot_general x6, matrix products, potential_tile(): jnp.einsum('lkf,lgf->lkg', weight_applied, right_side_values, preferred_e...  54.1 us
    gather x12, local copies, waits for them, and re-layouts, tile_terms(): right_side_values = basis_vals[grid_batch_index, fields_tile[2]]  40 us
    gather x12, local copies, waits for them, and re-layouts, tile_terms(): left_vals = basis_vals[grid_batch_index, fields_tile[1]]  40 us
    dot_general x6, matrix products, density_tile(): jnp.einsum('zhf,zfx->zhx', selected_entries, right_side_values, preferred...  35.5 us
    gather x6, local copies, waits for them, and re-layouts, density_tile(): selected_entries = received[slot_ids]  31.5 us
  transfers between devices with their start and end apart: 3, of which 2 were waited for; matrix products, arithmetic and copies ran while one was open for 62% of the time, Pallas kernels for 0%

commit v1 on v0

v1 whole, which is shorter than its diff:
```python
import functools

import jax
import jax.numpy as jnp
from jax import lax
from jax.experimental import pallas as pl
from jax.experimental.pallas import tpu as pltpu
from jax.sharding import PartitionSpec as P

F32 = jnp.float32
BF16 = jnp.bfloat16
LANES = 128
SUB = 8
CHUNK = 512


def dot_nn(a, b):
    return lax.dot_general(a, b, (((1,), (0,)), ((), ())), preferred_element_type=F32)


def dot_nt(a, b):
    return lax.dot_general(a, b, (((1,), (1,)), ((), ())), preferred_element_type=F32)


def dot_tn(a, b):
    return lax.dot_general(a, b, (((0,), (0,)), ((), ())), preferred_element_type=F32)


def split_pair(x):
    hi = x.astype(BF16)
    return hi, (x - hi.astype(F32)).astype(BF16)


def prep_kernel(count_ref, tasks_ref, v_ref, c_ref, ct_ref, v2_ref, flag_ref):
    nbat, kloc, bs, npt = v_ref.shape
    keys = nbat * kloc * kloc
    slots = c_ref.shape[2]
    tcap = tasks_ref.shape[1]
    step = CHUNK if tcap % CHUNK == 0 else tcap
    live = count_ref[0, 0]
    c = jnp.zeros((keys, slots), F32)
    ct = jnp.zeros((slots, keys), F32)
    for t in range(0, tcap, step):
        fields = tasks_ref[:, t : t + step]
        key = (fields[0:1] * kloc + fields[2:3]) * kloc + fields[1:2]
        lane = lax.broadcasted_iota(jnp.int32, (1, step), 1) + t
        key = jnp.where(lane < live, key, -1)
        key_hot = jnp.where(
            lax.broadcasted_iota(jnp.int32, (keys, step), 0) == key, 1.0, 0.0
        ).astype(BF16)
        slot_hot = jnp.where(
            lax.broadcasted_iota(jnp.int32, (slots, step), 0) == fields[3:4], 1.0, 0.0
        ).astype(BF16)
        c += dot_nt(key_hot, slot_hot)
        ct += dot_nt(slot_hot, key_hot)
    c_hi = jnp.floor(c * (1.0 / 256.0)) * 256.0
    ct_hi = jnp.floor(ct * (1.0 / 256.0)) * 256.0
    c_ref[0] = (c - c_hi).astype(BF16)
    c_ref[1] = c_hi.astype(BF16)
    ct_ref[0] = (ct - ct_hi).astype(BF16)
    ct_ref[1] = ct_hi.astype(BF16)
    flag_ref[0, 0] = jnp.where(jnp.max(c) > 255.5, 1, 0).astype(jnp.int32)
    half = bs // 2
    for b in range(nbat):
        vals = jnp.swapaxes(v_ref[b].astype(F32), 0, 1)
        for h in range(2):
            part = vals[h * half : (h + 1) * half].reshape(half * kloc, npt)
            v2_ref[b, :, h * npt : (h + 1) * npt] = part.astype(BF16)


def send_kernel(req_ref, own_ref, o_ref):
    nblk, bs, _ = own_ref.shape
    half = bs // 2
    slabs, _, cap, _ = o_ref.shape
    slots = slabs * cap
    own = own_ref[...].astype(F32)
    own = jnp.concatenate([own[:, :half], own[:, half:]], axis=2)
    own = jnp.swapaxes(own, 0, 1).astype(BF16)
    hot = jnp.where(
        lax.broadcasted_iota(jnp.int32, (nblk, slots), 0) == req_ref[...], 1.0, 0.0
    ).astype(BF16)
    for jp in range(half // 2):
        rhs = jnp.concatenate([own[2 * jp], own[2 * jp + 1]], axis=1)
        res = dot_tn(hot, rhs).astype(BF16)
        o_ref[:, 2 * jp] = res[:, :LANES].reshape(slabs, cap, LANES)
        o_ref[:, 2 * jp + 1] = res[:, LANES:].reshape(slabs, cap, LANES)


def fill_values(bd_ref, v_ref, b, kloc, bs):
    for l in range(kloc):
        v = v_ref[b, l]
        bd_ref[l * LANES : l * LANES + bs, 0:LANES] = v
        bd_ref[l * LANES + bs : (l + 1) * LANES, LANES:] = v


def density_kernel(flag_ref, r_ref, c_ref, v_ref, v2_ref, d_ref, res, hi_s, lo_s, bd):
    nbat, kloc, bs, npt = v_ref.shape
    half = bs // 2
    slabs, _, cap, _ = r_ref.shape
    slots = slabs * cap

    def build(jp, carry):
        r0 = r_ref[:, 2 * jp].reshape(slots, LANES)
        r1 = r_ref[:, 2 * jp + 1].reshape(slots, LANES)
        rhs = jnp.concatenate([r0, r1], axis=1)
        res[...] = dot_nn(c_ref[0], rhs)

        @pl.when(flag_ref[0, 0] > 0)
        def _():
            res[...] += dot_nn(c_ref[1], rhs)

        row = pl.multiple_of(jp * 2 * SUB, 2 * SUB)
        for b in range(nbat):
            for l in range(kloc):
                r = (b * kloc + l) * SUB
                x = jnp.concatenate(
                    [res[r : r + SUB, :LANES], res[r : r + SUB, LANES:]], axis=0
                )
                hi, lo = split_pair(x)
                hi_s[b, pl.ds(row, 2 * SUB), l * LANES : (l + 1) * LANES] = hi
                lo_s[b, pl.ds(row, 2 * SUB), l * LANES : (l + 1) * LANES] = lo
        return carry

    lax.fori_loop(0, half // 2, build, 0)
    bd[...] = jnp.zeros_like(bd)

    def one_batch(b, carry):
        fill_values(bd, v_ref, b, kloc, bs)
        values = bd[...]
        image = dot_nn(hi_s[b], values) + dot_nn(lo_s[b], values)
        d = jnp.sum(image * v2_ref[b].astype(F32), axis=0, keepdims=True)
        d_ref[pl.ds(b, 1), :] = d[:, :npt] + d[:, npt:]
        return carry

    lax.fori_loop(0, nbat, one_batch, 0)


def potential_kernel(flag_ref, d_ref, ct_ref, v_ref, v2_ref, o_ref, g, hi_s, lo_s, bd):
    nbat, kloc, bs, npt = v_ref.shape
    half = bs // 2
    slabs, _, cap, _ = o_ref.shape
    bd[...] = jnp.zeros_like(bd)

    def one_batch(b, carry):
        fill_values(bd, v_ref, b, kloc, bs)
        d = d_ref[pl.ds(b, 1), :]
        pot = d / jnp.sqrt(1.0 + d * d)
        pot2 = jnp.concatenate([pot, pot], axis=1)
        weighted = (v2_ref[b].astype(F32) * pot2).astype(BF16)
        g[...] = dot_nt(weighted, bd[...])
        for lp in range(kloc // 2):
            row = pl.multiple_of((b * kloc + 2 * lp) * SUB, 2 * SUB)
            for j in range(half):
                x = jnp.concatenate(
                    [
                        g[j * SUB : (j + 1) * SUB, 2 * lp * LANES : (2 * lp + 1) * LANES],
                        g[j * SUB : (j + 1) * SUB, (2 * lp + 1) * LANES : (2 * lp + 2) * LANES],
                    ],
                    axis=0,
                )
                hi, lo = split_pair(x)
                hi_s[pl.ds(row, 2 * SUB), j * LANES : (j + 1) * LANES] = hi
                lo_s[pl.ds(row, 2 * SUB), j * LANES : (j + 1) * LANES] = lo
        return carry

    lax.fori_loop(0, nbat, one_batch, 0)
    for jp in range(half // 2):
        cols = slice(2 * jp * LANES, (2 * jp + 2) * LANES)

        def sums(n):
            return dot_nn(ct_ref[n], hi_s[:, cols]) + dot_nn(ct_ref[n], lo_s[:, cols])

        out = lax.cond(flag_ref[0, 0] > 0, lambda: sums(0) + sums(1), lambda: sums(0))
        out = out.astype(BF16)
        o_ref[:, 2 * jp] = out[:, :LANES].reshape(slabs, cap, LANES)
        o_ref[:, 2 * jp + 1] = out[:, LANES:].reshape(slabs, cap, LANES)


def owner_kernel(req_ref, ret_ref, o_ref):
    nblk, bs, _ = o_ref.shape
    half = bs // 2
    slabs, _, cap, _ = ret_ref.shape
    slots = slabs * cap
    hot = jnp.where(
        lax.broadcasted_iota(jnp.int32, (nblk, slots), 0) == req_ref[...], 1.0, 0.0
    ).astype(BF16)
    parts = []
    for jp in range(half // 2):
        r0 = ret_ref[:, 2 * jp].reshape(slots, LANES)
        r1 = ret_ref[:, 2 * jp + 1].reshape(slots, LANES)
        res = dot_nn(hot, jnp.concatenate([r0, r1], axis=1))
        parts += [res[:, :LANES], res[:, LANES:]]
    sums = jnp.swapaxes(jnp.stack(parts, axis=0), 0, 1)
    o_ref[:, :half] = sums[:, :, :bs]
    o_ref[:, half:] = sums[:, :, bs:]


SMEM = pl.BlockSpec(memory_space=pltpu.SMEM)
VMEM = pl.BlockSpec(memory_space=pltpu.VMEM)


def body(p_blocks, basis_vals, need_list, tasks, task_counts):
    own = p_blocks[0]
    blk_dev, bs, _ = own.shape
    nbat, kloc, _, npt = basis_vals.shape
    slabs, cap = need_list.shape[2:]
    slots = slabs * cap
    half = bs // 2
    keys = nbat * kloc * kloc
    wide = (slabs, half, cap, LANES)
    vmem_limit = pltpu.CompilerParams(vmem_limit_bytes=56 << 20)

    requested = lax.all_to_all(need_list[0, 0], "slab", split_axis=0, concat_axis=0, tiled=True)
    requested = requested.reshape(1, slots)

    counts, counts_t, v2, flag = pl.pallas_call(
        prep_kernel,
        out_shape=(
            jax.ShapeDtypeStruct((2, keys, slots), BF16),
            jax.ShapeDtypeStruct((2, slots, keys), BF16),
            jax.ShapeDtypeStruct((nbat, half * kloc, 2 * npt), BF16),
            jax.ShapeDtypeStruct((1, 1), jnp.int32),
        ),
        in_specs=[SMEM, VMEM, VMEM],
        out_specs=(VMEM, VMEM, VMEM, SMEM),
        compiler_params=vmem_limit,
        name="prep",
    )(task_counts, tasks[0, 0], basis_vals)

    sends = pl.pallas_call(
        send_kernel,
        out_shape=jax.ShapeDtypeStruct(wide, BF16),
        in_specs=[VMEM, VMEM],
        out_specs=VMEM,
        compiler_params=vmem_limit,
        name="send",
    )(requested, own)
    received = lax.all_to_all(sends, "slab", split_axis=0, concat_axis=0, tiled=True)

    partial = pl.pallas_call(
        density_kernel,
        out_shape=jax.ShapeDtypeStruct((nbat, npt), F32),
        in_specs=[SMEM, VMEM, VMEM, VMEM, VMEM],
        out_specs=VMEM,
        scratch_shapes=[
            pltpu.VMEM((keys, 2 * LANES), F32),
            pltpu.VMEM((nbat, half * kloc, kloc * LANES), BF16),
            pltpu.VMEM((nbat, half * kloc, kloc * LANES), BF16),
            pltpu.VMEM((kloc * LANES, 2 * LANES), BF16),
        ],
        compiler_params=vmem_limit,
        name="density",
    )(flag, received, counts, basis_vals, v2)
    density = lax.psum(partial, "blk")

    slot_sums = pl.pallas_call(
        potential_kernel,
        out_shape=jax.ShapeDtypeStruct(wide, BF16),
        in_specs=[SMEM, VMEM, VMEM, VMEM, VMEM],
        out_specs=VMEM,
        scratch_shapes=[
            pltpu.VMEM((half * kloc, kloc * LANES), F32),
            pltpu.VMEM((keys, half * LANES), BF16),
            pltpu.VMEM((keys, half * LANES), BF16),
            pltpu.VMEM((kloc * LANES, 2 * LANES), BF16),
        ],
        compiler_params=vmem_limit,
        name="potential",
    )(flag, density, counts_t, basis_vals, v2)
    returned = lax.all_to_all(slot_sums, "slab", split_axis=0, concat_axis=0, tiled=True)

    owner_sums = pl.pallas_call(
        owner_kernel,
        out_shape=jax.ShapeDtypeStruct((blk_dev, bs, bs), F32),
        in_specs=[VMEM, VMEM],
        out_specs=VMEM,
        compiler_params=vmem_limit,
        name="owner",
    )(requested, returned)
    return (density, owner_sums[None])


def solution(mesh):
    in_specs = (
        P("blk", "slab", None, None),
        P("slab", None, None, None),
        P("blk", "slab", None, None),
        P("blk", "slab", None, None),
        P("blk", "slab"),
    )
    out_specs = (P("slab", None), P("blk", "slab", None, None))
    return jax.shard_map(body, mesh=mesh, in_specs=in_specs, out_specs=out_specs, check_vma=False)
```

time: 804 us -> 132 us (0.16)
  other arithmetic: 296 us -> 0.73 us
  waiting for transfers between devices: 207 us -> 24.2 us
  local copies, waits for them, and re-layouts: 159 us -> 3.31 us
  matrix products: 91.6 us -> 0 us
  blocking collectives: 2.46 us -> 60.9 us
  Pallas kernels: 0 us -> 36.3 us
  starting transfers between devices: 20.4 us -> 4.97 us
  between operations: 14.1 us -> 1.31 us
  loops' own time: 8.14 us -> 0 us
    scatter-add x7 -> x0, other arithmetic: 263 us -> none  [the longest x6 237 us: potential_tile(): return (slot_sums.at[slot_ids].add(incomplete_sum_terms), None)]
    all_gather x1 -> x0, waiting for transfers between devices: 152 us -> none  [body(): column_all = lax.all_gather(owned_blocks, 'slab', axis=0, tiled=True)]
    gather x37 -> x0, local copies, waits for them, and re-layouts: 121 us -> none  [the longest x12 40 us: tile_terms(): right_side_values = basis_vals[grid_batch_index, fields_tile[2]]]
    dot_general x18 -> x0, matrix products: 91.6 us -> none  [the longest x6 54.1 us: potential_tile(): jnp.einsum('lkf,lgf->lkg', weight_applied, right_side_values, preferred_e...]
    all_to_all x0 -> x2, blocking collectives: none -> 57.8 us  [the longest x1 36.9 us: body(): lax.all_to_all(slot_sums, 'slab', split_axis=0, concat_axis=0, tiled=True)]
    pallas_call x0 -> x5, Pallas kernels: none -> 36.3 us  [the longest x1 13.4 us: body(): pl.pallas_call(potential_kernel, out_shape=jax.ShapeDtypeStruct(wide, BF1...]
    all_to_all x2 -> x1, waiting for transfers between devices: 54.1 us -> 24.2 us  [body(): lax.all_to_all(sends, 'slab', split_axis=0, concat_axis=0, tiled=True)]
    unnamed x9 -> x3, local copies, waits for them, and re-layouts: 19.4 us -> 2.12 us
  transfers between devices with their start and end apart: 3 -> 1, of which waited for: 2 -> 1; matrix products, arithmetic and copies ran while one was open for 62% -> 0% of each run, Pallas kernels for 0% -> 3%
where the time goes in v1:
time: 132 us
  blocking collectives  60.9 us (46%)
  Pallas kernels  36.3 us (27%)
  waiting for transfers between devices  24.2 us (18%)
  starting transfers between devices  4.97 us (4%)
  local copies, waits for them, and re-layouts  3.31 us (3%)
    all_to_all x1, blocking collectives, body(): lax.all_to_all(slot_sums, 'slab', split_axis=0, concat_axis=0, tiled=True)  36.9 us
    all_to_all x1, waiting for transfers between devices, body(): lax.all_to_all(sends, 'slab', split_axis=0, concat_axis=0, tiled=True)  24.2 us
    all_to_all x1, blocking collectives, body(): lax.all_to_all(need_list[0, 0], 'slab', split_axis=0, concat_axis=0, tile...  20.9 us
    pallas_call x1, Pallas kernels, body(): pl.pallas_call(potential_kernel, out_shape=jax.ShapeDtypeStruct(wide, BF1...  13.4 us
    pallas_call x1, Pallas kernels, body(): pl.pallas_call(density_kernel, out_shape=jax.ShapeDtypeStruct((nbat, npt)...  12.4 us
    all_to_all x1, starting transfers between devices, body(): lax.all_to_all(sends, 'slab', split_axis=0, concat_axis=0, tiled=True)  4.97 us
    pallas_call x1, Pallas kernels, body(): pl.pallas_call(prep_kernel, out_shape=(jax.ShapeDtypeStruct((2, keys, slo...  3.89 us
    pallas_call x1, Pallas kernels, body(): pl.pallas_call(send_kernel, out_shape=jax.ShapeDtypeStruct(wide, BF16), i...  3.32 us
  transfers between devices with their start and end apart: 1, of which 1 were waited for; matrix products, arithmetic and copies ran while one was open for 0% of the time, Pallas kernels for 3%

profile of v1, /device:TPU:0, one launch (start us, length us, event | category | flops | bytes accessed | tf_op | source)
XLA Modules:
  0.0 131.7 jit_solution(10405209784987357739)
XLA Ops:
  0.6 0.8 copy.9
  1.4 20.9 %all_to_all.19 = s32[64,1,4]{2,1,0:T(1,128)S(1)} all-to-all(s32[64,1,4]{2,1,0:T(1,128)S(1)} %bitcast.6), channel_id=1, replica_groups=mesh['slab'=64,'blk'=2] {'slab'}, dimensions={0} | all-to-all | bytes 2048 | tf_op jit(solution)/shard_map/all_to_all | solution.py:213
  22.3 0.5 broadcast.3
  22.8 0.7 reduce.3
  23.5 0.7 reshape.11.req_ref
  24.2 3.3 %send.1 = bf16[64,32,4,128]{3,2,1,0:T(4,128)(2,1)} custom-call(s32[1,256]{1,0:T(1,128)} %reshape.11.req_ref, bf16[32,64,64]{2,1,0:T(8,128)(2,1)} %bitcast.5), custom_call_target="tpu_custom_call" | custom-call | tf_op jit(solution)/shard_map/send/pallas_call | solution.py:230
  27.5 5.0 %all-to-all-start.1 = ((bf16[64,32,4,128]{3,2,1,0:T(4,128)(2,1)}), bf16[64,32,4,128]{3,2,1,0:T(4,128)(2,1)S(1)}, u32[]{:S(2)}, u32[]{:S(2)}) async-start(bf16[64,32,4,128]{3,2,1,0:T(4,128)(2,1)} %send.1), calls=%async_computation.1 | async-start | bytes 4194304 | tf_op jit(solution)/shard_map/all_to_all | solution.py:238
  33.2 3.9 %prep.1 = (bf16[2,512,256]{2,1,0:T(8,128)(2,1)}, bf16[2,256,512]{2,1,0:T(8,128)(2,1)}, bf16[8,256,256]{2,1,0:T(8,128)(2,1)}, s32[1,1]{1,0:T(1,128)}) custom-call(s32[1,1]{1,0:T(1,128)S(6)} %copy.10.count_ref, s32[4,1536]{1,0:T(4,128)} %bitcast.7, bf16[8,8,64,128]{3,2,1,0:T(8,128)(2,1)} %v_ref.5), custom_call_target="tpu_custom_call" | custom-call | tf_op jit(solution)/shard_map/prep/pallas_call | solution.py:216
  37.1 24.2 %all-to-all-done.1.r_ref = bf16[64,32,4,128]{3,2,1,0:T(4,128)(2,1)S(1)} async-done(((bf16[64,32,4,128]{3,2,1,0:T(4,128)(2,1)}), bf16[64,32,4,128]{3,2,1,0:T(4,128)(2,1)S(1)}, u32[]{:S(2)}, u32[]{:S(2)}) %all-to-all-start.1) | async-done | bytes 2097184 | tf_op jit(solution)/shard_map/all_to_all | solution.py:238
  61.3 0.0 copy-start
  61.3 1.3 %copy-done = bf16[64,32,4,128]{3,2,1,0:T(4,128)(2,1)} copy-done((bf16[64,32,4,128]{3,2,1,0:T(4,128)(2,1)}, bf16[64,32,4,128]{3,2,1,0:T(4,128)(2,1)S(1)}, u32[]{:S(2)}) %copy-start) | copy-done | bytes 2097176
  62.6 12.4 %density.1 = f32[8,128]{1,0:T(8,128)} custom-call(s32[1,1]{1,0:T(1,128)} %get-tuple-element.6.flag_ref, bf16[64,32,4,128]{3,2,1,0:T(4,128)(2,1)} %copy-done, bf16[2,512,256]{2,1,0:T(8,128)(2,1)} %get-tuple-element.7.c_ref, bf16[8,8,64,128]{3,2,1,0:T(8,128)(2,1)} %v_ref.5, bf16[8,256,256]{2,1,0:T(8,128)(2,1)} %get-tuple-element.8.v2_ref), custom_call_target="tpu_custom_call" | custom-call | tf_op jit(solution)/shard_map/density/pallas_call | solution.py:240
  75.0 3.2 %psum.7.d_ref = f32[8,128]{1,0:T(8,128)} all-reduce(f32[8,128]{1,0:T(8,128)} %density.1), channel_id=1, replica_groups=mesh['slab'=64,'blk'=2] {'blk'}, use_global_device_ids=true, to_apply=%region_0.0 | all-reduce | flops 1024 | bytes 8192 | tf_op jit(solution)/shard_map/psum | solution.py:254
  78.2 13.4 %potential.1 = bf16[64,32,4,128]{3,2,1,0:T(4,128)(2,1)} custom-call(s32[1,1]{1,0:T(1,128)} %get-tuple-element.6.flag_ref, f32[8,128]{1,0:T(8,128)} %psum.7.d_ref, bf16[2,256,512]{2,1,0:T(8,128)(2,1)} %get-tuple-element.9.ct_ref, bf16[8,8,64,128]{3,2,1,0:T(8,128)(2,1)} %v_ref.5, bf16[8,256,256]{2,1,0:T(8,128)(2,1)} %get-tuple-element.8.v2_ref), custom_call_target="tpu_custom_call" | custom-call | tf_op jit(solution)/shard_map/potential/pallas_call | solution.py:256
  91.6 36.9 %all_to_all.20.ret_ref = bf16[64,32,4,128]{3,2,1,0:T(4,128)(2,1)} all-to-all(bf16[64,32,4,128]{3,2,1,0:T(4,128)(2,1)} %potential.1), channel_id=1, replica_groups=mesh['slab'=64,'blk'=2] {'slab'}, dimensions={0} | all-to-all | bytes 4194304 | tf_op jit(solution)/shard_map/all_to_all | solution.py:270
  128.4 3.3 %owner.1 = f32[32,64,64]{2,1,0:T(8,128)} custom-call(s32[1,256]{1,0:T(1,128)} %reshape.11.req_ref, bf16[64,32,4,128]{3,2,1,0:T(4,128)(2,1)} %all_to_all.20.ret_ref), custom_call_target="tpu_custom_call" | custom-call | tf_op jit(solution)/shard_map/owner/pallas_call | solution.py:272
Async XLA Ops:
  27.5 33.8 %all-to-all-start.1 = ((bf16[64,32,4,128]{3,2,1,0:T(4,128)(2,1)}), bf16[64,32,4,128]{3,2,1,0:T(4,128)(2,1)S(1)}, u32[]{:S(2)}, u32[]{:S(2)}) async-start(bf16[64,32,4,128]{3,2,1,0:T(4,128)(2,1)} %send.1), calls=%async_computation.1 | async-start | bytes 4194304 | tf_op jit(solution)/shard_map/all_to_all | solution.py:238
  61.3 1.4 %copy-start = (bf16[64,32,4,128]{3,2,1,0:T(4,128)(2,1)}, bf16[64,32,4,128]{3,2,1,0:T(4,128)(2,1)S(1)}, u32[]{:S(2)}) copy-start(bf16[64,32,4,128]{3,2,1,0:T(4,128)(2,1)S(1)} %all-to-all-done.1.r_ref) | copy-start | bytes 6291460

commit v2 on v1

v2 whole, which is shorter than its diff:
```python
import functools

import jax
import jax.numpy as jnp
from jax import lax
from jax.experimental import pallas as pl
from jax.experimental.pallas import tpu as pltpu
from jax.sharding import PartitionSpec as P

F32 = jnp.float32
BF16 = jnp.bfloat16
LANES = 128
SUB = 8
TASK_STEP = 512
PARTS = 2


def dot_nn(a, b):
    return lax.dot_general(a, b, (((1,), (0,)), ((), ())), preferred_element_type=F32)


def dot_nt(a, b):
    return lax.dot_general(a, b, (((1,), (1,)), ((), ())), preferred_element_type=F32)


def dot_tn(a, b):
    return lax.dot_general(a, b, (((0,), (0,)), ((), ())), preferred_element_type=F32)


def split_pair(x):
    hi = x.astype(BF16)
    return hi, (x - hi.astype(F32)).astype(BF16)


def own_kernel(own_ref, o_ref):
    half = own_ref.shape[1] // 2
    own = own_ref[...].astype(F32)
    own = jnp.concatenate([own[:, :half], own[:, half:]], axis=2)
    own = jnp.swapaxes(own, 0, 1).astype(BF16)
    for j in range(half):
        o_ref[j // 2, :, (j % 2) * LANES : (j % 2 + 1) * LANES] = own[j]


def prep_kernel(count_ref, tasks_ref, v_ref, c_ref, ct_ref, v2_ref, flag_ref):
    nbat, kloc, bs, npt = v_ref.shape
    keys = nbat * kloc * kloc
    slots = c_ref.shape[2]
    tcap = tasks_ref.shape[1]
    step = TASK_STEP if tcap % TASK_STEP == 0 else tcap
    live = count_ref[0, 0]
    c = jnp.zeros((keys, slots), F32)
    ct = jnp.zeros((slots, keys), F32)
    for t in range(0, tcap, step):
        fields = tasks_ref[:, t : t + step]
        key = (fields[0:1] * kloc + fields[2:3]) * kloc + fields[1:2]
        lane = lax.broadcasted_iota(jnp.int32, (1, step), 1) + t
        key = jnp.where(lane < live, key, -1)
        key_hot = jnp.where(
            lax.broadcasted_iota(jnp.int32, (keys, step), 0) == key, 1.0, 0.0
        ).astype(BF16)
        slot_hot = jnp.where(
            lax.broadcasted_iota(jnp.int32, (slots, step), 0) == fields[3:4], 1.0, 0.0
        ).astype(BF16)
        c += dot_nt(key_hot, slot_hot)
        ct += dot_nt(slot_hot, key_hot)
    c_hi = jnp.floor(c * (1.0 / 256.0)) * 256.0
    ct_hi = jnp.floor(ct * (1.0 / 256.0)) * 256.0
    c_ref[0] = (c - c_hi).astype(BF16)
    c_ref[1] = c_hi.astype(BF16)
    ct_ref[0] = (ct - ct_hi).astype(BF16)
    ct_ref[1] = ct_hi.astype(BF16)
    flag_ref[0, 0] = jnp.where(jnp.max(c) > 255.5, 1, 0).astype(jnp.int32)
    half = bs // 2
    for b in range(nbat):
        vals = jnp.swapaxes(v_ref[b].astype(F32), 0, 1)
        for h in range(2):
            part = vals[h * half : (h + 1) * half].reshape(half * kloc, npt)
            v2_ref[b, :, h * npt : (h + 1) * npt] = part.astype(BF16)


def request_hot(req_ref, nblk):
    slabs, _, cap = req_ref.shape
    slots = slabs * cap
    req = req_ref[...].reshape(slabs, cap).astype(F32).astype(BF16)
    row = lax.broadcasted_iota(jnp.int32, (slots, slabs), 0) // cap
    col = lax.broadcasted_iota(jnp.int32, (slots, slabs), 1)
    spread = dot_nn(jnp.where(row == col, 1.0, 0.0).astype(BF16), req)
    nth = lax.broadcasted_iota(jnp.int32, (slots, cap), 0) % cap
    keep = lax.broadcasted_iota(jnp.int32, (slots, cap), 1) == nth
    ids = jnp.sum(jnp.where(keep, spread, 0.0), axis=1, keepdims=True).astype(jnp.int32)
    ids = jnp.broadcast_to(ids, (slots, nblk))
    same = lax.broadcasted_iota(jnp.int32, (slots, nblk), 1) == ids
    return jnp.where(same, 1.0, 0.0).astype(BF16)


def send_rows(hot, own_ref, o_ref, first):
    slabs, rows, cap, _ = o_ref.shape
    for jp in range(rows // 2):
        res = dot_nn(hot, own_ref[first // 2 + jp]).astype(BF16)
        o_ref[:, 2 * jp] = res[:, :LANES].reshape(slabs, cap, LANES)
        o_ref[:, 2 * jp + 1] = res[:, LANES:].reshape(slabs, cap, LANES)


def first_send_kernel(req_ref, own_ref, o_ref, hot_ref):
    hot = request_hot(req_ref, own_ref.shape[1])
    hot_ref[...] = hot
    send_rows(hot, own_ref, o_ref, 0)


def next_send_kernel(hot_ref, own_ref, o_ref, *, first):
    send_rows(hot_ref[...], own_ref, o_ref, first)


def slot_rows(ref, jp):
    slabs, _, cap, _ = ref.shape
    r0 = ref[:, 2 * jp].reshape(slabs * cap, LANES)
    r1 = ref[:, 2 * jp + 1].reshape(slabs * cap, LANES)
    return jnp.concatenate([r0, r1], axis=1)


def diagonal_values(v_ref, b):
    _, kloc, bs, npt = v_ref.shape
    zero = jnp.zeros((bs, npt), BF16)
    rows = []
    for l in range(kloc):
        v = v_ref[b, l]
        rows.append(jnp.concatenate([v, zero], axis=1))
        rows.append(jnp.concatenate([zero, v], axis=1))
    return jnp.concatenate(rows, axis=0)


def density_kernel(flag_ref, r_ref, c_ref, v_ref, v2_ref, d0_ref, d_ref, hi_s, lo_s, *, first):
    nbat, kloc, _, npt = v_ref.shape
    rows = r_ref.shape[1]
    keys, slots = c_ref.shape[1:]

    def build(jp, parts):
        rhs = slot_rows(r_ref, jp)
        res = dot_nn(c_ref[0], rhs)
        if parts == 2:
            res += dot_nn(c_ref[1], rhs)
        res = res.reshape(keys // SUB, SUB, 2 * LANES)
        hi, lo = split_pair(jnp.concatenate([res[:, :, :LANES], res[:, :, LANES:]], axis=1))
        at = pl.ds(pl.multiple_of(jp * 2 * SUB, 2 * SUB), 2 * SUB)
        hi_s[:, at, :] = hi
        lo_s[:, at, :] = lo

    def loop(parts, unroll):
        def step(jp, carry):
            build(jp, parts)
            return carry

        lax.fori_loop(0, rows // 2, step, 0, unroll=unroll)

    @pl.when(flag_ref[0, 0] == 0)
    def _():
        loop(1, 2)

    @pl.when(flag_ref[0, 0] != 0)
    def _():
        loop(2, 1)

    def one_batch(b, carry):
        lhs = jnp.concatenate(
            [
                jnp.concatenate([hi_s[b * kloc + l] for l in range(kloc)], axis=1),
                jnp.concatenate([lo_s[b * kloc + l] for l in range(kloc)], axis=1),
            ],
            axis=0,
        )
        image = dot_nn(lhs, diagonal_values(v_ref, b))
        image = image[: rows * SUB] + image[rows * SUB :]
        left = v2_ref[b, first * SUB : (first + rows) * SUB].astype(F32)
        d = jnp.sum(image * left, axis=0, keepdims=True)
        d_ref[pl.ds(b, 1), :] = d0_ref[pl.ds(b, 1), :] + d[:, :npt] + d[:, npt:]
        return carry

    lax.fori_loop(0, nbat, one_batch, 0)


def potential_kernel(flag_ref, d_ref, ct_ref, v_ref, v2_ref, o_ref, hi_s, lo_s, *, first):
    nbat, kloc, _, _ = v_ref.shape
    slabs, rows, cap, _ = o_ref.shape
    group = kloc * SUB

    def one_batch(b, carry):
        d = d_ref[pl.ds(b, 1), :]
        pot = d / jnp.sqrt(1.0 + d * d)
        pot = jnp.concatenate([pot, pot], axis=1)
        left = v2_ref[b, first * SUB : (first + rows) * SUB].astype(F32)
        g = dot_nt((left * pot).astype(BF16), diagonal_values(v_ref, b))
        at = pl.ds(pl.multiple_of(b * group, group), group)
        for j in range(rows):
            x = jnp.concatenate(
                [g[j * SUB : (j + 1) * SUB, l * LANES : (l + 1) * LANES] for l in range(kloc)],
                axis=0,
            )
            hi, lo = split_pair(x)
            hi_s[j, at, :] = hi
            lo_s[j, at, :] = lo
        return carry

    lax.fori_loop(0, nbat, one_batch, 0)

    def sums(jp, parts):
        hi = jnp.concatenate([hi_s[2 * jp], hi_s[2 * jp + 1]], axis=1)
        lo = jnp.concatenate([lo_s[2 * jp], lo_s[2 * jp + 1]], axis=1)
        lhs = [ct_ref[n] for n in range(parts) for _ in range(2)]
        out = dot_nn(jnp.concatenate(lhs, axis=1), jnp.concatenate([hi, lo] * parts, axis=0))
        out = out.astype(BF16)
        o_ref[:, 2 * jp] = out[:, :LANES].reshape(slabs, cap, LANES)
        o_ref[:, 2 * jp + 1] = out[:, LANES:].reshape(slabs, cap, LANES)

    def loop(parts, unroll):
        def step(jp, carry):
            sums(jp, parts)
            return carry

        lax.fori_loop(0, rows // 2, step, 0, unroll=unroll)

    @pl.when(flag_ref[0, 0] == 0)
    def _():
        loop(1, 2)

    @pl.when(flag_ref[0, 0] != 0)
    def _():
        loop(2, 1)


def owner_sums(hot_ref, ret_ref):
    hot = hot_ref[...]
    parts = []
    for jp in range(ret_ref.shape[1] // 2):
        res = dot_tn(hot, slot_rows(ret_ref, jp))
        parts += [res[:, :LANES], res[:, LANES:]]
    return jnp.swapaxes(jnp.stack(parts, axis=0), 0, 1)


def owner_kernel(hot_ref, ret_ref, old_ref, o_ref, buf, sem, *, first):
    bs = o_ref.shape[2]
    half = o_ref.shape[1] // 2
    rows = ret_ref.shape[1]
    sums = owner_sums(hot_ref, ret_ref)
    copies = []
    for h in range(2):
        buf[h] = sums[:, :, h * bs : (h + 1) * bs]
        copies.append(
            pltpu.make_async_copy(
                buf.at[h], o_ref.at[:, pl.ds(h * half + first, rows)], sem.at[h]
            )
        )
        copies[-1].start()
    for c in copies:
        c.wait()


SMEM = pl.BlockSpec(memory_space=pltpu.SMEM)
VMEM = pl.BlockSpec(memory_space=pltpu.VMEM)
ANY = pl.BlockSpec(memory_space=pl.ANY)
PARAMS = pltpu.CompilerParams(vmem_limit_bytes=32 << 20)


def exchange(x):
    x = lax.all_to_all(x, "slab", split_axis=0, concat_axis=0, tiled=True)
    return x


def body(p_blocks, basis_vals, need_list, tasks, task_counts):
    own = p_blocks[0]
    blk_dev, bs, _ = own.shape
    nbat, kloc, _, npt = basis_vals.shape
    slabs, cap = need_list.shape[2:]
    slots = slabs * cap
    half = bs // 2
    rows = half // PARTS
    keys = nbat * kloc * kloc
    wide = jax.ShapeDtypeStruct((slabs, rows, cap, LANES), BF16)

    requested = exchange(need_list.reshape(slabs, 1, cap))

    own_rows = pl.pallas_call(
        own_kernel,
        out_shape=jax.ShapeDtypeStruct((half // 2, blk_dev, 2 * LANES), BF16),
        in_specs=[VMEM],
        out_specs=VMEM,
        compiler_params=PARAMS,
        name="own",
    )(own)

    counts, counts_t, v2, flag = pl.pallas_call(
        prep_kernel,
        out_shape=(
            jax.ShapeDtypeStruct((2, keys, slots), BF16),
            jax.ShapeDtypeStruct((2, slots, keys), BF16),
            jax.ShapeDtypeStruct((nbat, half * kloc, 2 * npt), BF16),
            jax.ShapeDtypeStruct((1, 1), jnp.int32),
        ),
        in_specs=[SMEM, VMEM, VMEM],
        out_specs=(VMEM, VMEM, VMEM, SMEM),
        compiler_params=PARAMS,
        name="prep",
    )(task_counts, tasks[0, 0], basis_vals)

    sent, hot = pl.pallas_call(
        first_send_kernel,
        out_shape=(wide, jax.ShapeDtypeStruct((slots, blk_dev), BF16)),
        in_specs=[VMEM, VMEM],
        out_specs=(VMEM, VMEM),
        compiler_params=PARAMS,
        name="send0",
    )(requested, own_rows)
    received = [exchange(sent)]
    for n in range(1, PARTS):
        sent = pl.pallas_call(
            functools.partial(next_send_kernel, first=n * rows),
            out_shape=wide,
            in_specs=[VMEM, VMEM],
            out_specs=VMEM,
            compiler_params=PARAMS,
            name=f"send{n}",
        )(hot, own_rows)
        received.append(exchange(sent))

    partial = jnp.zeros((nbat, npt), F32)
    for n in range(PARTS):
        partial = pl.pallas_call(
            functools.partial(density_kernel, first=n * rows),
            out_shape=jax.ShapeDtypeStruct((nbat, npt), F32),
            in_specs=[SMEM] + [VMEM] * 5,
            out_specs=VMEM,
            scratch_shapes=[pltpu.VMEM((nbat * kloc, rows * SUB, LANES), BF16)] * 2,
            compiler_params=PARAMS,
            name=f"density{n}",
        )(flag, received[n], counts, basis_vals, v2, partial)
    density = lax.psum(partial, "blk")

    returned = []
    for n in range(PARTS):
        slot_sums = pl.pallas_call(
            functools.partial(potential_kernel, first=n * rows),
            out_shape=wide,
            in_specs=[SMEM] + [VMEM] * 4,
            out_specs=VMEM,
            scratch_shapes=[pltpu.VMEM((rows, keys, LANES), BF16)] * 2,
            compiler_params=PARAMS,
            name=f"potential{n}",
        )(flag, density, counts_t, basis_vals, v2)
        returned.append(exchange(slot_sums))

    out = pl.empty((blk_dev, bs, bs), F32) if False else None
    out_shape = jax.ShapeDtypeStruct((blk_dev, bs, bs), F32)
    for n in range(PARTS):
        args = (hot, returned[n]) + (() if out is None else (out,))
        kern = functools.partial(owner_kernel, first=n * rows)
        if out is None:
            kern = functools.partial(
                lambda h, r, o, b, s, first: owner_kernel(h, r, None, o, b, s, first=first),
                first=n * rows,
            )
        out = pl.pallas_call(
            kern,
            out_shape=out_shape,
            in_specs=[VMEM, VMEM] + [ANY] * (len(args) - 2),
            out_specs=ANY,
            scratch_shapes=[
                pltpu.VMEM((2, blk_dev, rows, bs), F32),
                pltpu.SemaphoreType.DMA((2,)),
            ],
            input_output_aliases={2: 0} if len(args) == 3 else {},
            compiler_params=PARAMS,
            name=f"owner{n}",
        )(*args)
    return (density, out[None])


def solution(mesh):
    in_specs = (
        P("blk", "slab", None, None),
        P("slab", None, None, None),
        P("blk", "slab", None, None),
        P("blk", "slab", None, None),
        P("blk", "slab"),
    )
    out_specs = (P("slab", None), P("blk", "slab", None, None))
    return jax.shard_map(body, mesh=mesh, in_specs=in_specs, out_specs=out_specs, check_vma=False)
```

time: 132 us -> 134 us (1.015)
  blocking collectives: 60.9 us -> 2.47 us
  waiting for transfers between devices: 24.2 us -> 61.8 us
  starting transfers between devices: 4.97 us -> 31.3 us
  Pallas kernels: 36.3 us -> 30 us
  local copies, waits for them, and re-layouts: 3.31 us -> 6.1 us
    all_to_all x2 -> x0, blocking collectives: 57.8 us -> none  [the longest x1 36.9 us: body(): lax.all_to_all(slot_sums, 'slab', split_axis=0, concat_axis=0, tiled=True)]
    all_to_all x1 -> x5, waiting for transfers between devices: 24.2 us -> 61.8 us  [exchange(): x = lax.all_to_all(x, 'slab', split_axis=0, concat_axis=0, tiled=True)]
    all_to_all x1 -> x5, starting transfers between devices: 4.97 us -> 31.3 us  [exchange(): x = lax.all_to_all(x, 'slab', split_axis=0, concat_axis=0, tiled=True)]
    pallas_call x4 -> x9, Pallas kernels: 32.4 us -> 28.3 us  [the longest x2 11.9 us: body(): pl.pallas_call(functools.partial(potential_kernel, first=n * rows), out_s...]
    unnamed x3 -> x19, local copies, waits for them, and re-layouts: 2.12 us -> 6.1 us
    pallas_call x1, Pallas kernels: 3.89 us -> 1.7 us  [body(): pl.pallas_call(prep_kernel, out_shape=(jax.ShapeDtypeStruct((2, keys, slo...]
  transfers between devices with their start and end apart: 1 -> 5, of which waited for: 1 -> 5; matrix products, arithmetic and copies ran while one was open for 0% -> 0% of each run, Pallas kernels for 3% -> 11%
where the time goes in v2:
time: 134 us; the launch traced here: 133 us
  waiting for transfers between devices  61.8 us (46%)
  starting transfers between devices  31.3 us (23%)
  Pallas kernels  30 us (22%)
  local copies, waits for them, and re-layouts  6.1 us (5%)
  blocking collectives  2.47 us (2%)
  between operations  1.42 us (1%)
    all_to_all x5, waiting for transfers between devices, exchange(): x = lax.all_to_all(x, 'slab', split_axis=0, concat_axis=0, tiled=True)  61.8 us
    all_to_all x5, starting transfers between devices, exchange(): x = lax.all_to_all(x, 'slab', split_axis=0, concat_axis=0, tiled=True)  31.3 us
    pallas_call x2, Pallas kernels, body(): pl.pallas_call(functools.partial(potential_kernel, first=n * rows), out_s...  11.9 us
    pallas_call x2, Pallas kernels, body(): pl.pallas_call(functools.partial(density_kernel, first=n * rows), out_sha...  10.6 us
    unnamed x19, local copies, waits for them, and re-layouts  6.1 us
  transfers between devices with their start and end apart: 5, of which 5 were waited for; matrix products, arithmetic and copies ran while one was open for 0% of the time, Pallas kernels for 11%

profile of v2, /device:TPU:0, one launch (start us, length us, event | category | flops | bytes accessed | tf_op | source)
XLA Modules:
  0.0 133.1 jit_solution(9357989643580730909)
XLA Ops:
  0.6 1.4 %copy.8 = s32[1,1,64,4]{3,2,1,0:T(8,128)} copy(s32[1,1,64,4]{2,3,1,0:T(4,128)} %param.7) | data formatting | bytes 2048 | tf_op args[2]
  2.0 11.5 %all-to-all-start = ((s32[64,1,4]{2,1,0:T(1,128)}), s32[64,1,4]{2,1,0:T(1,128)S(1)}, u32[]{:S(2)}, u32[]{:S(2)}) async-start(s32[64,1,4]{2,1,0:T(1,128)} %bitcast.1), calls=%async_computation | async-start | bytes 65536 | tf_op jit(solution)/shard_map/all_to_all | solution.py:264
  13.6 1.0 copy-done.6
  14.8 8.2 %all-to-all-done.req_ref = s32[64,1,4]{2,1,0:T(1,128)S(1)} async-done(((s32[64,1,4]{2,1,0:T(1,128)}), s32[64,1,4]{2,1,0:T(1,128)S(1)}, u32[]{:S(2)}, u32[]{:S(2)}) %all-to-all-start) | async-done | bytes 1056 | tf_op jit(solution)/shard_map/all_to_all | solution.py:264
  23.1 1.7 %send0.1 = (bf16[64,16,4,128]{3,2,1,0:T(4,128)(2,1)}, bf16[256,32]{1,0:T(8,128)(2,1)S(1)}) custom-call(s32[64,1,4]{2,1,0:T(1,128)S(1)} %all-to-all-done.req_ref, bf16[16,32,256]{2,1,0:T(8,128)(2,1)S(1)} %own.1.own_ref), custom_call_target="tpu_custom_call" | custom-call | tf_op jit(solution)/shard_map/send0/pallas_call | solution.py:304
  24.7 5.0 %all-to-all-start.2 = ((bf16[64,16,4,128]{3,2,1,0:T(4,128)(2,1)}), bf16[64,16,4,128]{3,2,1,0:T(4,128)(2,1)S(1)}, u32[]{:S(2)}, u32[]{:S(2)}) async-start(bf16[64,16,4,128]{3,2,1,0:T(4,128)(2,1)} %get-tuple-element.12), calls=%async_computation.2 | async-start | bytes 2097152 | tf_op jit(solution)/shard_map/all_to_all | solution.py:264
  29.7 1.5 %send1.1 = bf16[64,16,4,128]{3,2,1,0:T(4,128)(2,1)} custom-call(bf16[256,32]{1,0:T(8,128)(2,1)S(1)} %get-tuple-element.9.hot_ref.h, bf16[16,32,256]{2,1,0:T(8,128)(2,1)S(1)} %own.1.own_ref), custom_call_target="tpu_custom_call" | custom-call | tf_op jit(solution)/shard_map/send1/pallas_call | solution.py:314
  31.2 16.1 %all-to-all-done.2.r_ref = bf16[64,16,4,128]{3,2,1,0:T(4,128)(2,1)S(1)} async-done(((bf16[64,16,4,128]{3,2,1,0:T(4,128)(2,1)}), bf16[64,16,4,128]{3,2,1,0:T(4,128)(2,1)S(1)}, u32[]{:S(2)}, u32[]{:S(2)}) %all-to-all-start.2) | async-done | bytes 1048608 | tf_op jit(solution)/shard_map/all_to_all | solution.py:264
  47.2 5.5 %all-to-all-start.1 = ((bf16[64,16,4,128]{3,2,1,0:T(4,128)(2,1)}), bf16[64,16,4,128]{3,2,1,0:T(4,128)(2,1)}, u32[]{:S(2)}, u32[]{:S(2)}) async-start(bf16[64,16,4,128]{3,2,1,0:T(4,128)(2,1)} %send1.1), calls=%async_computation.1 | async-start | bytes 2097152 | tf_op jit(solution)/shard_map/all_to_all | solution.py:264
  53.4 1.7 %prep.1 = (bf16[2,512,256]{2,1,0:T(8,128)(2,1)S(1)}, bf16[2,256,512]{2,1,0:T(8,128)(2,1)S(1)}, bf16[8,256,256]{2,1,0:T(8,128)(2,1)S(1)}, s32[1,1]{1,0:T(1,128)}) custom-call(s32[1,1]{1,0:T(1,128)S(6)} %copy.10.count_ref, s32[4,1536]{1,0:T(4,128)S(1)} %bitcast.5, bf16[8,8,64,128]{3,2,1,0:T(8,128)(2,1)S(1)} %copy-done), custom_call_target="tpu_custom_call" | custom-call | tf_op jit(solution)/shard_map/prep/pallas_call | solution.py:290
  55.9 4.7 %density0.1.d0_ref = f32[8,128]{1,0:T(8,128)S(1)} custom-call(s32[1,1]{1,0:T(1,128)} %get-tuple-element.8.flag_ref, bf16[64,16,4,128]{3,2,1,0:T(4,128)(2,1)S(1)} %all-to-all-done.2.r_ref, bf16[2,512,256]{2,1,0:T(8,128)(2,1)S(1)} %get-tuple-element.10.c_ref, bf16[8,8,64,128]{3,2,1,0:T(8,128)(2,1)S(1)} %copy-done, ...), custom_call_target="tpu_custom_call" | custom-call | tf_op jit(solution)/shard_map/density0/pallas_call | solution.py:326
  61.4 7.7 %all-to-all-done.1.r_ref = bf16[64,16,4,128]{3,2,1,0:T(4,128)(2,1)} async-done(((bf16[64,16,4,128]{3,2,1,0:T(4,128)(2,1)}), bf16[64,16,4,128]{3,2,1,0:T(4,128)(2,1)}, u32[]{:S(2)}, u32[]{:S(2)}) %all-to-all-start.1) | async-done | bytes 1048608 | tf_op jit(solution)/shard_map/all_to_all | solution.py:264
  69.1 1.0 copy-done.5
  70.2 5.9 %density1.1 = f32[8,128]{1,0:T(8,128)S(1)} custom-call(s32[1,1]{1,0:T(1,128)} %get-tuple-element.8.flag_ref, bf16[64,16,4,128]{3,2,1,0:T(4,128)(2,1)} %all-to-all-done.1.r_ref, bf16[2,512,256]{2,1,0:T(8,128)(2,1)S(1)} %copy-done.5, bf16[8,8,64,128]{3,2,1,0:T(8,128)(2,1)S(1)} %copy-done, bf16[8,256,256]{2,1,0:T(8,128)(2,1)S(1)} %get-tuple-element.11.v2_ref, ...), custom_call_target="tpu_custom_call" | custom-call | tf_op jit(solution)/shard_map/density1/pallas_call | solution.py:326
  76.1 2.5 %psum.7.d_ref = f32[8,128]{1,0:T(8,128)S(1)} all-reduce(f32[8,128]{1,0:T(8,128)S(1)} %density1.1), channel_id=1, replica_groups=mesh['slab'=64,'blk'=2] {'blk'}, use_global_device_ids=true, to_apply=%region_0.0 | all-reduce | flops 1024 | bytes 8192 | tf_op jit(solution)/shard_map/psum | solution.py:335
  78.6 5.9 %potential0.1 = bf16[64,16,4,128]{3,2,1,0:T(4,128)(2,1)} custom-call(s32[1,1]{1,0:T(1,128)} %get-tuple-element.8.flag_ref, f32[8,128]{1,0:T(8,128)S(1)} %psum.7.d_ref, bf16[2,256,512]{2,1,0:T(8,128)(2,1)S(1)} %copy-done.2, bf16[8,8,64,128]{3,2,1,0:T(8,128)(2,1)S(1)} %copy-done, bf16[8,256,256]{2,1,0:T(8,128)(2,1)S(1)} %get-tuple-element.11.v2_ref), custom_call_target="tpu_custom_call" | custom-call | tf_op jit(solution)/shard_map/potential0/pallas_call | solution.py:339
  84.5 4.7 %all-to-all-start.4 = ((bf16[64,16,4,128]{3,2,1,0:T(4,128)(2,1)}), bf16[64,16,4,128]{3,2,1,0:T(4,128)(2,1)S(1)}, u32[]{:S(2)}, u32[]{:S(2)}) async-start(bf16[64,16,4,128]{3,2,1,0:T(4,128)(2,1)} %potential0.1), calls=%async_computation.4 | async-start | bytes 2097152 | tf_op jit(solution)/shard_map/all_to_all | solution.py:264
  89.2 1.0 copy-done.3
  90.2 5.9 %potential1.1 = bf16[64,16,4,128]{3,2,1,0:T(4,128)(2,1)} custom-call(s32[1,1]{1,0:T(1,128)} %get-tuple-element.8.flag_ref, f32[8,128]{1,0:T(8,128)S(1)} %psum.7.d_ref, bf16[2,256,512]{2,1,0:T(8,128)(2,1)S(1)} %copy-done.3, bf16[8,8,64,128]{3,2,1,0:T(8,128)(2,1)S(1)} %copy-done, bf16[8,256,256]{2,1,0:T(8,128)(2,1)S(1)} %get-tuple-element.11.v2_ref), custom_call_target="tpu_custom_call" | custom-call | tf_op jit(solution)/shard_map/potential1/pallas_call | solution.py:339
  96.2 12.6 %all-to-all-done.4.r = bf16[64,16,4,128]{3,2,1,0:T(4,128)(2,1)S(1)} async-done(((bf16[64,16,4,128]{3,2,1,0:T(4,128)(2,1)}), bf16[64,16,4,128]{3,2,1,0:T(4,128)(2,1)S(1)}, u32[]{:S(2)}, u32[]{:S(2)}) %all-to-all-start.4) | async-done | bytes 1048608 | tf_op jit(solution)/shard_map/all_to_all | solution.py:264
  108.8 4.7 %all-to-all-start.3 = ((bf16[64,16,4,128]{3,2,1,0:T(4,128)(2,1)}), bf16[64,16,4,128]{3,2,1,0:T(4,128)(2,1)S(1)}, u32[]{:S(2)}, u32[]{:S(2)}) async-start(bf16[64,16,4,128]{3,2,1,0:T(4,128)(2,1)} %potential1.1), calls=%async_computation.3 | async-start | bytes 2097152 | tf_op jit(solution)/shard_map/all_to_all | solution.py:264
  113.4 1.2 owner0.1.old_ref
  114.6 17.3 %all-to-all-done.3.ret_ref = bf16[64,16,4,128]{3,2,1,0:T(4,128)(2,1)S(1)} async-done(((bf16[64,16,4,128]{3,2,1,0:T(4,128)(2,1)}), bf16[64,16,4,128]{3,2,1,0:T(4,128)(2,1)S(1)}, u32[]{:S(2)}, u32[]{:S(2)}) %all-to-all-start.3) | async-done | bytes 1048608 | tf_op jit(solution)/shard_map/all_to_all | solution.py:264
  131.9 1.2 owner1.1
  (17 shorter events, 1.8 us)
Async XLA Ops:
  2.0 21.0 %all-to-all-start = ((s32[64,1,4]{2,1,0:T(1,128)}), s32[64,1,4]{2,1,0:T(1,128)S(1)}, u32[]{:S(2)}, u32[]{:S(2)}) async-start(s32[64,1,4]{2,1,0:T(1,128)} %bitcast.1), calls=%async_computation | async-start | bytes 65536 | tf_op jit(solution)/shard_map/all_to_all | solution.py:264
  13.5 1.0 copy-start.6
  24.7 22.5 %all-to-all-start.2 = ((bf16[64,16,4,128]{3,2,1,0:T(4,128)(2,1)}), bf16[64,16,4,128]{3,2,1,0:T(4,128)(2,1)S(1)}, u32[]{:S(2)}, u32[]{:S(2)}) async-start(bf16[64,16,4,128]{3,2,1,0:T(4,128)(2,1)} %get-tuple-element.12), calls=%async_computation.2 | async-start | bytes 2097152 | tf_op jit(solution)/shard_map/all_to_all | solution.py:264
  31.2 22.2 %copy-start = (bf16[8,8,64,128]{3,2,1,0:T(8,128)(2,1)S(1)}, bf16[8,8,64,128]{3,2,1,0:T(8,128)(2,1)}, u32[]{:S(2)}) copy-start(bf16[8,8,64,128]{3,2,1,0:T(8,128)(2,1)} %v_ref.9) | copy-start | bytes 3145732
  31.2 22.2 %copy-start.8 = (s32[1,1,4,1536]{3,2,1,0:T(4,128)S(1)}, s32[1,1,4,1536]{3,2,1,0:T(4,128)}, u32[]{:S(2)}) copy-start(s32[1,1,4,1536]{3,2,1,0:T(4,128)} %param.8) | copy-start | bytes 73732
  47.2 21.9 %all-to-all-start.1 = ((bf16[64,16,4,128]{3,2,1,0:T(4,128)(2,1)}), bf16[64,16,4,128]{3,2,1,0:T(4,128)(2,1)}, u32[]{:S(2)}, u32[]{:S(2)}) async-start(bf16[64,16,4,128]{3,2,1,0:T(4,128)(2,1)} %send1.1), calls=%async_computation.1 | async-start | bytes 2097152 | tf_op jit(solution)/shard_map/all_to_all | solution.py:264
  55.1 0.8 copy-start.1
  60.6 0.8 copy-start.4
  61.4 17.2 %copy-start.2 = (bf16[2,256,512]{2,1,0:T(8,128)(2,1)S(1)}, bf16[2,256,512]{2,1,0:T(8,128)(2,1)}, u32[]{:S(2)}) copy-start(bf16[2,256,512]{2,1,0:T(8,128)(2,1)} %copy-done.1) | copy-start | bytes 1572868
  69.1 1.0 copy-start.5
  78.6 10.6 %copy-start.7 = (f32[8,128]{1,0:T(8,128)}, f32[8,128]{1,0:T(8,128)S(1)}, u32[]{:S(2)}) copy-start(f32[8,128]{1,0:T(8,128)S(1)} %psum.7.d_ref) | copy-start | bytes 12292
  84.5 24.2 %all-to-all-start.4 = ((bf16[64,16,4,128]{3,2,1,0:T(4,128)(2,1)}), bf16[64,16,4,128]{3,2,1,0:T(4,128)(2,1)S(1)}, u32[]{:S(2)}, u32[]{:S(2)}) async-start(bf16[64,16,4,128]{3,2,1,0:T(4,128)(2,1)} %potential0.1), calls=%async_computation.4 | async-start | bytes 2097152 | tf_op jit(solution)/shard_map/all_to_all | solution.py:264
  89.2 1.0 copy-start.3
  108.8 23.1 %all-to-all-start.3 = ((bf16[64,16,4,128]{3,2,1,0:T(4,128)(2,1)}), bf16[64,16,4,128]{3,2,1,0:T(4,128)(2,1)S(1)}, u32[]{:S(2)}, u32[]{:S(2)}) async-start(bf16[64,16,4,128]{3,2,1,0:T(4,128)(2,1)} %potential1.1), calls=%async_computation.3 | async-start | bytes 2097152 | tf_op jit(solution)/shard_map/all_to_all | solution.py:264

commit v3 on v2

v3 whole, which is shorter than its diff:
```python
import jax
import jax.numpy as jnp
from jax import lax
from jax.experimental import pallas as pl
from jax.experimental.pallas import tpu as pltpu
from jax.sharding import PartitionSpec as P

F32 = jnp.float32
BF16 = jnp.bfloat16
LANES = 128
SUB = 8
TASK_STEP = 512


def dot_nn(a, b):
    return lax.dot_general(a, b, (((1,), (0,)), ((), ())), preferred_element_type=F32)


def dot_nt(a, b):
    return lax.dot_general(a, b, (((1,), (1,)), ((), ())), preferred_element_type=F32)


def split_pair(x):
    hi = x.astype(BF16)
    return hi, (x - hi.astype(F32)).astype(BF16)


def turn_kernel(x_ref, o_ref):
    x = jnp.transpose(x_ref[...])
    o_ref[...] = x.reshape(o_ref.shape)


def own_kernel(own_ref, o_ref):
    half = own_ref.shape[1] // 2
    own = own_ref[...].astype(F32)
    own = jnp.concatenate([own[:, :half], own[:, half:]], axis=2)
    own = jnp.swapaxes(own, 0, 1).astype(BF16)
    for j in range(half):
        o_ref[j // 2, :, (j % 2) * LANES : (j % 2 + 1) * LANES] = own[j]


def prep_kernel(
    count_ref, tasks_ref, v_ref, hot_ref, c_ref, ct_ref, v2_ref, hot_t_ref, flag_ref
):
    hot_t_ref[...] = jnp.transpose(hot_ref[...].astype(F32)).astype(BF16)
    nbat, kloc, bs, npt = v_ref.shape
    keys = nbat * kloc * kloc
    slots = c_ref.shape[2]
    tcap = tasks_ref.shape[1]
    step = TASK_STEP if tcap % TASK_STEP == 0 else tcap
    live = count_ref[0, 0]
    c = jnp.zeros((keys, slots), F32)
    ct = jnp.zeros((slots, keys), F32)
    for t in range(0, tcap, step):
        fields = tasks_ref[:, t : t + step]
        key = (fields[0:1] * kloc + fields[2:3]) * kloc + fields[1:2]
        lane = lax.broadcasted_iota(jnp.int32, (1, step), 1) + t
        key = jnp.where(lane < live, key, -1)
        key_hot = jnp.where(
            lax.broadcasted_iota(jnp.int32, (keys, step), 0) == key, 1.0, 0.0
        ).astype(BF16)
        slot_hot = jnp.where(
            lax.broadcasted_iota(jnp.int32, (slots, step), 0) == fields[3:4], 1.0, 0.0
        ).astype(BF16)
        c += dot_nt(key_hot, slot_hot)
        ct += dot_nt(slot_hot, key_hot)
    c_hi = jnp.floor(c * (1.0 / 256.0)) * 256.0
    ct_hi = jnp.floor(ct * (1.0 / 256.0)) * 256.0
    c_ref[0] = (c - c_hi).astype(BF16)
    c_ref[1] = c_hi.astype(BF16)
    ct_ref[0] = (ct - ct_hi).astype(BF16)
    ct_ref[1] = ct_hi.astype(BF16)
    flag_ref[0, 0] = jnp.where(jnp.max(c) > 255.5, 1, 0).astype(jnp.int32)
    half = bs // 2
    for b in range(nbat):
        vals = jnp.swapaxes(v_ref[b].astype(F32), 0, 1)
        for h in range(2):
            part = vals[h * half : (h + 1) * half].reshape(half * kloc, npt)
            v2_ref[b, :, h * npt : (h + 1) * npt] = part.astype(BF16)


def request_hot(req_ref, nblk):
    slabs, _, cap = req_ref.shape
    slots = slabs * cap
    req = req_ref[...].reshape(slabs, cap).astype(F32).astype(BF16)
    row = lax.broadcasted_iota(jnp.int32, (slots, slabs), 0) // cap
    col = lax.broadcasted_iota(jnp.int32, (slots, slabs), 1)
    spread = dot_nn(jnp.where(row == col, 1.0, 0.0).astype(BF16), req)
    nth = lax.broadcasted_iota(jnp.int32, (slots, cap), 0) % cap
    keep = lax.broadcasted_iota(jnp.int32, (slots, cap), 1) == nth
    ids = jnp.sum(jnp.where(keep, spread, 0.0), axis=1, keepdims=True).astype(jnp.int32)
    ids = jnp.broadcast_to(ids, (slots, nblk))
    same = lax.broadcasted_iota(jnp.int32, (slots, nblk), 1) == ids
    return jnp.where(same, 1.0, 0.0).astype(BF16)


def send_kernel(req_ref, own_ref, o_ref, hot_ref, buf, sem):
    slabs, rows, cap, _ = buf.shape
    hot = request_hot(req_ref, own_ref.shape[1])
    hot_ref[...] = hot
    group = rows // sem.shape[0]
    copies = []
    for jp in range(rows // 2):
        res = dot_nn(hot, own_ref[jp]).astype(BF16)
        buf[:, 2 * jp] = res[:, :LANES].reshape(slabs, cap, LANES)
        buf[:, 2 * jp + 1] = res[:, LANES:].reshape(slabs, cap, LANES)
        if (2 * jp + 2) % group == 0:
            n = len(copies)
            part = pl.ds(n * group, group)
            copies.append(pltpu.make_async_copy(buf.at[:, part], o_ref.at[:, part], sem.at[n]))
            copies[n].start()
    for copy in copies:
        copy.wait()


def slot_rows(ref, jp):
    slabs, _, cap, _ = ref.shape
    r0 = ref[:, 2 * jp].reshape(slabs * cap, LANES)
    r1 = ref[:, 2 * jp + 1].reshape(slabs * cap, LANES)
    return jnp.concatenate([r0, r1], axis=1)


def diagonal_values(v_ref, b):
    _, kloc, bs, npt = v_ref.shape
    zero = jnp.zeros((bs, npt), BF16)
    rows = []
    for l in range(kloc):
        v = v_ref[b, l]
        rows.append(jnp.concatenate([v, zero], axis=1))
        rows.append(jnp.concatenate([zero, v], axis=1))
    return jnp.concatenate(rows, axis=0)


def density_kernel(
    flag_ref, r_ref, c_hbm, v_hbm, v2_hbm, d_ref, c_ref, v_ref, v2_ref, hi_s, lo_s, even, odd, sem
):
    nbat, kloc, _, npt = v_ref.shape
    rows = r_ref.shape[1]
    keys = c_ref.shape[1]
    get_c = pltpu.make_async_copy(c_hbm, c_ref, sem.at[0])
    get_v = pltpu.make_async_copy(v_hbm, v_ref, sem.at[1])
    get_v2 = pltpu.make_async_copy(v2_hbm, v2_ref, sem.at[2])
    get_c.start()
    get_v.start()
    get_v2.start()

    def build(jp, rhs_ref, parts):
        rhs = rhs_ref[...]
        res = dot_nn(c_ref[0], rhs)
        if parts == 2:
            res += dot_nn(c_ref[1], rhs)
        res = res.reshape(keys // SUB, SUB, 2 * LANES)
        hi, lo = split_pair(jnp.concatenate([res[:, :, :LANES], res[:, :, LANES:]], axis=1))
        at = pl.ds(pl.multiple_of(jp * 2 * SUB, 2 * SUB), 2 * SUB)
        hi_s[:, at, :] = hi
        lo_s[:, at, :] = lo

    even[...] = slot_rows(r_ref, 0)
    get_c.wait()

    def loop(parts):

        def step(i, carry):
            odd[...] = slot_rows(r_ref, 2 * i + 1)
            build(2 * i, even, parts)
            even[...] = slot_rows(r_ref, jnp.minimum(2 * i + 2, rows // 2 - 1))
            build(2 * i + 1, odd, parts)
            return carry

        lax.fori_loop(0, rows // 4, step, 0)

    @pl.when(flag_ref[0, 0] == 0)
    def _():
        loop(1)

    @pl.when(flag_ref[0, 0] != 0)
    def _():
        loop(2)

    get_v.wait()
    get_v2.wait()

    def one_batch(b, carry):
        lhs = jnp.concatenate(
            [
                jnp.concatenate([hi_s[b * kloc + l] for l in range(kloc)], axis=1),
                jnp.concatenate([lo_s[b * kloc + l] for l in range(kloc)], axis=1),
            ],
            axis=0,
        )
        image = dot_nn(lhs, diagonal_values(v_ref, b))
        image = image[: rows * SUB] + image[rows * SUB :]
        d = jnp.sum(image * v2_ref[b].astype(F32), axis=0, keepdims=True)
        d_ref[pl.ds(b, 1), :] = d[:, :npt] + d[:, npt:]
        return carry

    lax.fori_loop(0, nbat, one_batch, 0, unroll=2)


def potential_kernel(
    flag_ref, d_ref, ct_hbm, v_hbm, v2_hbm, o_ref, ct_ref, v_ref, v2_ref, hi_s, lo_s, pot_s, sem
):
    nbat, kloc, _, _ = v_ref.shape

    def get_batch(b):
        return (
            pltpu.make_async_copy(v_hbm.at[b], v_ref.at[b], sem.at[0, b]),
            pltpu.make_async_copy(v2_hbm.at[b], v2_ref.at[b], sem.at[1, b]),
        )

    get_ct = pltpu.make_async_copy(ct_hbm, ct_ref, sem.at[2, 0])
    for b in range(nbat):
        for copy in get_batch(b):
            copy.start()
    get_ct.start()
    slabs, rows, cap, _ = o_ref.shape
    group = kloc * SUB
    d = d_ref[...]
    pot = d / jnp.sqrt(1.0 + d * d)
    pot_s[...] = jnp.concatenate([pot, pot], axis=1)

    def one_batch(b, carry):
        for copy in get_batch(b):
            copy.wait()
        weighted = (v2_ref[b].astype(F32) * pot_s[pl.ds(b, 1), :]).astype(BF16)
        g = dot_nt(weighted, diagonal_values(v_ref, b))
        at = pl.ds(pl.multiple_of(b * group, group), group)
        for j in range(rows):
            x = jnp.concatenate(
                [g[j * SUB : (j + 1) * SUB, l * LANES : (l + 1) * LANES] for l in range(kloc)],
                axis=0,
            )
            hi, lo = split_pair(x)
            hi_s[j, at, :] = hi
            lo_s[j, at, :] = lo
        return carry

    lax.fori_loop(0, nbat, one_batch, 0, unroll=1)
    get_ct.wait()

    def sums(jp, parts):
        hi = jnp.concatenate([hi_s[2 * jp], hi_s[2 * jp + 1]], axis=1)
        lo = jnp.concatenate([lo_s[2 * jp], lo_s[2 * jp + 1]], axis=1)
        lhs = [ct_ref[n] for n in range(parts) for _ in range(2)]
        out = dot_nn(jnp.concatenate(lhs, axis=1), jnp.concatenate([hi, lo] * parts, axis=0))
        out = out.astype(BF16)
        o_ref[:, 2 * jp] = out[:, :LANES].reshape(slabs, cap, LANES)
        o_ref[:, 2 * jp + 1] = out[:, LANES:].reshape(slabs, cap, LANES)

    def loop(parts, unroll):
        def step(jp, carry):
            sums(jp, parts)
            return carry

        lax.fori_loop(0, rows // 2, step, 0, unroll=unroll)

    @pl.when(flag_ref[0, 0] == 0)
    def _():
        loop(1, 2)

    @pl.when(flag_ref[0, 0] != 0)
    def _():
        loop(2, 1)


def owner_kernel(hot_ref, ret_ref, o_ref):
    bs = o_ref.shape[2]
    half = o_ref.shape[1] // 2
    hot = hot_ref[...]
    parts = []
    for jp in range(half // 2):
        res = dot_nn(hot, slot_rows(ret_ref, jp))
        parts += [res[:, :LANES], res[:, LANES:]]
    sums = jnp.swapaxes(jnp.stack(parts, axis=0), 0, 1)
    o_ref[:, :half] = sums[:, :, :bs]
    o_ref[:, half:] = sums[:, :, bs:]


SMEM = pl.BlockSpec(memory_space=pltpu.SMEM)
VMEM = pl.BlockSpec(memory_space=pltpu.VMEM)
HBM = pl.BlockSpec(memory_space=pltpu.HBM)


def kernel_call(kernel, name, mib, **kwargs):
    params = pltpu.CompilerParams(vmem_limit_bytes=mib << 20)
    return pl.pallas_call(kernel, compiler_params=params, name=name, **kwargs)


def in_hbm(x):
    return pltpu.with_memory_space_constraint(x, pltpu.HBM)


def exchange(x):
    return lax.all_to_all(x, "slab", split_axis=0, concat_axis=0, tiled=True)


def body(p_blocks, basis_vals, need_list, tasks, task_counts):
    own = p_blocks[0]
    blk_dev, bs, _ = own.shape
    nbat, kloc, _, npt = basis_vals.shape
    slabs, cap = need_list.shape[2:]
    slots = slabs * cap
    half = bs // 2
    keys = nbat * kloc * kloc
    wide = jax.ShapeDtypeStruct((slabs, half, cap, LANES), BF16)

    wanted = kernel_call(
        turn_kernel,
        "turn",
        4,
        out_shape=jax.ShapeDtypeStruct((slabs, 1, cap), jnp.int32),
        in_specs=[VMEM],
        out_specs=VMEM,
    )(need_list[0, 0].T)
    requested = exchange(wanted)

    own_rows = kernel_call(
        own_kernel,
        "own",
        8,
        out_shape=jax.ShapeDtypeStruct((half // 2, blk_dev, 2 * LANES), BF16),
        in_specs=[VMEM],
        out_specs=VMEM,
    )(own)

    sent, hot = kernel_call(
        send_kernel,
        "send",
        8,
        out_shape=(pltpu.HBM(wide.shape, BF16), jax.ShapeDtypeStruct((slots, blk_dev), BF16)),
        in_specs=[VMEM, VMEM],
        out_specs=(HBM, VMEM),
        scratch_shapes=[pltpu.VMEM(wide.shape, BF16), pltpu.SemaphoreType.DMA((4,))],
    )(requested, own_rows)
    received = exchange(sent)

    counts, counts_t, v2, hot_t, flag = kernel_call(
        prep_kernel,
        "prep",
        16,
        out_shape=(
            jax.ShapeDtypeStruct((2, keys, slots), BF16),
            jax.ShapeDtypeStruct((2, slots, keys), BF16),
            jax.ShapeDtypeStruct((nbat, half * kloc, 2 * npt), BF16),
            jax.ShapeDtypeStruct((blk_dev, slots), BF16),
            jax.ShapeDtypeStruct((1, 1), jnp.int32),
        ),
        in_specs=[SMEM, VMEM, VMEM, VMEM],
        out_specs=(VMEM, VMEM, VMEM, VMEM, SMEM),
    )(task_counts, tasks[0, 0], basis_vals, hot)

    partial = kernel_call(
        density_kernel,
        "density",
        16,
        out_shape=jax.ShapeDtypeStruct((nbat, npt), F32),
        in_specs=[SMEM, VMEM, HBM, HBM, HBM],
        out_specs=VMEM,
        scratch_shapes=[
            pltpu.VMEM(counts.shape, BF16),
            pltpu.VMEM(basis_vals.shape, BF16),
            pltpu.VMEM(v2.shape, BF16),
        ]
        + [pltpu.VMEM((nbat * kloc, half * SUB, LANES), BF16)] * 2
        + [pltpu.VMEM((slots, 2 * LANES), BF16)] * 2
        + [pltpu.SemaphoreType.DMA((3,))],
    )(flag, received, in_hbm(counts), in_hbm(basis_vals), in_hbm(v2))
    density = lax.psum(partial, "blk")

    slot_sums = kernel_call(
        potential_kernel,
        "potential",
        16,
        out_shape=wide,
        in_specs=[SMEM, VMEM, HBM, HBM, HBM],
        out_specs=VMEM,
        scratch_shapes=[
            pltpu.VMEM(counts_t.shape, BF16),
            pltpu.VMEM(basis_vals.shape, BF16),
            pltpu.VMEM(v2.shape, BF16),
        ]
        + [pltpu.VMEM((half, keys, LANES), BF16)] * 2
        + [pltpu.VMEM((nbat, 2 * npt), F32), pltpu.SemaphoreType.DMA((3, nbat))],
    )(flag, density, in_hbm(counts_t), in_hbm(basis_vals), in_hbm(v2))
    returned = exchange(slot_sums)

    owner_sums = kernel_call(
        owner_kernel,
        "owner",
        8,
        out_shape=jax.ShapeDtypeStruct((blk_dev, bs, bs), F32),
        in_specs=[VMEM, VMEM],
        out_specs=VMEM,
    )(hot_t, returned)
    return (density, owner_sums[None])


def solution(mesh):
    in_specs = (
        P("blk", "slab", None, None),
        P("slab", None, None, None),
        P("blk", "slab", None, None),
        P("blk", "slab", None, None),
        P("blk", "slab"),
    )
    out_specs = (P("slab", None), P("blk", "slab", None, None))
    return jax.shard_map(body, mesh=mesh, in_specs=in_specs, out_specs=out_specs, check_vma=False)
```

time: 134 us -> 115 us (0.86)
  blocking collectives: 2.47 us -> 37.9 us
  waiting for transfers between devices: 61.8 us -> 32.1 us
  starting transfers between devices: 31.3 us -> 16.6 us
  Pallas kernels: 30 us -> 22.2 us
  local copies, waits for them, and re-layouts: 6.1 us -> 4.29 us
    all_to_all x0 -> x1, blocking collectives: none -> 35.4 us  [exchange(): return lax.all_to_all(x, 'slab', split_axis=0, concat_axis=0, tiled=True)]
    all_to_all x5 -> x2, waiting for transfers between devices: 61.8 us -> 32.1 us  [exchange(): return lax.all_to_all(x, 'slab', split_axis=0, concat_axis=0, tiled=True)]
    all_to_all x5 -> x2, starting transfers between devices: 31.3 us -> 16.6 us  [exchange(): return lax.all_to_all(x, 'slab', split_axis=0, concat_axis=0, tiled=True)]
    pallas_call x10 -> x7, Pallas kernels: 30 us -> 22.2 us  [the longest x1 8.2 us: body(): kernel_call(potential_kernel, 'potential', 16, out_shape=wide, in_specs=[...]
    unnamed x19 -> x16, local copies, waits for them, and re-layouts: 6.1 us -> 4.29 us
  transfers between devices with their start and end apart: 5 -> 2, of which waited for: 5 -> 2; matrix products, arithmetic and copies ran while one was open for 0% -> 0% of each run, Pallas kernels for 11% -> 2%
where the time goes in v3:
time: 115 us; the launch traced here: 114 us
  blocking collectives  37.9 us (33%)
  waiting for transfers between devices  32.1 us (28%)
  Pallas kernels  22.2 us (19%)
  starting transfers between devices  16.6 us (14%)
  local copies, waits for them, and re-layouts  4.29 us (4%)
  between operations  1.4 us (1%)
    all_to_all x1, blocking collectives, exchange(): return lax.all_to_all(x, 'slab', split_axis=0, concat_axis=0, tiled=True)  35.4 us
    all_to_all x2, waiting for transfers between devices, exchange(): return lax.all_to_all(x, 'slab', split_axis=0, concat_axis=0, tiled=True)  32.1 us
    all_to_all x2, starting transfers between devices, exchange(): return lax.all_to_all(x, 'slab', split_axis=0, concat_axis=0, tiled=True)  16.6 us
    pallas_call x1, Pallas kernels, body(): kernel_call(potential_kernel, 'potential', 16, out_shape=wide, in_specs=[...  8.2 us
    pallas_call x1, Pallas kernels, body(): kernel_call(density_kernel, 'density', 16, out_shape=jax.ShapeDtypeStruct...  7.7 us
    unnamed x16, local copies, waits for them, and re-layouts  4.29 us
    psum x1, blocking collectives, body(): density = lax.psum(partial, 'blk')  2.47 us
  transfers between devices with their start and end apart: 2, of which 2 were waited for; matrix products, arithmetic and copies ran while one was open for 0% of the time, Pallas kernels for 2%

profile of v3, /device:TPU:0, one launch (start us, length us, event | category | flops | bytes accessed | tf_op | source)
XLA Modules:
  0.0 114.4 jit_solution(5769342564321213215)
XLA Ops:
  0.6 0.0 copy-start.7
  0.6 0.7 copy-done.7
  1.3 0.7 turn.1
  2.0 11.5 %all-to-all-start = ((s32[64,1,4]{2,1,0:T(1,128)}), s32[64,1,4]{2,1,0:T(1,128)S(1)}, u32[]{:S(2)}, u32[]{:S(2)}) async-start(s32[64,1,4]{2,1,0:T(1,128)} %turn.1), calls=%async_computation | async-start | bytes 65536 | tf_op jit(solution)/shard_map/all_to_all | solution.py:294
  13.5 0.0 copy-start.2
  13.6 1.0 copy-done.2
  14.6 0.2 own.1.own_ref
  14.8 8.2 %all-to-all-done.req_ref = s32[64,1,4]{2,1,0:T(1,128)S(1)} async-done(((s32[64,1,4]{2,1,0:T(1,128)}), s32[64,1,4]{2,1,0:T(1,128)S(1)}, u32[]{:S(2)}, u32[]{:S(2)}) %all-to-all-start) | async-done | bytes 1056 | tf_op jit(solution)/shard_map/all_to_all | solution.py:294
  23.1 1.9 %send.1 = (bf16[64,32,4,128]{3,2,1,0:T(4,128)(2,1)}, bf16[256,32]{1,0:T(8,128)(2,1)S(1)}) custom-call(s32[64,1,4]{2,1,0:T(1,128)S(1)} %all-to-all-done.req_ref, bf16[16,32,256]{2,1,0:T(8,128)(2,1)S(1)} %own.1.own_ref), custom_call_target="tpu_custom_call" | custom-call | tf_op jit(solution)/shard_map/send/pallas_call | solution.py:326
  25.0 0.0 copy-start
  25.0 0.0 copy-start.5
  25.0 5.1 %all-to-all-start.1 = ((bf16[64,32,4,128]{3,2,1,0:T(4,128)(2,1)}), bf16[64,32,4,128]{3,2,1,0:T(4,128)(2,1)S(1)}, u32[]{:S(2)}, u32[]{:S(2)}) async-start(bf16[64,32,4,128]{3,2,1,0:T(4,128)(2,1)} %get-tuple-element.11), calls=%async_computation.1 | async-start | bytes 4194304 | tf_op jit(solution)/shard_map/all_to_all | solution.py:294
  30.8 0.0 copy-done
  30.8 1.7 %prep.1 = (bf16[2,512,256]{2,1,0:T(8,128)(2,1)S(1)}, bf16[2,256,512]{2,1,0:T(8,128)(2,1)S(1)}, bf16[8,256,256]{2,1,0:T(8,128)(2,1)S(1)}, bf16[32,256]{1,0:T(8,128)(2,1)S(1)}, s32[1,1]{1,0:T(1,128)}) custom-call(s32[1,1]{1,0:T(1,128)S(6)} %copy.7.count_ref, s32[4,1536]{1,0:T(4,128)S(1)} %bitcast.7, bf16[8,8,64,128]{3,2,1,0:T(8,128)(2,1)S(1)} %copy-done, ...), custom_call_target="tpu_custom_call" | custom-call | tf_op jit(solution)/shard_map/prep/pallas_call | solution.py:337
  32.5 0.0 copy-start.1
  32.5 1.0 copy-done.1
  33.5 0.8 copy-done.3
  34.3 0.8 copy-done.4
  35.1 23.8 %all-to-all-done.1.r_ref = bf16[64,32,4,128]{3,2,1,0:T(4,128)(2,1)S(1)} async-done(((bf16[64,32,4,128]{3,2,1,0:T(4,128)(2,1)}), bf16[64,32,4,128]{3,2,1,0:T(4,128)(2,1)S(1)}, u32[]{:S(2)}, u32[]{:S(2)}) %all-to-all-start.1) | async-done | bytes 2097184 | tf_op jit(solution)/shard_map/all_to_all | solution.py:294
  58.9 7.7 %density.1 = f32[8,128]{1,0:T(8,128)S(1)} custom-call(s32[1,1]{1,0:T(1,128)} %get-tuple-element.10.flag_ref, bf16[64,32,4,128]{3,2,1,0:T(4,128)(2,1)S(1)} %all-to-all-done.1.r_ref, bf16[2,512,256]{2,1,0:T(8,128)(2,1)} %copy-done.4, bf16[8,8,64,128]{3,2,1,0:T(8,128)(2,1)} %v_hbm.3, bf16[8,256,256]{2,1,0:T(8,128)(2,1)} %copy-done.1), custom_call_target="tpu_custom_call" | custom-call | tf_op jit(solution)/shard_map/density/pallas_call | solution.py:352
  66.6 2.5 %psum.7.d_ref = f32[8,128]{1,0:T(8,128)S(1)} all-reduce(f32[8,128]{1,0:T(8,128)S(1)} %density.1), channel_id=1, replica_groups=mesh['slab'=64,'blk'=2] {'blk'}, use_global_device_ids=true, to_apply=%region_0.0 | all-reduce | flops 1024 | bytes 8192 | tf_op jit(solution)/shard_map/psum | solution.py:368
  69.1 8.2 %potential.1 = bf16[64,32,4,128]{3,2,1,0:T(4,128)(2,1)S(1)} custom-call(s32[1,1]{1,0:T(1,128)} %get-tuple-element.10.flag_ref, f32[8,128]{1,0:T(8,128)S(1)} %psum.7.d_ref, bf16[2,256,512]{2,1,0:T(8,128)(2,1)} %copy-done.3, bf16[8,8,64,128]{3,2,1,0:T(8,128)(2,1)} %v_hbm.3, bf16[8,256,256]{2,1,0:T(8,128)(2,1)} %copy-done.1), custom_call_target="tpu_custom_call" | custom-call | tf_op jit(solution)/shard_map/potential/pallas_call | solution.py:370
  77.3 35.4 %all_to_all.15.ret_ref = bf16[64,32,4,128]{3,2,1,0:T(4,128)(2,1)S(1)} all-to-all(bf16[64,32,4,128]{3,2,1,0:T(4,128)(2,1)S(1)} %potential.1), channel_id=1, replica_groups=mesh['slab'=64,'blk'=2] {'slab'}, dimensions={0} | all-to-all | bytes 4194304 | tf_op jit(solution)/shard_map/all_to_all | solution.py:294
  112.7 1.7 %owner.1 = f32[32,64,64]{2,1,0:T(8,128)} custom-call(bf16[32,256]{1,0:T(8,128)(2,1)S(1)} %get-tuple-element.14.hot_ref, bf16[64,32,4,128]{3,2,1,0:T(4,128)(2,1)S(1)} %all_to_all.15.ret_ref), custom_call_target="tpu_custom_call" | custom-call | tf_op jit(solution)/shard_map/owner/pallas_call | solution.py:387
  (5 shorter events, 0.0 us)
Async XLA Ops:
  0.6 0.7 copy-start.7
  2.0 21.0 %all-to-all-start = ((s32[64,1,4]{2,1,0:T(1,128)}), s32[64,1,4]{2,1,0:T(1,128)S(1)}, u32[]{:S(2)}, u32[]{:S(2)}) async-start(s32[64,1,4]{2,1,0:T(1,128)} %turn.1), calls=%async_computation | async-start | bytes 65536 | tf_op jit(solution)/shard_map/all_to_all | solution.py:294
  13.5 1.0 copy-start.2
  25.0 5.8 %copy-start = (bf16[8,8,64,128]{3,2,1,0:T(8,128)(2,1)S(1)}, bf16[8,8,64,128]{3,2,1,0:T(8,128)(2,1)}, u32[]{:S(2)}) copy-start(bf16[8,8,64,128]{3,2,1,0:T(8,128)(2,1)} %v_hbm.3) | copy-start | bytes 3145732
  25.0 5.8 %copy-start.5 = (s32[1,1,4,1536]{3,2,1,0:T(4,128)S(1)}, s32[1,1,4,1536]{3,2,1,0:T(4,128)}, u32[]{:S(2)}) copy-start(s32[1,1,4,1536]{3,2,1,0:T(4,128)} %param.8) | copy-start | bytes 73732
  25.0 33.9 %all-to-all-start.1 = ((bf16[64,32,4,128]{3,2,1,0:T(4,128)(2,1)}), bf16[64,32,4,128]{3,2,1,0:T(4,128)(2,1)S(1)}, u32[]{:S(2)}, u32[]{:S(2)}) async-start(bf16[64,32,4,128]{3,2,1,0:T(4,128)(2,1)} %get-tuple-element.11), calls=%async_computation.1 | async-start | bytes 4194304 | tf_op jit(solution)/shard_map/all_to_all | solution.py:294
  32.5 1.0 copy-start.1
  33.5 0.8 copy-start.3
  34.3 0.8 copy-start.4
  69.1 8.2 %copy-start.6 = (f32[8,128]{1,0:T(8,128)}, f32[8,128]{1,0:T(8,128)S(1)}, u32[]{:S(2)}) copy-start(f32[8,128]{1,0:T(8,128)S(1)} %psum.7.d_ref) | copy-start | bytes 12292

commit v4 on v3

--- a/solution.py
+++ b/solution.py
@@ -10,6 +10,8 @@
 LANES = 128
 SUB = 8
 TASK_STEP = 512
+GROUP = 4
+BATCH_GROUP = 4
 
 
 def dot_nn(a, b):
@@ -40,7 +42,7 @@
 
 
 def prep_kernel(
-    count_ref, tasks_ref, v_ref, hot_ref, c_ref, ct_ref, v2_ref, hot_t_ref, flag_ref
+    count_ref, tasks_ref, v_ref, hot_ref, c_ref, ct_ref, v2_ref, vt_ref, hot_t_ref, flag_ref
 ):
     hot_t_ref[...] = jnp.transpose(hot_ref[...].astype(F32)).astype(BF16)
     nbat, kloc, bs, npt = v_ref.shape
@@ -77,6 +79,11 @@
         for h in range(2):
             part = vals[h * half : (h + 1) * half].reshape(half * kloc, npt)
             v2_ref[b, :, h * npt : (h + 1) * npt] = part.astype(BF16)
+        zero = jnp.zeros((npt, bs), F32)
+        for l in range(kloc):
+            vt = jnp.transpose(v_ref[b, l].astype(F32))
+            vt_ref[b, l, :npt] = jnp.concatenate([vt, zero], axis=1).astype(BF16)
+            vt_ref[b, l, npt:] = jnp.concatenate([zero, vt], axis=1).astype(BF16)
 
 
 def request_hot(req_ref, nblk):
@@ -132,7 +139,7 @@
 
 
 def density_kernel(
-    flag_ref, r_ref, c_hbm, v_hbm, v2_hbm, d_ref, c_ref, v_ref, v2_ref, hi_s, lo_s, even, odd, sem
+    flag_ref, r_ref, c_hbm, v_hbm, v2_hbm, d_ref, c_ref, v_ref, v2_ref, hi_s, lo_s, sem
 ):
     nbat, kloc, _, npt = v_ref.shape
     rows = r_ref.shape[1]
@@ -144,8 +151,8 @@
     get_v.start()
     get_v2.start()
 
-    def build(jp, rhs_ref, parts):
-        rhs = rhs_ref[...]
+    def build(jp, parts):
+        rhs = slot_rows(r_ref, jp)
         res = dot_nn(c_ref[0], rhs)
         if parts == 2:
             res += dot_nn(c_ref[1], rhs)
@@ -155,27 +162,23 @@
         hi_s[:, at, :] = hi
         lo_s[:, at, :] = lo
 
-    even[...] = slot_rows(r_ref, 0)
     get_c.wait()
 
-    def loop(parts):
-
+    def loop(parts, group):
         def step(i, carry):
-            odd[...] = slot_rows(r_ref, 2 * i + 1)
-            build(2 * i, even, parts)
-            even[...] = slot_rows(r_ref, jnp.minimum(2 * i + 2, rows // 2 - 1))
-            build(2 * i + 1, odd, parts)
+            for n in range(group):
+                build(group * i + n, parts)
             return carry
 
-        lax.fori_loop(0, rows // 4, step, 0)
+        lax.fori_loop(0, rows // (2 * group), step, 0)
 
     @pl.when(flag_ref[0, 0] == 0)
     def _():
-        loop(1)
+        loop(1, GROUP)
 
     @pl.when(flag_ref[0, 0] != 0)
     def _():
-        loop(2)
+        loop(2, 1)
 
     get_v.wait()
     get_v2.wait()
@@ -194,17 +197,18 @@
         d_ref[pl.ds(b, 1), :] = d[:, :npt] + d[:, npt:]
         return carry
 
-    lax.fori_loop(0, nbat, one_batch, 0, unroll=2)
+    lax.fori_loop(0, nbat, one_batch, 0, unroll=4)
 
 
 def potential_kernel(
-    flag_ref, d_ref, ct_hbm, v_hbm, v2_hbm, o_ref, ct_ref, v_ref, v2_ref, hi_s, lo_s, pot_s, sem
+    flag_ref, d_ref, ct_hbm, vt_hbm, v2_hbm, o_ref, ct_ref, vt_ref, v2_ref, g_s, pot_s, sem
 ):
-    nbat, kloc, _, _ = v_ref.shape
+    nbat, kloc, _, _ = vt_ref.shape
+    slabs, rows, cap, _ = o_ref.shape
 
     def get_batch(b):
         return (
-            pltpu.make_async_copy(v_hbm.at[b], v_ref.at[b], sem.at[0, b]),
+            pltpu.make_async_copy(vt_hbm.at[b], vt_ref.at[b], sem.at[0, b]),
             pltpu.make_async_copy(v2_hbm.at[b], v2_ref.at[b], sem.at[1, b]),
         )
 
@@ -213,50 +217,50 @@
         for copy in get_batch(b):
             copy.start()
     get_ct.start()
-    slabs, rows, cap, _ = o_ref.shape
-    group = kloc * SUB
     d = d_ref[...]
     pot = d / jnp.sqrt(1.0 + d * d)
     pot_s[...] = jnp.concatenate([pot, pot], axis=1)
 
-    def one_batch(b, carry):
-        for copy in get_batch(b):
-            copy.wait()
+    def one_batch(b):
         weighted = (v2_ref[b].astype(F32) * pot_s[pl.ds(b, 1), :]).astype(BF16)
-        g = dot_nt(weighted, diagonal_values(v_ref, b))
-        at = pl.ds(pl.multiple_of(b * group, group), group)
-        for j in range(rows):
-            x = jnp.concatenate(
-                [g[j * SUB : (j + 1) * SUB, l * LANES : (l + 1) * LANES] for l in range(kloc)],
-                axis=0,
-            )
-            hi, lo = split_pair(x)
-            hi_s[j, at, :] = hi
-            lo_s[j, at, :] = lo
+        for lp in range(kloc // 2):
+            rhs = jnp.concatenate([vt_ref[b, 2 * lp], vt_ref[b, 2 * lp + 1]], axis=1)
+            g = dot_nn(weighted, rhs).reshape(rows, SUB, 2 * LANES)
+            g = jnp.concatenate([g[:, :, :LANES], g[:, :, LANES:]], axis=1)
+            row = pl.multiple_of((b * kloc + 2 * lp) * SUB, 2 * SUB)
+            g_s[:, pl.ds(row, 2 * SUB), :] = g.astype(BF16)
+
+    def some_batches(i, carry):
+        for n in range(BATCH_GROUP):
+            for copy in get_batch(i * BATCH_GROUP + n):
+                copy.wait()
+        for n in range(BATCH_GROUP):
+            one_batch(i * BATCH_GROUP + n)
         return carry
 
-    lax.fori_loop(0, nbat, one_batch, 0, unroll=1)
+    lax.fori_loop(0, nbat // BATCH_GROUP, some_batches, 0)
     get_ct.wait()
 
     def sums(jp, parts):
-        hi = jnp.concatenate([hi_s[2 * jp], hi_s[2 * jp + 1]], axis=1)
-        lo = jnp.concatenate([lo_s[2 * jp], lo_s[2 * jp + 1]], axis=1)
-        lhs = [ct_ref[n] for n in range(parts) for _ in range(2)]
-        out = dot_nn(jnp.concatenate(lhs, axis=1), jnp.concatenate([hi, lo] * parts, axis=0))
+        rhs = jnp.concatenate([g_s[2 * jp], g_s[2 * jp + 1]], axis=1)
+        out = dot_nn(ct_ref[0], rhs)
+        if parts == 2:
+            out += dot_nn(ct_ref[1], rhs)
         out = out.astype(BF16)
         o_ref[:, 2 * jp] = out[:, :LANES].reshape(slabs, cap, LANES)
         o_ref[:, 2 * jp + 1] = out[:, LANES:].reshape(slabs, cap, LANES)
 
-    def loop(parts, unroll):
-        def step(jp, carry):
-            sums(jp, parts)
+    def loop(parts, group):
+        def step(i, carry):
+            for n in range(group):
+                sums(group * i + n, parts)
             return carry
 
-        lax.fori_loop(0, rows // 2, step, 0, unroll=unroll)
+        lax.fori_loop(0, rows // (2 * group), step, 0)
 
     @pl.when(flag_ref[0, 0] == 0)
     def _():
-        loop(1, 2)
+        loop(1, 8)
 
     @pl.when(flag_ref[0, 0] != 0)
     def _():
@@ -334,19 +338,20 @@
     )(requested, own_rows)
     received = exchange(sent)
 
-    counts, counts_t, v2, hot_t, flag = kernel_call(
+    counts, counts_t, v2, vt, hot_t, flag = kernel_call(
         prep_kernel,
         "prep",
-        16,
+        24,
         out_shape=(
             jax.ShapeDtypeStruct((2, keys, slots), BF16),
             jax.ShapeDtypeStruct((2, slots, keys), BF16),
             jax.ShapeDtypeStruct((nbat, half * kloc, 2 * npt), BF16),
+            jax.ShapeDtypeStruct((nbat, kloc, 2 * npt, LANES), BF16),
             jax.ShapeDtypeStruct((blk_dev, slots), BF16),
             jax.ShapeDtypeStruct((1, 1), jnp.int32),
         ),
         in_specs=[SMEM, VMEM, VMEM, VMEM],
-        out_specs=(VMEM, VMEM, VMEM, VMEM, SMEM),
+        out_specs=(VMEM, VMEM, VMEM, VMEM, VMEM, SMEM),
     )(task_counts, tasks[0, 0], basis_vals, hot)
 
     partial = kernel_call(
@@ -362,7 +367,6 @@
             pltpu.VMEM(v2.shape, BF16),
         ]
         + [pltpu.VMEM((nbat * kloc, half * SUB, LANES), BF16)] * 2
-        + [pltpu.VMEM((slots, 2 * LANES), BF16)] * 2
         + [pltpu.SemaphoreType.DMA((3,))],
     )(flag, received, in_hbm(counts), in_hbm(basis_vals), in_hbm(v2))
     density = lax.psum(partial, "blk")
@@ -370,18 +374,19 @@
     slot_sums = kernel_call(
         potential_kernel,
         "potential",
-        16,
+        24,
         out_shape=wide,
         in_specs=[SMEM, VMEM, HBM, HBM, HBM],
         out_specs=VMEM,
         scratch_shapes=[
             pltpu.VMEM(counts_t.shape, BF16),
-            pltpu.VMEM(basis_vals.shape, BF16),
+            pltpu.VMEM(vt.shape, BF16),
             pltpu.VMEM(v2.shape, BF16),
-        ]
-        + [pltpu.VMEM((half, keys, LANES), BF16)] * 2
-        + [pltpu.VMEM((nbat, 2 * npt), F32), pltpu.SemaphoreType.DMA((3, nbat))],
-    )(flag, density, in_hbm(counts_t), in_hbm(basis_vals), in_hbm(v2))
+            pltpu.VMEM((half, keys, LANES), BF16),
+            pltpu.VMEM((nbat, 2 * npt), F32),
+            pltpu.SemaphoreType.DMA((3, nbat)),
+        ],
+    )(flag, density, in_hbm(counts_t), in_hbm(vt), in_hbm(v2))
     returned = exchange(slot_sums)
 
     owner_sums = kernel_call(

time: 115 us -> 111 us (0.965)
  waiting for transfers between devices: 32.1 us -> 29.2 us
  Pallas kernels: 22.2 us -> 19.7 us
  local copies, waits for them, and re-layouts: 4.29 us -> 6.23 us
    all_to_all x2, waiting for transfers between devices: 32.1 us -> 29.2 us  [exchange(): return lax.all_to_all(x, 'slab', split_axis=0, concat_axis=0, tiled=True)]
    unnamed x16 -> x18, local copies, waits for them, and re-layouts: 4.29 us -> 6.23 us
    pallas_call x2, Pallas kernels: 9.9 us -> 8.4 us  [the longest x1 5.78 us: body(): kernel_call(potential_kernel, 'potential', 24, out_shape=wide, in_specs=[...]
  transfers between devices with their start and end apart: 2 -> 2, of which waited for: 2 -> 2; matrix products, arithmetic and copies ran while one was open for 0% -> 0% of each run, Pallas kernels for 2% -> 3%
where the time goes in v4:
time: 111 us
  blocking collectives  37.9 us (34%)
  waiting for transfers between devices  29.2 us (26%)
  Pallas kernels  19.7 us (18%)
  starting transfers between devices  16.6 us (15%)
  local copies, waits for them, and re-layouts  6.23 us (6%)
  between operations  1.4 us (1%)
    all_to_all x1, blocking collectives, exchange(): return lax.all_to_all(x, 'slab', split_axis=0, concat_axis=0, tiled=True)  35.4 us
    all_to_all x2, waiting for transfers between devices, exchange(): return lax.all_to_all(x, 'slab', split_axis=0, concat_axis=0, tiled=True)  29.2 us
    all_to_all x2, starting transfers between devices, exchange(): return lax.all_to_all(x, 'slab', split_axis=0, concat_axis=0, tiled=True)  16.6 us
    pallas_call x1, Pallas kernels, body(): kernel_call(density_kernel, 'density', 16, out_shape=jax.ShapeDtypeStruct...  6.7 us
    unnamed x18, local copies, waits for them, and re-layouts  6.23 us
    pallas_call x1, Pallas kernels, body(): kernel_call(potential_kernel, 'potential', 24, out_shape=wide, in_specs=[...  5.78 us
    pallas_call x1, Pallas kernels, body(): kernel_call(prep_kernel, 'prep', 24, out_shape=(jax.ShapeDtypeStruct((2,...  2.62 us
    psum x1, blocking collectives, body(): density = lax.psum(partial, 'blk')  2.47 us
  transfers between devices with their start and end apart: 2, of which 2 were waited for; matrix products, arithmetic and copies ran while one was open for 0% of the time, Pallas kernels for 3%

profile of v4, /device:TPU:0, one launch (start us, length us, event | category | flops | bytes accessed | tf_op | source)
XLA Modules:
  0.0 111.1 jit_solution(5892499945406180369)
XLA Ops:
  0.6 0.0 copy-start.8
  0.6 0.7 copy-done.8
  1.3 0.7 turn.1
  2.0 11.5 %all-to-all-start = ((s32[64,1,4]{2,1,0:T(1,128)}), s32[64,1,4]{2,1,0:T(1,128)S(1)}, u32[]{:S(2)}, u32[]{:S(2)}) async-start(s32[64,1,4]{2,1,0:T(1,128)} %turn.1), calls=%async_computation | async-start | bytes 65536 | tf_op jit(solution)/shard_map/all_to_all | solution.py:298
  13.5 0.0 copy-start.4
  13.6 1.0 copy-done.4
  14.6 0.2 own.1.own_ref
  14.8 8.2 %all-to-all-done.req_ref = s32[64,1,4]{2,1,0:T(1,128)S(1)} async-done(((s32[64,1,4]{2,1,0:T(1,128)}), s32[64,1,4]{2,1,0:T(1,128)S(1)}, u32[]{:S(2)}, u32[]{:S(2)}) %all-to-all-start) | async-done | bytes 1056 | tf_op jit(solution)/shard_map/all_to_all | solution.py:298
  23.1 1.9 %send.1 = (bf16[64,32,4,128]{3,2,1,0:T(4,128)(2,1)}, bf16[256,32]{1,0:T(8,128)(2,1)S(1)}) custom-call(s32[64,1,4]{2,1,0:T(1,128)S(1)} %all-to-all-done.req_ref, bf16[16,32,256]{2,1,0:T(8,128)(2,1)S(1)} %own.1.own_ref), custom_call_target="tpu_custom_call" | custom-call | tf_op jit(solution)/shard_map/send/pallas_call | solution.py:330
  25.0 0.0 copy-start.2
  25.0 0.0 copy-start.6
  25.0 5.1 %all-to-all-start.1 = ((bf16[64,32,4,128]{3,2,1,0:T(4,128)(2,1)}), bf16[64,32,4,128]{3,2,1,0:T(4,128)(2,1)S(1)}, u32[]{:S(2)}, u32[]{:S(2)}) async-start(bf16[64,32,4,128]{3,2,1,0:T(4,128)(2,1)} %get-tuple-element.12), calls=%async_computation.1 | async-start | bytes 4194304 | tf_op jit(solution)/shard_map/all_to_all | solution.py:298
  30.8 2.6 %prep.1 = (bf16[2,512,256]{2,1,0:T(8,128)(2,1)S(1)}, bf16[2,256,512]{2,1,0:T(8,128)(2,1)S(1)}, bf16[8,256,256]{2,1,0:T(8,128)(2,1)S(1)}, bf16[8,8,256,128]{3,2,1...) custom-call(s32[1,1]{1,0:T(1,128)S(6)} %copy.7.count_ref, s32[4,1536]{1,0:T(4,128)S(1)} %bitcast.7, ...), custom_call_target="tpu_custom_call" | custom-call | tf_op jit(solution)/shard_map/prep/pallas_call | solution.py:341
  33.4 1.9 %copy-done = bf16[8,8,256,128]{3,2,1,0:T(8,128)(2,1)} copy-done((bf16[8,8,256,128]{3,2,1,0:T(8,128)(2,1)}, bf16[8,8,256,128]{3,2,1,0:T(8,128)(2,1)S(1)}, u32[]{:S(2)}) %copy-start) | copy-done | bytes 4194328
  35.4 1.0 copy-done.1
  36.4 0.8 copy-done.3
  37.2 0.8 copy-done.5
  37.9 21.0 %all-to-all-done.1.r_ref = bf16[64,32,4,128]{3,2,1,0:T(4,128)(2,1)S(1)} async-done(((bf16[64,32,4,128]{3,2,1,0:T(4,128)(2,1)}), bf16[64,32,4,128]{3,2,1,0:T(4,128)(2,1)S(1)}, u32[]{:S(2)}, u32[]{:S(2)}) %all-to-all-start.1) | async-done | bytes 2097184 | tf_op jit(solution)/shard_map/all_to_all | solution.py:298
  58.9 6.7 %density.1 = f32[8,128]{1,0:T(8,128)S(1)} custom-call(s32[1,1]{1,0:T(1,128)} %get-tuple-element.11.flag_ref, bf16[64,32,4,128]{3,2,1,0:T(4,128)(2,1)S(1)} %all-to-all-done.1.r_ref, bf16[2,512,256]{2,1,0:T(8,128)(2,1)} %copy-done.5, bf16[8,8,64,128]{3,2,1,0:T(8,128)(2,1)} %v_hbm.1, bf16[8,256,256]{2,1,0:T(8,128)(2,1)} %copy-done.1), custom_call_target="tpu_custom_call" | custom-call | tf_op jit(solution)/shard_map/density/pallas_call | solution.py:357
  65.6 2.5 %psum.7.d_ref = f32[8,128]{1,0:T(8,128)S(1)} all-reduce(f32[8,128]{1,0:T(8,128)S(1)} %density.1), channel_id=1, replica_groups=mesh['slab'=64,'blk'=2] {'blk'}, use_global_device_ids=true, to_apply=%region_0.0 | all-reduce | flops 1024 | bytes 8192 | tf_op jit(solution)/shard_map/psum | solution.py:372
  68.1 5.8 %potential.1 = bf16[64,32,4,128]{3,2,1,0:T(4,128)(2,1)S(1)} custom-call(s32[1,1]{1,0:T(1,128)} %get-tuple-element.11.flag_ref, f32[8,128]{1,0:T(8,128)S(1)} %psum.7.d_ref, bf16[2,256,512]{2,1,0:T(8,128)(2,1)} %copy-done.3, bf16[8,8,256,128]{3,2,1,0:T(8,128)(2,1)} %copy-done, bf16[8,256,256]{2,1,0:T(8,128)(2,1)} %copy-done.1), custom_call_target="tpu_custom_call" | custom-call | tf_op jit(solution)/shard_map/potential/pallas_call | solution.py:374
  73.9 0.0 copy-done.7
  73.9 35.4 %all_to_all.15.ret_ref = bf16[64,32,4,128]{3,2,1,0:T(4,128)(2,1)S(1)} all-to-all(bf16[64,32,4,128]{3,2,1,0:T(4,128)(2,1)S(1)} %potential.1), channel_id=1, replica_groups=mesh['slab'=64,'blk'=2] {'slab'}, dimensions={0} | all-to-all | bytes 4194304 | tf_op jit(solution)/shard_map/all_to_all | solution.py:298
  109.4 1.7 %owner.1 = f32[32,64,64]{2,1,0:T(8,128)} custom-call(bf16[32,256]{1,0:T(8,128)(2,1)S(1)} %get-tuple-element.15.hot_ref, bf16[64,32,4,128]{3,2,1,0:T(4,128)(2,1)S(1)} %all_to_all.15.ret_ref), custom_call_target="tpu_custom_call" | custom-call | tf_op jit(solution)/shard_map/owner/pallas_call | solution.py:392
  (7 shorter events, 0.0 us)
Async XLA Ops:
  0.6 0.7 copy-start.8
  2.0 21.0 %all-to-all-start = ((s32[64,1,4]{2,1,0:T(1,128)}), s32[64,1,4]{2,1,0:T(1,128)S(1)}, u32[]{:S(2)}, u32[]{:S(2)}) async-start(s32[64,1,4]{2,1,0:T(1,128)} %turn.1), calls=%async_computation | async-start | bytes 65536 | tf_op jit(solution)/shard_map/all_to_all | solution.py:298
  13.5 1.0 copy-start.4
  25.0 5.8 %copy-start.2 = (bf16[8,8,64,128]{3,2,1,0:T(8,128)(2,1)S(1)}, bf16[8,8,64,128]{3,2,1,0:T(8,128)(2,1)}, u32[]{:S(2)}) copy-start(bf16[8,8,64,128]{3,2,1,0:T(8,128)(2,1)} %v_hbm.1) | copy-start | bytes 3145732
  25.0 5.8 %copy-start.6 = (s32[1,1,4,1536]{3,2,1,0:T(4,128)S(1)}, s32[1,1,4,1536]{3,2,1,0:T(4,128)}, u32[]{:S(2)}) copy-start(s32[1,1,4,1536]{3,2,1,0:T(4,128)} %param.8) | copy-start | bytes 73732
  25.0 33.9 %all-to-all-start.1 = ((bf16[64,32,4,128]{3,2,1,0:T(4,128)(2,1)}), bf16[64,32,4,128]{3,2,1,0:T(4,128)(2,1)S(1)}, u32[]{:S(2)}, u32[]{:S(2)}) async-start(bf16[64,32,4,128]{3,2,1,0:T(4,128)(2,1)} %get-tuple-element.12), calls=%async_computation.1 | async-start | bytes 4194304 | tf_op jit(solution)/shard_map/all_to_all | solution.py:298
  33.4 2.0 %copy-start = (bf16[8,8,256,128]{3,2,1,0:T(8,128)(2,1)}, bf16[8,8,256,128]{3,2,1,0:T(8,128)(2,1)S(1)}, u32[]{:S(2)}) copy-start(bf16[8,8,256,128]{3,2,1,0:T(8,128)(2,1)S(1)} %get-tuple-element.17.vt_hbm) | copy-start | bytes 12582916
  35.4 1.0 copy-start.1
  36.4 0.8 copy-start.3
  37.2 0.8 copy-start.5
  68.1 5.8 %copy-start.7 = (f32[8,128]{1,0:T(8,128)}, f32[8,128]{1,0:T(8,128)S(1)}, u32[]{:S(2)}) copy-start(f32[8,128]{1,0:T(8,128)S(1)} %psum.7.d_ref) | copy-start | bytes 12292

commit v5 on v4

--- a/solution.py
+++ b/solution.py
@@ -79,11 +79,9 @@
         for h in range(2):
             part = vals[h * half : (h + 1) * half].reshape(half * kloc, npt)
             v2_ref[b, :, h * npt : (h + 1) * npt] = part.astype(BF16)
-        zero = jnp.zeros((npt, bs), F32)
         for l in range(kloc):
             vt = jnp.transpose(v_ref[b, l].astype(F32))
-            vt_ref[b, l, :npt] = jnp.concatenate([vt, zero], axis=1).astype(BF16)
-            vt_ref[b, l, npt:] = jnp.concatenate([zero, vt], axis=1).astype(BF16)
+            vt_ref[b, l] = jnp.concatenate([vt, vt], axis=1).astype(BF16)
 
 
 def request_hot(req_ref, nblk):
@@ -144,12 +142,13 @@
     nbat, kloc, _, npt = v_ref.shape
     rows = r_ref.shape[1]
     keys = c_ref.shape[1]
-    get_c = pltpu.make_async_copy(c_hbm, c_ref, sem.at[0])
-    get_v = pltpu.make_async_copy(v_hbm, v_ref, sem.at[1])
-    get_v2 = pltpu.make_async_copy(v2_hbm, v2_ref, sem.at[2])
-    get_c.start()
+    get_c = [pltpu.make_async_copy(c_hbm.at[n], c_ref.at[n], sem.at[n]) for n in range(2)]
+    get_v = pltpu.make_async_copy(v_hbm, v_ref, sem.at[2])
+    get_v2 = pltpu.make_async_copy(v2_hbm, v2_ref, sem.at[3])
+    get_c[0].start()
     get_v.start()
     get_v2.start()
+    get_c[1].start()
 
     def build(jp, parts):
         rhs = slot_rows(r_ref, jp)
@@ -162,7 +161,7 @@
         hi_s[:, at, :] = hi
         lo_s[:, at, :] = lo
 
-    get_c.wait()
+    get_c[0].wait()
 
     def loop(parts, group):
         def step(i, carry):
@@ -174,7 +173,9 @@
 
     @pl.when(flag_ref[0, 0] == 0)
     def _():
-        loop(1, GROUP)
+        loop(1, 8)
+
+    get_c[1].wait()
 
     @pl.when(flag_ref[0, 0] != 0)
     def _():
@@ -201,9 +202,23 @@
 
 
 def potential_kernel(
-    flag_ref, d_ref, ct_hbm, vt_hbm, v2_hbm, o_ref, ct_ref, vt_ref, v2_ref, g_s, pot_s, sem
+    flag_ref,
+    mine_ref,
+    other_ref,
+    ct_hbm,
+    vt_hbm,
+    v2_hbm,
+    o_ref,
+    d_ref,
+    ct_ref,
+    vt_ref,
+    v2_ref,
+    g_s,
+    pot_s,
+    sem,
 ):
-    nbat, kloc, _, _ = vt_ref.shape
+    nbat, kloc, npt, _ = vt_ref.shape
+    low = lax.broadcasted_iota(jnp.int32, (npt, LANES), 1) < LANES // 2
     slabs, rows, cap, _ = o_ref.shape
 
     def get_batch(b):
@@ -217,14 +232,19 @@
         for copy in get_batch(b):
             copy.start()
     get_ct.start()
-    d = d_ref[...]
+    d = mine_ref[...] + other_ref[...]
+    d_ref[...] = d
     pot = d / jnp.sqrt(1.0 + d * d)
     pot_s[...] = jnp.concatenate([pot, pot], axis=1)
 
     def one_batch(b):
         weighted = (v2_ref[b].astype(F32) * pot_s[pl.ds(b, 1), :]).astype(BF16)
         for lp in range(kloc // 2):
-            rhs = jnp.concatenate([vt_ref[b, 2 * lp], vt_ref[b, 2 * lp + 1]], axis=1)
+            pair = [vt_ref[b, 2 * lp], vt_ref[b, 2 * lp + 1]]
+            zero = jnp.zeros_like(pair[0])
+            top = jnp.concatenate([jnp.where(low, x, zero) for x in pair], axis=1)
+            bottom = jnp.concatenate([jnp.where(low, zero, x) for x in pair], axis=1)
+            rhs = jnp.concatenate([top, bottom], axis=0)
             g = dot_nn(weighted, rhs).reshape(rows, SUB, 2 * LANES)
             g = jnp.concatenate([g[:, :, :LANES], g[:, :, LANES:]], axis=1)
             row = pl.multiple_of((b * kloc + 2 * lp) * SUB, 2 * SUB)
@@ -346,7 +366,7 @@
             jax.ShapeDtypeStruct((2, keys, slots), BF16),
             jax.ShapeDtypeStruct((2, slots, keys), BF16),
             jax.ShapeDtypeStruct((nbat, half * kloc, 2 * npt), BF16),
-            jax.ShapeDtypeStruct((nbat, kloc, 2 * npt, LANES), BF16),
+            jax.ShapeDtypeStruct((nbat, kloc, npt, LANES), BF16),
             jax.ShapeDtypeStruct((blk_dev, slots), BF16),
             jax.ShapeDtypeStruct((1, 1), jnp.int32),
         ),
@@ -367,17 +387,18 @@
             pltpu.VMEM(v2.shape, BF16),
         ]
         + [pltpu.VMEM((nbat * kloc, half * SUB, LANES), BF16)] * 2
-        + [pltpu.SemaphoreType.DMA((3,))],
+        + [pltpu.SemaphoreType.DMA((4,))],
     )(flag, received, in_hbm(counts), in_hbm(basis_vals), in_hbm(v2))
-    density = lax.psum(partial, "blk")
-
-    slot_sums = kernel_call(
+    swap = [(0, 1), (1, 0)]
+    other = lax.ppermute(partial, "blk", swap)
+
+    slot_sums, density = kernel_call(
         potential_kernel,
         "potential",
         24,
-        out_shape=wide,
-        in_specs=[SMEM, VMEM, HBM, HBM, HBM],
-        out_specs=VMEM,
+        out_shape=(wide, jax.ShapeDtypeStruct((nbat, npt), F32)),
+        in_specs=[SMEM, VMEM, VMEM, HBM, HBM, HBM],
+        out_specs=(VMEM, VMEM),
         scratch_shapes=[
             pltpu.VMEM(counts_t.shape, BF16),
             pltpu.VMEM(vt.shape, BF16),
@@ -386,7 +407,7 @@
             pltpu.VMEM((nbat, 2 * npt), F32),
             pltpu.SemaphoreType.DMA((3, nbat)),
         ],
-    )(flag, density, in_hbm(counts_t), in_hbm(vt), in_hbm(v2))
+    )(flag, partial, other, in_hbm(counts_t), in_hbm(vt), in_hbm(v2))
     returned = exchange(slot_sums)
 
     owner_sums = kernel_call(

time: 111 us -> 110 us (level)
  blocking collectives: 37.9 us -> 35.5 us
  waiting for transfers between devices: 29.2 us -> 31.2 us
    psum x1 -> x0, blocking collectives: 2.47 us -> none  [body(): density = lax.psum(partial, 'blk')]
    ppermute x0 -> x1, waiting for transfers between devices: none -> 1.15 us  [body(): other = lax.ppermute(partial, 'blk', swap)]
    unnamed x18 -> x16, local copies, waits for them, and re-layouts: 6.23 us -> 5.62 us
  transfers between devices with their start and end apart: 2 -> 3, of which waited for: 2 -> 3; matrix products, arithmetic and copies ran while one was open for 0% -> 0% of each run, Pallas kernels for 3% -> 2%
where the time goes in v5:
time: 110 us; the launch traced here: 109 us
  blocking collectives  35.5 us (32%)
  waiting for transfers between devices  31.2 us (28%)
  Pallas kernels  19.1 us (17%)
  starting transfers between devices  16.7 us (15%)
  local copies, waits for them, and re-layouts  5.62 us (5%)
  between operations  1.4 us (1%)
    all_to_all x1, blocking collectives, exchange(): return lax.all_to_all(x, 'slab', split_axis=0, concat_axis=0, tiled=True)  35.5 us
    all_to_all x2, waiting for transfers between devices, exchange(): return lax.all_to_all(x, 'slab', split_axis=0, concat_axis=0, tiled=True)  30 us
    all_to_all x2, starting transfers between devices, exchange(): return lax.all_to_all(x, 'slab', split_axis=0, concat_axis=0, tiled=True)  16.6 us
    pallas_call x1, Pallas kernels, body(): kernel_call(density_kernel, 'density', 16, out_shape=jax.ShapeDtypeStruct...  6.19 us
    pallas_call x1, Pallas kernels, body(): kernel_call(potential_kernel, 'potential', 24, out_shape=(wide, jax.Shape...  5.92 us
    unnamed x16, local copies, waits for them, and re-layouts  5.62 us
    pallas_call x1, Pallas kernels, body(): kernel_call(prep_kernel, 'prep', 24, out_shape=(jax.ShapeDtypeStruct((2,...  2.38 us
  transfers between devices with their start and end apart: 3, of which 3 were waited for; matrix products, arithmetic and copies ran while one was open for 0% of the time, Pallas kernels for 2%

profile of v5, /device:TPU:0, one launch (start us, length us, event | category | flops | bytes accessed | tf_op | source)
XLA Modules:
  0.0 109.5 jit_solution(4379138567277628652)
XLA Ops:
  0.6 0.7 copy-done.7
  1.3 0.7 turn.1
  2.0 11.5 %all-to-all-start = ((s32[64,1,4]{2,1,0:T(1,128)}), s32[64,1,4]{2,1,0:T(1,128)S(1)}, u32[]{:S(2)}, u32[]{:S(2)}) async-start(s32[64,1,4]{2,1,0:T(1,128)} %turn.1), calls=%async_computation | async-start | bytes 65536 | tf_op jit(solution)/shard_map/all_to_all | solution.py:318
  13.5 0.0 copy-start.3
  13.6 1.0 copy-done.3
  14.6 0.2 own.1.own_ref
  14.8 8.2 %all-to-all-done.req_ref = s32[64,1,4]{2,1,0:T(1,128)S(1)} async-done(((s32[64,1,4]{2,1,0:T(1,128)}), s32[64,1,4]{2,1,0:T(1,128)S(1)}, u32[]{:S(2)}, u32[]{:S(2)}) %all-to-all-start) | async-done | bytes 1056 | tf_op jit(solution)/shard_map/all_to_all | solution.py:318
  23.1 2.0 %send.1 = (bf16[64,32,4,128]{3,2,1,0:T(4,128)(2,1)}, bf16[256,32]{1,0:T(8,128)(2,1)S(1)}) custom-call(s32[64,1,4]{2,1,0:T(1,128)S(1)} %all-to-all-done.req_ref, bf16[16,32,256]{2,1,0:T(8,128)(2,1)S(1)} %own.1.own_ref), custom_call_target="tpu_custom_call" | custom-call | tf_op jit(solution)/shard_map/send/pallas_call | solution.py:350
  25.0 0.0 copy-start
  25.0 0.0 copy-start.6
  25.0 5.1 %all-to-all-start.1 = ((bf16[64,32,4,128]{3,2,1,0:T(4,128)(2,1)}), bf16[64,32,4,128]{3,2,1,0:T(4,128)(2,1)S(1)}, u32[]{:S(2)}, u32[]{:S(2)}) async-start(bf16[64,32,4,128]{3,2,1,0:T(4,128)(2,1)} %get-tuple-element.14), calls=%async_computation.1 | async-start | bytes 4194304 | tf_op jit(solution)/shard_map/all_to_all | solution.py:318
  30.8 2.4 %prep.1 = (bf16[2,512,256]{2,1,0:T(8,128)(2,1)S(1)}, bf16[2,256,512]{2,1,0:T(8,128)(2,1)S(1)}, bf16[8,256,256]{2,1,0:T(8,128)(2,1)S(1)}, bf16[8,8,128,128]{3,2,1...) custom-call(s32[1,1]{1,0:T(1,128)S(6)} %copy.7.count_ref, s32[4,1536]{1,0:T(4,128)S(1)} %bitcast.7, ...), custom_call_target="tpu_custom_call" | custom-call | tf_op jit(solution)/shard_map/prep/pallas_call | solution.py:361
  33.2 0.0 copy-start.1
  33.2 1.0 copy-done.1
  34.2 1.3 %copy-done.2 = bf16[8,8,128,128]{3,2,1,0:T(8,128)(2,1)} copy-done((bf16[8,8,128,128]{3,2,1,0:T(8,128)(2,1)}, bf16[8,8,128,128]{3,2,1,0:T(8,128)(2,1)S(1)}, u32[]{:S(2)}) %copy-start.2) | copy-done | bytes 2097176
  35.5 0.8 copy-done.4
  36.3 0.8 copy-done.5
  37.1 21.8 %all-to-all-done.1.r_ref = bf16[64,32,4,128]{3,2,1,0:T(4,128)(2,1)S(1)} async-done(((bf16[64,32,4,128]{3,2,1,0:T(4,128)(2,1)}), bf16[64,32,4,128]{3,2,1,0:T(4,128)(2,1)S(1)}, u32[]{:S(2)}, u32[]{:S(2)}) %all-to-all-start.1) | async-done | bytes 2097184 | tf_op jit(solution)/shard_map/all_to_all | solution.py:318
  58.9 6.2 %density.1.mine_ref = f32[8,128]{1,0:T(8,128)S(1)} custom-call(s32[1,1]{1,0:T(1,128)} %get-tuple-element.13.flag_ref, bf16[64,32,4,128]{3,2,1,0:T(4,128)(2,1)S(1)} %all-to-all-done.1.r_ref, bf16[2,512,256]{2,1,0:T(8,128)(2,1)} %copy-done.5, bf16[8,8,64,128]{3,2,1,0:T(8,128)(2,1)} %v_hbm.1, bf16[8,256,256]{2,1,0:T(8,128)(2,1)} %copy-done.1), custom_call_target="tpu_custom_call" | custom-call | tf_op jit(solution)/shard_map/density/pallas_call | solution.py:377
  65.1 0.1 collective-permute-start
  65.2 1.2 %collective-permute-done.other_ref = f32[8,128]{1,0:T(8,128)S(1)} collective-permute-done((f32[8,128]{1,0:T(8,128)S(1)}, f32[8,128]{1,0:T(8,128)S(1)}, u32[]{:S(2)}, u32[]{:S(2)}) %collective-permute-start) | collective-permute-done | bytes 4128 | tf_op jit(solution)/shard_map/ppermute | solution.py:393
  66.4 5.9 %potential.1 = (bf16[64,32,4,128]{3,2,1,0:T(4,128)(2,1)S(1)}, f32[8,128]{1,0:T(8,128)}) custom-call(s32[1,1]{1,0:T(1,128)} %get-tuple-element.13.flag_ref, f32[8,128]{1,0:T(8,128)S(1)} %density.1.mine_ref, f32[8,128]{1,0:T(8,128)S(1)} %collective-permute-done.other_ref, bf16[2,256,512]{2,1,0:T(8,128)(2,1)} %copy-done.4, bf16[8,8,128,128]{3,2,1,0:T(8,128)(2,1)} %copy-done.2, ...), custom_call_target="tpu_custom_call" | custom-call | tf_op jit(solution)/shard_map/potential/pallas_call | solution.py:395
  72.3 35.5 %all_to_all.15.ret_ref = bf16[64,32,4,128]{3,2,1,0:T(4,128)(2,1)S(1)} all-to-all(bf16[64,32,4,128]{3,2,1,0:T(4,128)(2,1)S(1)} %get-tuple-element.21), channel_id=1, replica_groups=mesh['slab'=64,'blk'=2] {'slab'}, dimensions={0} | all-to-all | bytes 4194304 | tf_op jit(solution)/shard_map/all_to_all | solution.py:318
  107.8 1.7 %owner.1 = f32[32,64,64]{2,1,0:T(8,128)} custom-call(bf16[32,256]{1,0:T(8,128)(2,1)S(1)} %get-tuple-element.20.hot_ref, bf16[64,32,4,128]{3,2,1,0:T(4,128)(2,1)S(1)} %all_to_all.15.ret_ref), custom_call_target="tpu_custom_call" | custom-call | tf_op jit(solution)/shard_map/owner/pallas_call | solution.py:413
  (6 shorter events, 0.0 us)
Async XLA Ops:
  0.6 0.7 copy-start.7
  2.0 21.0 %all-to-all-start = ((s32[64,1,4]{2,1,0:T(1,128)}), s32[64,1,4]{2,1,0:T(1,128)S(1)}, u32[]{:S(2)}, u32[]{:S(2)}) async-start(s32[64,1,4]{2,1,0:T(1,128)} %turn.1), calls=%async_computation | async-start | bytes 65536 | tf_op jit(solution)/shard_map/all_to_all | solution.py:318
  13.5 1.0 copy-start.3
  25.0 5.8 %copy-start = (bf16[8,8,64,128]{3,2,1,0:T(8,128)(2,1)S(1)}, bf16[8,8,64,128]{3,2,1,0:T(8,128)(2,1)}, u32[]{:S(2)}) copy-start(bf16[8,8,64,128]{3,2,1,0:T(8,128)(2,1)} %v_hbm.1) | copy-start | bytes 3145732
  25.0 5.8 %copy-start.6 = (s32[1,1,4,1536]{3,2,1,0:T(4,128)S(1)}, s32[1,1,4,1536]{3,2,1,0:T(4,128)}, u32[]{:S(2)}) copy-start(s32[1,1,4,1536]{3,2,1,0:T(4,128)} %param.8) | copy-start | bytes 73732
  25.0 33.9 %all-to-all-start.1 = ((bf16[64,32,4,128]{3,2,1,0:T(4,128)(2,1)}), bf16[64,32,4,128]{3,2,1,0:T(4,128)(2,1)S(1)}, u32[]{:S(2)}, u32[]{:S(2)}) async-start(bf16[64,32,4,128]{3,2,1,0:T(4,128)(2,1)} %get-tuple-element.14), calls=%async_computation.1 | async-start | bytes 4194304 | tf_op jit(solution)/shard_map/all_to_all | solution.py:318
  33.2 1.0 copy-start.1
  34.2 1.3 %copy-start.2 = (bf16[8,8,128,128]{3,2,1,0:T(8,128)(2,1)}, bf16[8,8,128,128]{3,2,1,0:T(8,128)(2,1)S(1)}, u32[]{:S(2)}) copy-start(bf16[8,8,128,128]{3,2,1,0:T(8,128)(2,1)S(1)} %get-tuple-element.18.vt_hbm) | copy-start | bytes 6291460
  35.5 0.8 copy-start.4
  36.3 0.8 copy-start.5
  65.1 1.2 %collective-permute-start = (f32[8,128]{1,0:T(8,128)S(1)}, f32[8,128]{1,0:T(8,128)S(1)}, u32[]{:S(2)}, u32[]{:S(2)}) collective-permute-start(f32[8,128]{1,0:T(8,128)S(1)} %density.1.mine_ref), channel_id=1, source_target_pairs={{0,1},{1,0},{2,3},{3,2},{4,5},{5,4},{6,7},{7,6},{8,9},{9,8},{10,11... | collective-permute-start | bytes 12296 | tf_op jit(solution)/shard_map/ppermute | solution.py:393

commit v6 on v5

--- a/solution.py
+++ b/solution.py
@@ -205,33 +205,18 @@
     flag_ref,
     mine_ref,
     other_ref,
-    ct_hbm,
-    vt_hbm,
-    v2_hbm,
-    o_ref,
-    d_ref,
     ct_ref,
     vt_ref,
     v2_ref,
+    o_ref,
+    d_ref,
     g_s,
     pot_s,
-    sem,
 ):
     nbat, kloc, npt, _ = vt_ref.shape
     low = lax.broadcasted_iota(jnp.int32, (npt, LANES), 1) < LANES // 2
     slabs, rows, cap, _ = o_ref.shape
 
-    def get_batch(b):
-        return (
-            pltpu.make_async_copy(vt_hbm.at[b], vt_ref.at[b], sem.at[0, b]),
-            pltpu.make_async_copy(v2_hbm.at[b], v2_ref.at[b], sem.at[1, b]),
-        )
-
-    get_ct = pltpu.make_async_copy(ct_hbm, ct_ref, sem.at[2, 0])
-    for b in range(nbat):
-        for copy in get_batch(b):
-            copy.start()
-    get_ct.start()
     d = mine_ref[...] + other_ref[...]
     d_ref[...] = d
     pot = d / jnp.sqrt(1.0 + d * d)
@@ -252,14 +237,10 @@
 
     def some_batches(i, carry):
         for n in range(BATCH_GROUP):
-            for copy in get_batch(i * BATCH_GROUP + n):
-                copy.wait()
-        for n in range(BATCH_GROUP):
             one_batch(i * BATCH_GROUP + n)
         return carry
 
     lax.fori_loop(0, nbat // BATCH_GROUP, some_batches, 0)
-    get_ct.wait()
 
     def sums(jp, parts):
         rhs = jnp.concatenate([g_s[2 * jp], g_s[2 * jp + 1]], axis=1)
@@ -291,13 +272,14 @@
     bs = o_ref.shape[2]
     half = o_ref.shape[1] // 2
     hot = hot_ref[...]
-    parts = []
-    for jp in range(half // 2):
-        res = dot_nn(hot, slot_rows(ret_ref, jp))
-        parts += [res[:, :LANES], res[:, LANES:]]
-    sums = jnp.swapaxes(jnp.stack(parts, axis=0), 0, 1)
-    o_ref[:, :half] = sums[:, :, :bs]
-    o_ref[:, half:] = sums[:, :, bs:]
+    for j in range(0, half, SUB):
+        parts = []
+        for jp in range(j // 2, (j + SUB) // 2):
+            res = dot_nn(hot, slot_rows(ret_ref, jp))
+            parts += [res[:, :LANES], res[:, LANES:]]
+        sums = jnp.swapaxes(jnp.stack(parts, axis=0), 0, 1)
+        o_ref[:, j : j + SUB] = sums[:, :, :bs]
+        o_ref[:, half + j : half + j + SUB] = sums[:, :, bs:]
 
 
 SMEM = pl.BlockSpec(memory_space=pltpu.SMEM)
@@ -397,17 +379,13 @@
         "potential",
         24,
         out_shape=(wide, jax.ShapeDtypeStruct((nbat, npt), F32)),
-        in_specs=[SMEM, VMEM, VMEM, HBM, HBM, HBM],
+        in_specs=[SMEM] + [VMEM] * 5,
         out_specs=(VMEM, VMEM),
         scratch_shapes=[
-            pltpu.VMEM(counts_t.shape, BF16),
-            pltpu.VMEM(vt.shape, BF16),
-            pltpu.VMEM(v2.shape, BF16),
             pltpu.VMEM((half, keys, LANES), BF16),
             pltpu.VMEM((nbat, 2 * npt), F32),
-            pltpu.SemaphoreType.DMA((3, nbat)),
         ],
-    )(flag, partial, other, in_hbm(counts_t), in_hbm(vt), in_hbm(v2))
+    )(flag, partial, other, counts_t, vt, v2)
     returned = exchange(slot_sums)
 
     owner_sums = kernel_call(

time: 110 us -> 109 us (level)
  Pallas kernels: 19.1 us -> 18 us
    pallas_call x1, Pallas kernels: 5.92 us -> 4.38 us  [body(): kernel_call(potential_kernel, 'potential', 24, out_shape=(wide, jax.Shape...]
    unnamed x16 -> x22, local copies, waits for them, and re-layouts: 5.62 us -> 5.63 us
where the time goes in v6:
time: 109 us; the launch traced here: 108 us
  blocking collectives  35.4 us (32%)
  waiting for transfers between devices  31.2 us (29%)
  Pallas kernels  18 us (17%)
  starting transfers between devices  16.7 us (15%)
  local copies, waits for them, and re-layouts  5.63 us (5%)
  between operations  1.4 us (1%)
    all_to_all x1, blocking collectives, exchange(): return lax.all_to_all(x, 'slab', split_axis=0, concat_axis=0, tiled=True)  35.4 us
    all_to_all x2, waiting for transfers between devices, exchange(): return lax.all_to_all(x, 'slab', split_axis=0, concat_axis=0, tiled=True)  30 us
    all_to_all x2, starting transfers between devices, exchange(): return lax.all_to_all(x, 'slab', split_axis=0, concat_axis=0, tiled=True)  16.6 us
    pallas_call x1, Pallas kernels, body(): kernel_call(density_kernel, 'density', 16, out_shape=jax.ShapeDtypeStruct...  6.75 us
    unnamed x22, local copies, waits for them, and re-layouts  5.63 us
    pallas_call x1, Pallas kernels, body(): kernel_call(potential_kernel, 'potential', 24, out_shape=(wide, jax.Shape...  4.38 us
    pallas_call x1, Pallas kernels, body(): kernel_call(prep_kernel, 'prep', 24, out_shape=(jax.ShapeDtypeStruct((2,...  2.38 us
  transfers between devices with their start and end apart: 3, of which 3 were waited for; matrix products, arithmetic and copies ran while one was open for 0% of the time, Pallas kernels for 2%

profile of v6, /device:TPU:0, one launch (start us, length us, event | category | flops | bytes accessed | tf_op | source)
XLA Modules:
  0.0 108.4 jit_solution(13947672566292081948)
XLA Ops:
  0.6 0.7 copy-done.10
  1.3 0.7 turn.1
  2.0 11.5 %all-to-all-start = ((s32[64,1,4]{2,1,0:T(1,128)}), s32[64,1,4]{2,1,0:T(1,128)S(1)}, u32[]{:S(2)}, u32[]{:S(2)}) async-start(s32[64,1,4]{2,1,0:T(1,128)} %turn.1), calls=%async_computation | async-start | bytes 65536 | tf_op jit(solution)/shard_map/all_to_all | solution.py:300
  13.5 0.0 copy-start.5
  13.6 1.0 copy-done.5
  14.6 0.2 own.1.own_ref
  14.8 8.2 %all-to-all-done.req_ref = s32[64,1,4]{2,1,0:T(1,128)S(1)} async-done(((s32[64,1,4]{2,1,0:T(1,128)}), s32[64,1,4]{2,1,0:T(1,128)S(1)}, u32[]{:S(2)}, u32[]{:S(2)}) %all-to-all-start) | async-done | bytes 1056 | tf_op jit(solution)/shard_map/all_to_all | solution.py:300
  23.1 1.9 %send.1 = (bf16[64,32,4,128]{3,2,1,0:T(4,128)(2,1)}, bf16[256,32]{1,0:T(8,128)(2,1)S(1)}) custom-call(s32[64,1,4]{2,1,0:T(1,128)S(1)} %all-to-all-done.req_ref, bf16[16,32,256]{2,1,0:T(8,128)(2,1)S(1)} %own.1.own_ref), custom_call_target="tpu_custom_call" | custom-call | tf_op jit(solution)/shard_map/send/pallas_call | solution.py:332
  25.0 0.0 copy-start
  25.0 0.0 copy-start.9
  25.0 5.1 %all-to-all-start.1 = ((bf16[64,32,4,128]{3,2,1,0:T(4,128)(2,1)}), bf16[64,32,4,128]{3,2,1,0:T(4,128)(2,1)S(1)}, u32[]{:S(2)}, u32[]{:S(2)}) async-start(bf16[64,32,4,128]{3,2,1,0:T(4,128)(2,1)} %get-tuple-element.14), calls=%async_computation.1 | async-start | bytes 4194304 | tf_op jit(solution)/shard_map/all_to_all | solution.py:300
  30.8 2.4 %prep.1 = (bf16[2,512,256]{2,1,0:T(8,128)(2,1)S(1)}, bf16[2,256,512]{2,1,0:T(8,128)(2,1)S(1)}, bf16[8,256,256]{2,1,0:T(8,128)(2,1)S(1)}, bf16[8,8,128,128]{3,2,1...) custom-call(s32[1,1]{1,0:T(1,128)S(6)} %copy.7.count_ref, s32[4,1536]{1,0:T(4,128)S(1)} %bitcast.7, ...), custom_call_target="tpu_custom_call" | custom-call | tf_op jit(solution)/shard_map/prep/pallas_call | solution.py:343
  33.2 0.0 copy-start.1
  33.2 1.0 copy-done.1
  34.2 1.3 %copy-done.3 = bf16[8,8,128,128]{3,2,1,0:T(8,128)(2,1)} copy-done((bf16[8,8,128,128]{3,2,1,0:T(8,128)(2,1)}, bf16[8,8,128,128]{3,2,1,0:T(8,128)(2,1)S(1)}, u32[]{:S(2)}) %copy-start.3) | copy-done | bytes 2097176
  35.5 0.8 copy-done.6
  36.3 0.8 copy-done.8
  37.1 21.8 %all-to-all-done.1.r_ref = bf16[64,32,4,128]{3,2,1,0:T(4,128)(2,1)S(1)} async-done(((bf16[64,32,4,128]{3,2,1,0:T(4,128)(2,1)}), bf16[64,32,4,128]{3,2,1,0:T(4,128)(2,1)S(1)}, u32[]{:S(2)}, u32[]{:S(2)}) %all-to-all-start.1) | async-done | bytes 2097184 | tf_op jit(solution)/shard_map/all_to_all | solution.py:300
  58.9 6.7 %density.1.mine_ref = f32[8,128]{1,0:T(8,128)S(1)} custom-call(s32[1,1]{1,0:T(1,128)} %get-tuple-element.13.flag_ref, bf16[64,32,4,128]{3,2,1,0:T(4,128)(2,1)S(1)} %all-to-all-done.1.r_ref, bf16[2,512,256]{2,1,0:T(8,128)(2,1)} %copy-done.8, bf16[8,8,64,128]{3,2,1,0:T(8,128)(2,1)} %v_hbm.1, bf16[8,256,256]{2,1,0:T(8,128)(2,1)} %copy-done.1), custom_call_target="tpu_custom_call" | custom-call | tf_op jit(solution)/shard_map/density/pallas_call | solution.py:359
  65.7 0.1 collective-permute-start
  65.8 1.2 %collective-permute-done.other_ref = f32[8,128]{1,0:T(8,128)S(1)} collective-permute-done((f32[8,128]{1,0:T(8,128)S(1)}, f32[8,128]{1,0:T(8,128)S(1)}, u32[]{:S(2)}, u32[]{:S(2)}) %collective-permute-start) | collective-permute-done | bytes 4128 | tf_op jit(solution)/shard_map/ppermute | solution.py:375
  66.9 4.4 %potential.1 = (bf16[64,32,4,128]{3,2,1,0:T(4,128)(2,1)S(1)}, f32[8,128]{1,0:T(8,128)}) custom-call(s32[1,1]{1,0:T(1,128)} %get-tuple-element.13.flag_ref, f32[8,128]{1,0:T(8,128)S(1)} %density.1.mine_ref, f32[8,128]{1,0:T(8,128)S(1)} %collective-permute-done.other_ref, bf16[2,256,512]{2,1,0:T(8,128)(2,1)S(1)} %copy-done.7, ...), custom_call_target="tpu_custom_call" | custom-call | tf_op jit(solution)/shard_map/potential/pallas_call | solution.py:377
  71.3 35.4 %all_to_all.15.ret_ref = bf16[64,32,4,128]{3,2,1,0:T(4,128)(2,1)S(1)} all-to-all(bf16[64,32,4,128]{3,2,1,0:T(4,128)(2,1)S(1)} %get-tuple-element.21), channel_id=1, replica_groups=mesh['slab'=64,'blk'=2] {'slab'}, dimensions={0} | all-to-all | bytes 4194304 | tf_op jit(solution)/shard_map/all_to_all | solution.py:300
  106.7 1.7 %owner.1 = f32[32,64,64]{2,1,0:T(8,128)} custom-call(bf16[32,256]{1,0:T(8,128)(2,1)S(1)} %get-tuple-element.20.hot_ref, bf16[64,32,4,128]{3,2,1,0:T(4,128)(2,1)S(1)} %all_to_all.15.ret_ref), custom_call_target="tpu_custom_call" | custom-call | tf_op jit(solution)/shard_map/owner/pallas_call | solution.py:391
  (12 shorter events, 0.0 us)
Async XLA Ops:
  0.6 0.7 copy-start.10
  2.0 21.0 %all-to-all-start = ((s32[64,1,4]{2,1,0:T(1,128)}), s32[64,1,4]{2,1,0:T(1,128)S(1)}, u32[]{:S(2)}, u32[]{:S(2)}) async-start(s32[64,1,4]{2,1,0:T(1,128)} %turn.1), calls=%async_computation | async-start | bytes 65536 | tf_op jit(solution)/shard_map/all_to_all | solution.py:300
  13.5 1.0 copy-start.5
  25.0 5.8 %copy-start = (bf16[8,8,64,128]{3,2,1,0:T(8,128)(2,1)S(1)}, bf16[8,8,64,128]{3,2,1,0:T(8,128)(2,1)}, u32[]{:S(2)}) copy-start(bf16[8,8,64,128]{3,2,1,0:T(8,128)(2,1)} %v_hbm.1) | copy-start | bytes 3145732
  25.0 5.8 %copy-start.9 = (s32[1,1,4,1536]{3,2,1,0:T(4,128)S(1)}, s32[1,1,4,1536]{3,2,1,0:T(4,128)}, u32[]{:S(2)}) copy-start(s32[1,1,4,1536]{3,2,1,0:T(4,128)} %param.8) | copy-start | bytes 73732
  25.0 33.9 %all-to-all-start.1 = ((bf16[64,32,4,128]{3,2,1,0:T(4,128)(2,1)}), bf16[64,32,4,128]{3,2,1,0:T(4,128)(2,1)S(1)}, u32[]{:S(2)}, u32[]{:S(2)}) async-start(bf16[64,32,4,128]{3,2,1,0:T(4,128)(2,1)} %get-tuple-element.14), calls=%async_computation.1 | async-start | bytes 4194304 | tf_op jit(solution)/shard_map/all_to_all | solution.py:300
  33.2 1.0 copy-start.1
  34.2 1.3 %copy-start.3 = (bf16[8,8,128,128]{3,2,1,0:T(8,128)(2,1)}, bf16[8,8,128,128]{3,2,1,0:T(8,128)(2,1)S(1)}, u32[]{:S(2)}) copy-start(bf16[8,8,128,128]{3,2,1,0:T(8,128)(2,1)S(1)} %get-tuple-element.18.vt_ref) | copy-start | bytes 6291460
  35.5 0.8 copy-start.6
  36.3 0.8 copy-start.8
  58.9 8.0 %copy-start.2 = (bf16[8,256,256]{2,1,0:T(8,128)(2,1)S(1)}, bf16[8,256,256]{2,1,0:T(8,128)(2,1)}, u32[]{:S(2)}) copy-start(bf16[8,256,256]{2,1,0:T(8,128)(2,1)} %copy-done.1) | copy-start | bytes 3145732
  58.9 8.0 %copy-start.4 = (bf16[8,8,128,128]{3,2,1,0:T(8,128)(2,1)S(1)}, bf16[8,8,128,128]{3,2,1,0:T(8,128)(2,1)}, u32[]{:S(2)}) copy-start(bf16[8,8,128,128]{3,2,1,0:T(8,128)(2,1)} %copy-done.3) | copy-start | bytes 6291460
  58.9 8.0 %copy-start.7 = (bf16[2,256,512]{2,1,0:T(8,128)(2,1)S(1)}, bf16[2,256,512]{2,1,0:T(8,128)(2,1)}, u32[]{:S(2)}) copy-start(bf16[2,256,512]{2,1,0:T(8,128)(2,1)} %copy-done.6) | copy-start | bytes 1572868
  65.7 1.2 %collective-permute-start = (f32[8,128]{1,0:T(8,128)S(1)}, f32[8,128]{1,0:T(8,128)S(1)}, u32[]{:S(2)}, u32[]{:S(2)}) collective-permute-start(f32[8,128]{1,0:T(8,128)S(1)} %density.1.mine_ref), channel_id=1, source_target_pairs={{0,1},{1,0},{2,3},{3,2},{4,5},{5,4},{6,7},{7,6},{8,9},{9,8},{10,11... | collective-permute-start | bytes 12296 | tf_op jit(solution)/shard_map/ppermute | solution.py:375

commit v7 on v6

--- a/solution.py
+++ b/solution.py
@@ -5,12 +5,12 @@
 from jax.experimental.pallas import tpu as pltpu
 from jax.sharding import PartitionSpec as P
 
+
 F32 = jnp.float32
 BF16 = jnp.bfloat16
 LANES = 128
 SUB = 8
 TASK_STEP = 512
-GROUP = 4
 BATCH_GROUP = 4
 
 
@@ -42,12 +42,11 @@
 
 
 def prep_kernel(
-    count_ref, tasks_ref, v_ref, hot_ref, c_ref, ct_ref, v2_ref, vt_ref, hot_t_ref, flag_ref
+    count_ref, tasks_ref, v_ref, c_ref, c_hi_ref, ct_ref, ct_hi_ref, v2_ref, vt_ref, flag_ref
 ):
-    hot_t_ref[...] = jnp.transpose(hot_ref[...].astype(F32)).astype(BF16)
     nbat, kloc, bs, npt = v_ref.shape
     keys = nbat * kloc * kloc
-    slots = c_ref.shape[2]
+    slots = c_ref.shape[1]
     tcap = tasks_ref.shape[1]
     step = TASK_STEP if tcap % TASK_STEP == 0 else tcap
     live = count_ref[0, 0]
@@ -68,10 +67,10 @@
         ct += dot_nt(slot_hot, key_hot)
     c_hi = jnp.floor(c * (1.0 / 256.0)) * 256.0
     ct_hi = jnp.floor(ct * (1.0 / 256.0)) * 256.0
-    c_ref[0] = (c - c_hi).astype(BF16)
-    c_ref[1] = c_hi.astype(BF16)
-    ct_ref[0] = (ct - ct_hi).astype(BF16)
-    ct_ref[1] = ct_hi.astype(BF16)
+    c_ref[...] = (c - c_hi).astype(BF16)
+    c_hi_ref[...] = c_hi.astype(BF16)
+    ct_ref[...] = (ct - ct_hi).astype(BF16)
+    ct_hi_ref[...] = ct_hi.astype(BF16)
     flag_ref[0, 0] = jnp.where(jnp.max(c) > 255.5, 1, 0).astype(jnp.int32)
     half = bs // 2
     for b in range(nbat):
@@ -137,32 +136,28 @@
 
 
 def density_kernel(
-    flag_ref, r_ref, c_hbm, v_hbm, v2_hbm, d_ref, c_ref, v_ref, v2_ref, hi_s, lo_s, sem
+    flag_ref, r_ref, c_ref, c_hbm, v_hbm, v2_hbm, d_ref, c_hi_ref, v_ref, v2_ref, hi_s, lo_s, sem
 ):
     nbat, kloc, _, npt = v_ref.shape
     rows = r_ref.shape[1]
-    keys = c_ref.shape[1]
-    get_c = [pltpu.make_async_copy(c_hbm.at[n], c_ref.at[n], sem.at[n]) for n in range(2)]
-    get_v = pltpu.make_async_copy(v_hbm, v_ref, sem.at[2])
-    get_v2 = pltpu.make_async_copy(v2_hbm, v2_ref, sem.at[3])
-    get_c[0].start()
+    keys = c_ref.shape[0]
+    get_c = pltpu.make_async_copy(c_hbm, c_hi_ref, sem.at[0])
+    get_v = pltpu.make_async_copy(v_hbm, v_ref, sem.at[1])
+    get_v2 = pltpu.make_async_copy(v2_hbm, v2_ref, sem.at[2])
     get_v.start()
     get_v2.start()
-    get_c[1].start()
 
     def build(jp, parts):
         rhs = slot_rows(r_ref, jp)
-        res = dot_nn(c_ref[0], rhs)
+        res = dot_nn(c_ref[...], rhs)
         if parts == 2:
-            res += dot_nn(c_ref[1], rhs)
+            res += dot_nn(c_hi_ref[...], rhs)
         res = res.reshape(keys // SUB, SUB, 2 * LANES)
         hi, lo = split_pair(jnp.concatenate([res[:, :, :LANES], res[:, :, LANES:]], axis=1))
         at = pl.ds(pl.multiple_of(jp * 2 * SUB, 2 * SUB), 2 * SUB)
         hi_s[:, at, :] = hi
         lo_s[:, at, :] = lo
 
-    get_c[0].wait()
-
     def loop(parts, group):
         def step(i, carry):
             for n in range(group):
@@ -175,10 +170,10 @@
     def _():
         loop(1, 8)
 
-    get_c[1].wait()
-
     @pl.when(flag_ref[0, 0] != 0)
     def _():
+        get_c.start()
+        get_c.wait()
         loop(2, 1)
 
     get_v.wait()
@@ -206,12 +201,17 @@
     mine_ref,
     other_ref,
     ct_ref,
+    ct_hbm,
     vt_ref,
     v2_ref,
     o_ref,
     d_ref,
     g_s,
     pot_s,
+    ct_hi_ref,
+    buf,
+    sem,
+    out_sem,
 ):
     nbat, kloc, npt, _ = vt_ref.shape
     low = lax.broadcasted_iota(jnp.int32, (npt, LANES), 1) < LANES // 2
@@ -244,17 +244,25 @@
 
     def sums(jp, parts):
         rhs = jnp.concatenate([g_s[2 * jp], g_s[2 * jp + 1]], axis=1)
-        out = dot_nn(ct_ref[0], rhs)
+        out = dot_nn(ct_ref[...], rhs)
         if parts == 2:
-            out += dot_nn(ct_ref[1], rhs)
+            out += dot_nn(ct_hi_ref[...], rhs)
         out = out.astype(BF16)
-        o_ref[:, 2 * jp] = out[:, :LANES].reshape(slabs, cap, LANES)
-        o_ref[:, 2 * jp + 1] = out[:, LANES:].reshape(slabs, cap, LANES)
+        buf[:, 2 * jp] = out[:, :LANES].reshape(slabs, cap, LANES)
+        buf[:, 2 * jp + 1] = out[:, LANES:].reshape(slabs, cap, LANES)
+
+    width = rows // out_sem.shape[0]
+
+    def put(n):
+        part = pl.ds(n * width, width)
+        return pltpu.make_async_copy(buf.at[:, part], o_ref.at[:, part], out_sem.at[n])
 
     def loop(parts, group):
         def step(i, carry):
             for n in range(group):
                 sums(group * i + n, parts)
+                if (n + 1) % (width // 2) == 0:
+                    put((group * i + n) // (width // 2)).start()
             return carry
 
         lax.fori_loop(0, rows // (2 * group), step, 0)
@@ -265,7 +273,17 @@
 
     @pl.when(flag_ref[0, 0] != 0)
     def _():
-        loop(2, 1)
+        get_ct = pltpu.make_async_copy(ct_hbm, ct_hi_ref, sem.at[0])
+        get_ct.start()
+        get_ct.wait()
+        loop(2, width // 2)
+
+    for n in range(out_sem.shape[0]):
+        put(n).wait()
+
+
+def flip_kernel(hot_ref, o_ref):
+    o_ref[...] = jnp.transpose(hot_ref[...].astype(F32)).astype(BF16)
 
 
 def owner_kernel(hot_ref, ret_ref, o_ref):
@@ -287,9 +305,9 @@
 HBM = pl.BlockSpec(memory_space=pltpu.HBM)
 
 
-def kernel_call(kernel, name, mib, **kwargs):
+def kernel_call(kernel, mib, **kwargs):
     params = pltpu.CompilerParams(vmem_limit_bytes=mib << 20)
-    return pl.pallas_call(kernel, compiler_params=params, name=name, **kwargs)
+    return pl.pallas_call(kernel, compiler_params=params, **kwargs)
 
 
 def in_hbm(x):
@@ -312,7 +330,6 @@
 
     wanted = kernel_call(
         turn_kernel,
-        "turn",
         4,
         out_shape=jax.ShapeDtypeStruct((slabs, 1, cap), jnp.int32),
         in_specs=[VMEM],
@@ -322,7 +339,6 @@
 
     own_rows = kernel_call(
         own_kernel,
-        "own",
         8,
         out_shape=jax.ShapeDtypeStruct((half // 2, blk_dev, 2 * LANES), BF16),
         in_specs=[VMEM],
@@ -331,7 +347,6 @@
 
     sent, hot = kernel_call(
         send_kernel,
-        "send",
         8,
         out_shape=(pltpu.HBM(wide.shape, BF16), jax.ShapeDtypeStruct((slots, blk_dev), BF16)),
         in_specs=[VMEM, VMEM],
@@ -340,28 +355,27 @@
     )(requested, own_rows)
     received = exchange(sent)
 
-    counts, counts_t, v2, vt, hot_t, flag = kernel_call(
+    counts, counts_hi, counts_t, counts_t_hi, v2, vt, flag = kernel_call(
         prep_kernel,
-        "prep",
         24,
         out_shape=(
-            jax.ShapeDtypeStruct((2, keys, slots), BF16),
-            jax.ShapeDtypeStruct((2, slots, keys), BF16),
+            jax.ShapeDtypeStruct((keys, slots), BF16),
+            jax.ShapeDtypeStruct((keys, slots), BF16),
+            jax.ShapeDtypeStruct((slots, keys), BF16),
+            jax.ShapeDtypeStruct((slots, keys), BF16),
             jax.ShapeDtypeStruct((nbat, half * kloc, 2 * npt), BF16),
             jax.ShapeDtypeStruct((nbat, kloc, npt, LANES), BF16),
-            jax.ShapeDtypeStruct((blk_dev, slots), BF16),
             jax.ShapeDtypeStruct((1, 1), jnp.int32),
         ),
-        in_specs=[SMEM, VMEM, VMEM, VMEM],
-        out_specs=(VMEM, VMEM, VMEM, VMEM, VMEM, SMEM),
-    )(task_counts, tasks[0, 0], basis_vals, hot)
+        in_specs=[SMEM, VMEM, VMEM],
+        out_specs=(VMEM,) * 6 + (SMEM,),
+    )(task_counts, tasks[0, 0], basis_vals)
 
     partial = kernel_call(
         density_kernel,
-        "density",
         16,
         out_shape=jax.ShapeDtypeStruct((nbat, npt), F32),
-        in_specs=[SMEM, VMEM, HBM, HBM, HBM],
+        in_specs=[SMEM, VMEM, VMEM, HBM, HBM, HBM],
         out_specs=VMEM,
         scratch_shapes=[
             pltpu.VMEM(counts.shape, BF16),
@@ -369,28 +383,37 @@
             pltpu.VMEM(v2.shape, BF16),
         ]
         + [pltpu.VMEM((nbat * kloc, half * SUB, LANES), BF16)] * 2
-        + [pltpu.SemaphoreType.DMA((4,))],
-    )(flag, received, in_hbm(counts), in_hbm(basis_vals), in_hbm(v2))
+        + [pltpu.SemaphoreType.DMA((3,))],
+    )(flag, received, counts, in_hbm(counts_hi), in_hbm(basis_vals), in_hbm(v2))
     swap = [(0, 1), (1, 0)]
     other = lax.ppermute(partial, "blk", swap)
 
     slot_sums, density = kernel_call(
         potential_kernel,
-        "potential",
         24,
-        out_shape=(wide, jax.ShapeDtypeStruct((nbat, npt), F32)),
-        in_specs=[SMEM] + [VMEM] * 5,
-        out_specs=(VMEM, VMEM),
+        out_shape=(pltpu.HBM(wide.shape, BF16), jax.ShapeDtypeStruct((nbat, npt), F32)),
+        in_specs=[SMEM, VMEM, VMEM, VMEM, HBM, VMEM, VMEM],
+        out_specs=(HBM, VMEM),
         scratch_shapes=[
             pltpu.VMEM((half, keys, LANES), BF16),
             pltpu.VMEM((nbat, 2 * npt), F32),
+            pltpu.VMEM(counts_t.shape, BF16),
+            pltpu.VMEM(wide.shape, BF16),
+            pltpu.SemaphoreType.DMA((1,)),
+            pltpu.SemaphoreType.DMA((4,)),
         ],
-    )(flag, partial, other, counts_t, vt, v2)
+    )(flag, partial, other, counts_t, in_hbm(counts_t_hi), vt, v2)
     returned = exchange(slot_sums)
+    hot_t = kernel_call(
+        flip_kernel,
+        4,
+        out_shape=jax.ShapeDtypeStruct((blk_dev, slots), BF16),
+        in_specs=[VMEM],
+        out_specs=VMEM,
+    )(hot)
 
     owner_sums = kernel_call(
         owner_kernel,
-        "owner",
         8,
         out_shape=jax.ShapeDtypeStruct((blk_dev, bs, bs), F32),
         in_specs=[VMEM, VMEM],

time: 109 us -> 109 us (level)
  blocking collectives: 35.4 us -> 0 us
  waiting for transfers between devices: 31.2 us -> 62 us
  starting transfers between devices: 16.7 us -> 21.4 us
    all_to_all x1 -> x0, blocking collectives: 35.4 us -> none  [exchange(): return lax.all_to_all(x, 'slab', split_axis=0, concat_axis=0, tiled=True)]
    all_to_all x2 -> x3, waiting for transfers between devices: 30 us -> 60.8 us  [exchange(): return lax.all_to_all(x, 'slab', split_axis=0, concat_axis=0, tiled=True)]
    all_to_all x2 -> x3, starting transfers between devices: 16.6 us -> 21.3 us  [exchange(): return lax.all_to_all(x, 'slab', split_axis=0, concat_axis=0, tiled=True)]
    unnamed x22 -> x24, local copies, waits for them, and re-layouts: 5.63 us -> 6.15 us
    pallas_call x7 -> x8, Pallas kernels: 18 us -> 17.6 us  [the longest x1 5.37 us: body(): kernel_call(density_kernel, 16, out_shape=jax.ShapeDtypeStruct((nbat, npt...]
  transfers between devices with their start and end apart: 3 -> 4, of which waited for: 3 -> 4; matrix products, arithmetic and copies ran while one was open for 0% -> 0% of each run, Pallas kernels for 2% -> 2%
where the time goes in v7:
time: 109 us
  waiting for transfers between devices  62 us (57%)
  starting transfers between devices  21.4 us (20%)
  Pallas kernels  17.6 us (16%)
  local copies, waits for them, and re-layouts  6.15 us (6%)
  between operations  1.42 us (1%)
    all_to_all x3, waiting for transfers between devices, exchange(): return lax.all_to_all(x, 'slab', split_axis=0, concat_axis=0, tiled=True)  60.8 us
    all_to_all x3, starting transfers between devices, exchange(): return lax.all_to_all(x, 'slab', split_axis=0, concat_axis=0, tiled=True)  21.3 us
    unnamed x24, local copies, waits for them, and re-layouts  6.15 us
    pallas_call x1, Pallas kernels, body(): kernel_call(density_kernel, 16, out_shape=jax.ShapeDtypeStruct((nbat, npt...  5.37 us
    pallas_call x1, Pallas kernels, body(): kernel_call(potential_kernel, 24, out_shape=(pltpu.HBM(wide.shape, BF16),...  5.22 us
    pallas_call x1, Pallas kernels, body(): kernel_call(prep_kernel, 24, out_shape=(jax.ShapeDtypeStruct((keys, slots...  2.4 us
  transfers between devices with their start and end apart: 4, of which 4 were waited for; matrix products, arithmetic and copies ran while one was open for 0% of the time, Pallas kernels for 2%

profile of v7, /device:TPU:0, one launch (start us, length us, event | category | flops | bytes accessed | tf_op | source)
XLA Modules:
  0.0 108.6 jit_solution(15400448288427990302)
XLA Ops:
  0.6 0.7 copy-done.11
  1.3 0.7 shard_map.69
  2.0 11.5 %all-to-all-start = ((s32[64,1,4]{2,1,0:T(1,128)}), s32[64,1,4]{2,1,0:T(1,128)S(1)}, u32[]{:S(2)}, u32[]{:S(2)}) async-start(s32[64,1,4]{2,1,0:T(1,128)} %shard_map.69), calls=%async_computation | async-start | bytes 65536 | tf_op jit(solution)/shard_map/all_to_all | solution.py:318
  13.5 0.0 copy-start.5
  13.6 1.0 copy-done.5
  14.6 0.2 shard_map.70.own_ref
  14.8 8.2 %all-to-all-done.req_ref = s32[64,1,4]{2,1,0:T(1,128)S(1)} async-done(((s32[64,1,4]{2,1,0:T(1,128)}), s32[64,1,4]{2,1,0:T(1,128)S(1)}, u32[]{:S(2)}, u32[]{:S(2)}) %all-to-all-start) | async-done | bytes 1056 | tf_op jit(solution)/shard_map/all_to_all | solution.py:318
  23.1 1.9 %shard_map.71 = (bf16[64,32,4,128]{3,2,1,0:T(4,128)(2,1)}, bf16[256,32]{1,0:T(8,128)(2,1)S(1)}) custom-call(s32[64,1,4]{2,1,0:T(1,128)S(1)} %all-to-all-done.req_ref, bf16[16,32,256]{2,1,0:T(8,128)(2,1)S(1)} %shard_map.70.own_ref), custom_call_target="tpu_custom_call" | custom-call | tf_op jit(solution)/shard_map/pallas_call | solution.py:348
  25.0 5.1 %all-to-all-start.1 = ((bf16[64,32,4,128]{3,2,1,0:T(4,128)(2,1)}), bf16[64,32,4,128]{3,2,1,0:T(4,128)(2,1)S(1)}, u32[]{:S(2)}, u32[]{:S(2)}) async-start(bf16[64,32,4,128]{3,2,1,0:T(4,128)(2,1)} %get-tuple-element.14), calls=%async_computation.1 | async-start | bytes 4194304 | tf_op jit(solution)/shard_map/all_to_all | solution.py:318
  30.8 2.4 %shard_map.68 = (bf16[512,256]{1,0:T(8,128)(2,1)S(1)}, bf16[512,256]{1,0:T(8,128)(2,1)S(1)}, bf16[256,512]{1,0:T(8,128)(2,1)S(1)}, bf16[256,512]{1,0:T(8,128)(2,...) custom-call(s32[1,1]{1,0:T(1,128)S(6)} %copy.7.count_ref, ...), custom_call_target="tpu_custom_call" | custom-call | tf_op jit(solution)/shard_map/pallas_call | solution.py:358
  33.2 1.0 copy-done.1
  34.2 1.3 %copy-done.3 = bf16[8,8,128,128]{3,2,1,0:T(8,128)(2,1)} copy-done((bf16[8,8,128,128]{3,2,1,0:T(8,128)(2,1)}, bf16[8,8,128,128]{3,2,1,0:T(8,128)(2,1)S(1)}, u32[]{:S(2)}) %copy-start.3) | copy-done | bytes 2097176
  35.5 0.7 copy-done.6
  36.2 0.7 copy-done.7
  36.9 0.7 copy-done.9
  37.6 21.3 %all-to-all-done.1.r_ref = bf16[64,32,4,128]{3,2,1,0:T(4,128)(2,1)S(1)} async-done(((bf16[64,32,4,128]{3,2,1,0:T(4,128)(2,1)}), bf16[64,32,4,128]{3,2,1,0:T(4,128)(2,1)S(1)}, u32[]{:S(2)}, u32[]{:S(2)}) %all-to-all-start.1) | async-done | bytes 2097184 | tf_op jit(solution)/shard_map/all_to_all | solution.py:318
  58.9 5.4 %shard_map.72.mine_ref = f32[8,128]{1,0:T(8,128)S(1)} custom-call(s32[1,1]{1,0:T(1,128)} %get-tuple-element.13.flag_ref, bf16[64,32,4,128]{3,2,1,0:T(4,128)(2,1)S(1)} %all-to-all-done.1.r_ref, bf16[512,256]{1,0:T(8,128)(2,1)S(1)} %get-tuple-element.15.c_ref, bf16[512,256]{1,0:T(8,128)(2,1)} %copy-done.6, bf16[8,8,64,128]{3,2,1,0:T(8,128)(2,1)} %v_hbm.1, ...), custom_call_target="tpu_custom_call" | custom-call | tf_op jit(solution)/shard_map/pallas_call | solution.py:374
  64.3 0.1 collective-permute-start
  64.4 1.2 %collective-permute-done.other_ref = f32[8,128]{1,0:T(8,128)S(1)} collective-permute-done((f32[8,128]{1,0:T(8,128)S(1)}, f32[8,128]{1,0:T(8,128)S(1)}, u32[]{:S(2)}, u32[]{:S(2)}) %collective-permute-start) | collective-permute-done | bytes 4128 | tf_op jit(solution)/shard_map/ppermute | solution.py:389
  65.5 5.2 %shard_map.73 = (bf16[64,32,4,128]{3,2,1,0:T(4,128)(2,1)}, f32[8,128]{1,0:T(8,128)}) custom-call(s32[1,1]{1,0:T(1,128)} %get-tuple-element.13.flag_ref, f32[8,128]{1,0:T(8,128)S(1)} %shard_map.72.mine_ref, f32[8,128]{1,0:T(8,128)S(1)} %collective-permute-done.other_ref, bf16[256,512]{1,0:T(8,128)(2,1)S(1)} %copy-done.8, bf16[256,512]{1,0:T(8,128)(2,1)} %copy-done.9, ...), custom_call_target="tpu_custom_call" | custom-call | tf_op jit(solution)/shard_map/pallas_call | solution.py:391
  70.8 4.7 %all-to-all-start.2 = ((bf16[64,32,4,128]{3,2,1,0:T(4,128)(2,1)}), bf16[64,32,4,128]{3,2,1,0:T(4,128)(2,1)S(1)}, u32[]{:S(2)}, u32[]{:S(2)}) async-start(bf16[64,32,4,128]{3,2,1,0:T(4,128)(2,1)} %get-tuple-element.23), calls=%async_computation.2 | async-start | bytes 4194304 | tf_op jit(solution)/shard_map/all_to_all | solution.py:318
  75.5 0.1 shard_map.74.hot_ref
  75.6 31.3 %all-to-all-done.2.ret_ref = bf16[64,32,4,128]{3,2,1,0:T(4,128)(2,1)S(1)} async-done(((bf16[64,32,4,128]{3,2,1,0:T(4,128)(2,1)}), bf16[64,32,4,128]{3,2,1,0:T(4,128)(2,1)S(1)}, u32[]{:S(2)}, u32[]{:S(2)}) %all-to-all-start.2) | async-done | bytes 2097184 | tf_op jit(solution)/shard_map/all_to_all | solution.py:318
  106.9 1.7 %shard_map.75 = f32[32,64,64]{2,1,0:T(8,128)} custom-call(bf16[32,256]{1,0:T(8,128)(2,1)S(1)} %shard_map.74.hot_ref, bf16[64,32,4,128]{3,2,1,0:T(4,128)(2,1)S(1)} %all-to-all-done.2.ret_ref), custom_call_target="tpu_custom_call" | custom-call | tf_op jit(solution)/shard_map/pallas_call | solution.py:415
  (16 shorter events, 0.0 us)
Async XLA Ops:
  0.6 0.7 copy-start.11
  2.0 21.0 %all-to-all-start = ((s32[64,1,4]{2,1,0:T(1,128)}), s32[64,1,4]{2,1,0:T(1,128)S(1)}, u32[]{:S(2)}, u32[]{:S(2)}) async-start(s32[64,1,4]{2,1,0:T(1,128)} %shard_map.69), calls=%async_computation | async-start | bytes 65536 | tf_op jit(solution)/shard_map/all_to_all | solution.py:318
  13.5 1.0 copy-start.5
  25.0 5.8 %copy-start = (bf16[8,8,64,128]{3,2,1,0:T(8,128)(2,1)S(1)}, bf16[8,8,64,128]{3,2,1,0:T(8,128)(2,1)}, u32[]{:S(2)}) copy-start(bf16[8,8,64,128]{3,2,1,0:T(8,128)(2,1)} %v_hbm.1) | copy-start | bytes 3145732
  25.0 5.8 %copy-start.10 = (s32[1,1,4,1536]{3,2,1,0:T(4,128)S(1)}, s32[1,1,4,1536]{3,2,1,0:T(4,128)}, u32[]{:S(2)}) copy-start(s32[1,1,4,1536]{3,2,1,0:T(4,128)} %param.8) | copy-start | bytes 73732
  25.0 33.9 %all-to-all-start.1 = ((bf16[64,32,4,128]{3,2,1,0:T(4,128)(2,1)}), bf16[64,32,4,128]{3,2,1,0:T(4,128)(2,1)S(1)}, u32[]{:S(2)}, u32[]{:S(2)}) async-start(bf16[64,32,4,128]{3,2,1,0:T(4,128)(2,1)} %get-tuple-element.14), calls=%async_computation.1 | async-start | bytes 4194304 | tf_op jit(solution)/shard_map/all_to_all | solution.py:318
  33.2 1.0 copy-start.1
  34.2 1.3 %copy-start.3 = (bf16[8,8,128,128]{3,2,1,0:T(8,128)(2,1)}, bf16[8,8,128,128]{3,2,1,0:T(8,128)(2,1)S(1)}, u32[]{:S(2)}) copy-start(bf16[8,8,128,128]{3,2,1,0:T(8,128)(2,1)S(1)} %get-tuple-element.20.vt_ref) | copy-start | bytes 6291460
  35.5 0.7 copy-start.6
  36.2 0.7 copy-start.7
  36.9 0.7 copy-start.9
  58.9 6.6 %copy-start.2 = (bf16[8,256,256]{2,1,0:T(8,128)(2,1)S(1)}, bf16[8,256,256]{2,1,0:T(8,128)(2,1)}, u32[]{:S(2)}) copy-start(bf16[8,256,256]{2,1,0:T(8,128)(2,1)} %copy-done.1) | copy-start | bytes 3145732
  58.9 6.6 %copy-start.4 = (bf16[8,8,128,128]{3,2,1,0:T(8,128)(2,1)S(1)}, bf16[8,8,128,128]{3,2,1,0:T(8,128)(2,1)}, u32[]{:S(2)}) copy-start(bf16[8,8,128,128]{3,2,1,0:T(8,128)(2,1)} %copy-done.3) | copy-start | bytes 6291460
  58.9 6.6 %copy-start.8 = (bf16[256,512]{1,0:T(8,128)(2,1)S(1)}, bf16[256,512]{1,0:T(8,128)(2,1)}, u32[]{:S(2)}) copy-start(bf16[256,512]{1,0:T(8,128)(2,1)} %copy-done.7) | copy-start | bytes 786436
  64.3 1.2 %collective-permute-start = (f32[8,128]{1,0:T(8,128)S(1)}, f32[8,128]{1,0:T(8,128)S(1)}, u32[]{:S(2)}, u32[]{:S(2)}) collective-permute-start(f32[8,128]{1,0:T(8,128)S(1)} %shard_map.72.mine_ref), channel_id=1, source_target_pairs={{0,1},{1,0},{2,3},{3,2},{4,5},{5,4},{6,7},{7,6},{8,9},{9,8},{10,11... | collective-permute-start | bytes 12296 | tf_op jit(solution)/shard_map/ppermute | solution.py:389
  70.8 36.1 %all-to-all-start.2 = ((bf16[64,32,4,128]{3,2,1,0:T(4,128)(2,1)}), bf16[64,32,4,128]{3,2,1,0:T(4,128)(2,1)S(1)}, u32[]{:S(2)}, u32[]{:S(2)}) async-start(bf16[64,32,4,128]{3,2,1,0:T(4,128)(2,1)} %get-tuple-element.23), calls=%async_computation.2 | async-start | bytes 4194304 | tf_op jit(solution)/shard_map/all_to_all | solution.py:318

commit v8 on v7

--- a/solution.py
+++ b/solution.py
@@ -5,12 +5,12 @@
 from jax.experimental.pallas import tpu as pltpu
 from jax.sharding import PartitionSpec as P
 
-
 F32 = jnp.float32
 BF16 = jnp.bfloat16
 LANES = 128
 SUB = 8
 TASK_STEP = 512
+GROUP = 4
 BATCH_GROUP = 4
 
 
@@ -42,8 +42,9 @@
 
 
 def prep_kernel(
-    count_ref, tasks_ref, v_ref, c_ref, c_hi_ref, ct_ref, ct_hi_ref, v2_ref, vt_ref, flag_ref
+    count_ref, tasks_ref, v_ref, hot_ref, c_ref, c_hi_ref, ct_ref, ct_hi_ref, v2_ref, vt_ref, hot_t_ref, flag_ref
 ):
+    hot_t_ref[...] = jnp.transpose(hot_ref[...].astype(F32)).astype(BF16)
     nbat, kloc, bs, npt = v_ref.shape
     keys = nbat * kloc * kloc
     slots = c_ref.shape[1]
@@ -209,9 +210,7 @@
     g_s,
     pot_s,
     ct_hi_ref,
-    buf,
     sem,
-    out_sem,
 ):
     nbat, kloc, npt, _ = vt_ref.shape
     low = lax.broadcasted_iota(jnp.int32, (npt, LANES), 1) < LANES // 2
@@ -248,21 +247,13 @@
         if parts == 2:
             out += dot_nn(ct_hi_ref[...], rhs)
         out = out.astype(BF16)
-        buf[:, 2 * jp] = out[:, :LANES].reshape(slabs, cap, LANES)
-        buf[:, 2 * jp + 1] = out[:, LANES:].reshape(slabs, cap, LANES)
-
-    width = rows // out_sem.shape[0]
-
-    def put(n):
-        part = pl.ds(n * width, width)
-        return pltpu.make_async_copy(buf.at[:, part], o_ref.at[:, part], out_sem.at[n])
+        o_ref[:, 2 * jp] = out[:, :LANES].reshape(slabs, cap, LANES)
+        o_ref[:, 2 * jp + 1] = out[:, LANES:].reshape(slabs, cap, LANES)
 
     def loop(parts, group):
         def step(i, carry):
             for n in range(group):
                 sums(group * i + n, parts)
-                if (n + 1) % (width // 2) == 0:
-                    put((group * i + n) // (width // 2)).start()
             return carry
 
         lax.fori_loop(0, rows // (2 * group), step, 0)
@@ -276,14 +267,7 @@
         get_ct = pltpu.make_async_copy(ct_hbm, ct_hi_ref, sem.at[0])
         get_ct.start()
         get_ct.wait()
-        loop(2, width // 2)
-
-    for n in range(out_sem.shape[0]):
-        put(n).wait()
-
-
-def flip_kernel(hot_ref, o_ref):
-    o_ref[...] = jnp.transpose(hot_ref[...].astype(F32)).astype(BF16)
+        loop(2, 1)
 
 
 def owner_kernel(hot_ref, ret_ref, o_ref):
@@ -305,9 +289,9 @@
 HBM = pl.BlockSpec(memory_space=pltpu.HBM)
 
 
-def kernel_call(kernel, mib, **kwargs):
+def kernel_call(kernel, name, mib, **kwargs):
     params = pltpu.CompilerParams(vmem_limit_bytes=mib << 20)
-    return pl.pallas_call(kernel, compiler_params=params, **kwargs)
+    return pl.pallas_call(kernel, compiler_params=params, name=name, **kwargs)
 
 
 def in_hbm(x):
@@ -330,6 +314,7 @@
 
     wanted = kernel_call(
         turn_kernel,
+        "turn",
         4,
         out_shape=jax.ShapeDtypeStruct((slabs, 1, cap), jnp.int32),
         in_specs=[VMEM],
@@ -339,6 +324,7 @@
 
     own_rows = kernel_call(
         own_kernel,
+        "own",
         8,
         out_shape=jax.ShapeDtypeStruct((half // 2, blk_dev, 2 * LANES), BF16),
         in_specs=[VMEM],
@@ -347,6 +333,7 @@
 
     sent, hot = kernel_call(
         send_kernel,
+        "send",
         8,
         out_shape=(pltpu.HBM(wide.shape, BF16), jax.ShapeDtypeStruct((slots, blk_dev), BF16)),
         in_specs=[VMEM, VMEM],
@@ -355,8 +342,9 @@
     )(requested, own_rows)
     received = exchange(sent)
 
-    counts, counts_hi, counts_t, counts_t_hi, v2, vt, flag = kernel_call(
+    counts, counts_hi, counts_t, counts_t_hi, v2, vt, hot_t, flag = kernel_call(
         prep_kernel,
+        "prep",
         24,
         out_shape=(
             jax.ShapeDtypeStruct((keys, slots), BF16),
@@ -365,14 +353,16 @@
             jax.ShapeDtypeStruct((slots, keys), BF16),
             jax.ShapeDtypeStruct((nbat, half * kloc, 2 * npt), BF16),
             jax.ShapeDtypeStruct((nbat, kloc, npt, LANES), BF16),
+            jax.ShapeDtypeStruct((blk_dev, slots), BF16),
             jax.ShapeDtypeStruct((1, 1), jnp.int32),
         ),
-        in_specs=[SMEM, VMEM, VMEM],
-        out_specs=(VMEM,) * 6 + (SMEM,),
-    )(task_counts, tasks[0, 0], basis_vals)
+        in_specs=[SMEM, VMEM, VMEM, VMEM],
+        out_specs=(VMEM,) * 7 + (SMEM,),
+    )(task_counts, tasks[0, 0], basis_vals, hot)
 
     partial = kernel_call(
         density_kernel,
+        "density",
         16,
         out_shape=jax.ShapeDtypeStruct((nbat, npt), F32),
         in_specs=[SMEM, VMEM, VMEM, HBM, HBM, HBM],
@@ -390,30 +380,23 @@
 
     slot_sums, density = kernel_call(
         potential_kernel,
+        "potential",
         24,
-        out_shape=(pltpu.HBM(wide.shape, BF16), jax.ShapeDtypeStruct((nbat, npt), F32)),
+        out_shape=(wide, jax.ShapeDtypeStruct((nbat, npt), F32)),
         in_specs=[SMEM, VMEM, VMEM, VMEM, HBM, VMEM, VMEM],
-        out_specs=(HBM, VMEM),
+        out_specs=(VMEM, VMEM),
         scratch_shapes=[
             pltpu.VMEM((half, keys, LANES), BF16),
             pltpu.VMEM((nbat, 2 * npt), F32),
             pltpu.VMEM(counts_t.shape, BF16),
-            pltpu.VMEM(wide.shape, BF16),
             pltpu.SemaphoreType.DMA((1,)),
-            pltpu.SemaphoreType.DMA((4,)),
         ],
     )(flag, partial, other, counts_t, in_hbm(counts_t_hi), vt, v2)
     returned = exchange(slot_sums)
-    hot_t = kernel_call(
-        flip_kernel,
-        4,
-        out_shape=jax.ShapeDtypeStruct((blk_dev, slots), BF16),
-        in_specs=[VMEM],
-        out_specs=VMEM,
-    )(hot)
 
     owner_sums = kernel_call(
         owner_kernel,
+        "owner",
         8,
         out_shape=jax.ShapeDtypeStruct((blk_dev, bs, bs), F32),
         in_specs=[VMEM, VMEM],

time: 109 us -> 107 us (0.982)
  blocking collectives: 0 us -> 35.4 us
  waiting for transfers between devices: 62 us -> 30.7 us
  starting transfers between devices: 21.4 us -> 16.7 us
    all_to_all x0 -> x1, blocking collectives: none -> 35.4 us  [exchange(): return lax.all_to_all(x, 'slab', split_axis=0, concat_axis=0, tiled=True)]
    all_to_all x3 -> x2, waiting for transfers between devices: 60.8 us -> 29.5 us  [exchange(): return lax.all_to_all(x, 'slab', split_axis=0, concat_axis=0, tiled=True)]
    all_to_all x3 -> x2, starting transfers between devices: 21.3 us -> 16.6 us  [exchange(): return lax.all_to_all(x, 'slab', split_axis=0, concat_axis=0, tiled=True)]
    pallas_call x8 -> x7, Pallas kernels: 17.6 us -> 16.7 us  [the longest x1 5.41 us: body(): kernel_call(density_kernel, 'density', 16, out_shape=jax.ShapeDtypeStruct...]
  transfers between devices with their start and end apart: 4 -> 3, of which waited for: 4 -> 3; matrix products, arithmetic and copies ran while one was open for 0% -> 0% of each run, Pallas kernels for 2% -> 2%
where the time goes in v8:
time: 107 us
  blocking collectives  35.4 us (33%)
  waiting for transfers between devices  30.7 us (29%)
  Pallas kernels  16.7 us (16%)
  starting transfers between devices  16.7 us (16%)
  local copies, waits for them, and re-layouts  6.14 us (6%)
  between operations  1.41 us (1%)
    all_to_all x1, blocking collectives, exchange(): return lax.all_to_all(x, 'slab', split_axis=0, concat_axis=0, tiled=True)  35.4 us
    all_to_all x2, waiting for transfers between devices, exchange(): return lax.all_to_all(x, 'slab', split_axis=0, concat_axis=0, tiled=True)  29.5 us
    all_to_all x2, starting transfers between devices, exchange(): return lax.all_to_all(x, 'slab', split_axis=0, concat_axis=0, tiled=True)  16.6 us
    unnamed x24, local copies, waits for them, and re-layouts  6.14 us
    pallas_call x1, Pallas kernels, body(): kernel_call(density_kernel, 'density', 16, out_shape=jax.ShapeDtypeStruct...  5.41 us
    pallas_call x1, Pallas kernels, body(): kernel_call(potential_kernel, 'potential', 24, out_shape=(wide, jax.Shape...  4.37 us
    pallas_call x1, Pallas kernels, body(): kernel_call(prep_kernel, 'prep', 24, out_shape=(jax.ShapeDtypeStruct((key...  2.38 us
  transfers between devices with their start and end apart: 3, of which 3 were waited for; matrix products, arithmetic and copies ran while one was open for 0% of the time, Pallas kernels for 2%

profile of v8, /device:TPU:0, one launch (start us, length us, event | category | flops | bytes accessed | tf_op | source)
XLA Modules:
  0.0 107.1 jit_solution(8343693817112643495)
XLA Ops:
  0.6 0.7 copy-done.11
  1.3 0.7 turn.1
  2.0 11.5 %all-to-all-start = ((s32[64,1,4]{2,1,0:T(1,128)}), s32[64,1,4]{2,1,0:T(1,128)S(1)}, u32[]{:S(2)}, u32[]{:S(2)}) async-start(s32[64,1,4]{2,1,0:T(1,128)} %turn.1), calls=%async_computation | async-start | bytes 65536 | tf_op jit(solution)/shard_map/all_to_all | solution.py:302
  13.5 0.0 copy-start.5
  13.6 1.0 copy-done.5
  14.6 0.2 own.1.own_ref
  14.8 8.2 %all-to-all-done.req_ref = s32[64,1,4]{2,1,0:T(1,128)S(1)} async-done(((s32[64,1,4]{2,1,0:T(1,128)}), s32[64,1,4]{2,1,0:T(1,128)S(1)}, u32[]{:S(2)}, u32[]{:S(2)}) %all-to-all-start) | async-done | bytes 1056 | tf_op jit(solution)/shard_map/all_to_all | solution.py:302
  23.1 1.9 %send.1 = (bf16[64,32,4,128]{3,2,1,0:T(4,128)(2,1)}, bf16[256,32]{1,0:T(8,128)(2,1)S(1)}) custom-call(s32[64,1,4]{2,1,0:T(1,128)S(1)} %all-to-all-done.req_ref, bf16[16,32,256]{2,1,0:T(8,128)(2,1)S(1)} %own.1.own_ref), custom_call_target="tpu_custom_call" | custom-call | tf_op jit(solution)/shard_map/send/pallas_call | solution.py:334
  25.0 0.0 copy-start.10
  25.0 5.1 %all-to-all-start.1 = ((bf16[64,32,4,128]{3,2,1,0:T(4,128)(2,1)}), bf16[64,32,4,128]{3,2,1,0:T(4,128)(2,1)S(1)}, u32[]{:S(2)}, u32[]{:S(2)}) async-start(bf16[64,32,4,128]{3,2,1,0:T(4,128)(2,1)} %get-tuple-element.16), calls=%async_computation.1 | async-start | bytes 4194304 | tf_op jit(solution)/shard_map/all_to_all | solution.py:302
  30.8 2.4 %prep.1 = (bf16[512,256]{1,0:T(8,128)(2,1)S(1)}, bf16[512,256]{1,0:T(8,128)(2,1)S(1)}, bf16[256,512]{1,0:T(8,128)(2,1)S(1)}, bf16[256,512]{1,0:T(8,128)(2,1)S(1)...) custom-call(s32[1,1]{1,0:T(1,128)S(6)} %copy.7.count_ref, ...), custom_call_target="tpu_custom_call" | custom-call | tf_op jit(solution)/shard_map/prep/pallas_call | solution.py:345
  33.2 0.0 copy-start.1
  33.2 1.0 copy-done.1
  34.2 1.3 %copy-done.3 = bf16[8,8,128,128]{3,2,1,0:T(8,128)(2,1)} copy-done((bf16[8,8,128,128]{3,2,1,0:T(8,128)(2,1)}, bf16[8,8,128,128]{3,2,1,0:T(8,128)(2,1)S(1)}, u32[]{:S(2)}) %copy-start.3) | copy-done | bytes 2097176
  35.5 0.7 copy-done.6
  36.2 0.7 copy-done.7
  36.9 0.7 copy-done.9
  37.6 21.3 %all-to-all-done.1.r_ref = bf16[64,32,4,128]{3,2,1,0:T(4,128)(2,1)S(1)} async-done(((bf16[64,32,4,128]{3,2,1,0:T(4,128)(2,1)}), bf16[64,32,4,128]{3,2,1,0:T(4,128)(2,1)S(1)}, u32[]{:S(2)}, u32[]{:S(2)}) %all-to-all-start.1) | async-done | bytes 2097184 | tf_op jit(solution)/shard_map/all_to_all | solution.py:302
  58.9 5.4 %density.1.mine_ref = f32[8,128]{1,0:T(8,128)S(1)} custom-call(s32[1,1]{1,0:T(1,128)} %get-tuple-element.15.flag_ref, bf16[64,32,4,128]{3,2,1,0:T(4,128)(2,1)S(1)} %all-to-all-done.1.r_ref, bf16[512,256]{1,0:T(8,128)(2,1)S(1)} %get-tuple-element.17.c_ref, bf16[512,256]{1,0:T(8,128)(2,1)} %copy-done.6, bf16[8,8,64,128]{3,2,1,0:T(8,128)(2,1)} %v_hbm.1, ...), custom_call_target="tpu_custom_call" | custom-call | tf_op jit(solution)/shard_map/density/pallas_call | solution.py:363
  64.3 0.1 collective-permute-start
  64.4 1.2 %collective-permute-done.other_ref = f32[8,128]{1,0:T(8,128)S(1)} collective-permute-done((f32[8,128]{1,0:T(8,128)S(1)}, f32[8,128]{1,0:T(8,128)S(1)}, u32[]{:S(2)}, u32[]{:S(2)}) %collective-permute-start) | collective-permute-done | bytes 4128 | tf_op jit(solution)/shard_map/ppermute | solution.py:379
  65.6 4.4 %potential.1 = (bf16[64,32,4,128]{3,2,1,0:T(4,128)(2,1)S(1)}, f32[8,128]{1,0:T(8,128)}) custom-call(s32[1,1]{1,0:T(1,128)} %get-tuple-element.15.flag_ref, f32[8,128]{1,0:T(8,128)S(1)} %density.1.mine_ref, f32[8,128]{1,0:T(8,128)S(1)} %collective-permute-done.other_ref, bf16[256,512]{1,0:T(8,128)(2,1)S(1)} %copy-done.8, bf16[256,512]{1,0:T(8,128)(2,1)} %copy-done.9, ...), custom_call_target="tpu_custom_call" | custom-call | tf_op jit(solution)/shard_map/potential/pallas_call | solution.py:381
  70.0 35.4 %all_to_all.15.ret_ref = bf16[64,32,4,128]{3,2,1,0:T(4,128)(2,1)S(1)} all-to-all(bf16[64,32,4,128]{3,2,1,0:T(4,128)(2,1)S(1)} %get-tuple-element.25), channel_id=1, replica_groups=mesh['slab'=64,'blk'=2] {'slab'}, dimensions={0} | all-to-all | bytes 4194304 | tf_op jit(solution)/shard_map/all_to_all | solution.py:302
  105.4 1.7 %owner.1 = f32[32,64,64]{2,1,0:T(8,128)} custom-call(bf16[32,256]{1,0:T(8,128)(2,1)S(1)} %get-tuple-element.24.hot_ref, bf16[64,32,4,128]{3,2,1,0:T(4,128)(2,1)S(1)} %all_to_all.15.ret_ref), custom_call_target="tpu_custom_call" | custom-call | tf_op jit(solution)/shard_map/owner/pallas_call | solution.py:397
  (14 shorter events, 0.0 us)
Async XLA Ops:
  0.6 0.7 copy-start.11
  2.0 21.0 %all-to-all-start = ((s32[64,1,4]{2,1,0:T(1,128)}), s32[64,1,4]{2,1,0:T(1,128)S(1)}, u32[]{:S(2)}, u32[]{:S(2)}) async-start(s32[64,1,4]{2,1,0:T(1,128)} %turn.1), calls=%async_computation | async-start | bytes 65536 | tf_op jit(solution)/shard_map/all_to_all | solution.py:302
  13.5 1.0 copy-start.5
  25.0 5.8 %copy-start = (bf16[8,8,64,128]{3,2,1,0:T(8,128)(2,1)S(1)}, bf16[8,8,64,128]{3,2,1,0:T(8,128)(2,1)}, u32[]{:S(2)}) copy-start(bf16[8,8,64,128]{3,2,1,0:T(8,128)(2,1)} %v_hbm.1) | copy-start | bytes 3145732
  25.0 5.8 %copy-start.10 = (s32[1,1,4,1536]{3,2,1,0:T(4,128)S(1)}, s32[1,1,4,1536]{3,2,1,0:T(4,128)}, u32[]{:S(2)}) copy-start(s32[1,1,4,1536]{3,2,1,0:T(4,128)} %param.8) | copy-start | bytes 73732
  25.0 33.9 %all-to-all-start.1 = ((bf16[64,32,4,128]{3,2,1,0:T(4,128)(2,1)}), bf16[64,32,4,128]{3,2,1,0:T(4,128)(2,1)S(1)}, u32[]{:S(2)}, u32[]{:S(2)}) async-start(bf16[64,32,4,128]{3,2,1,0:T(4,128)(2,1)} %get-tuple-element.16), calls=%async_computation.1 | async-start | bytes 4194304 | tf_op jit(solution)/shard_map/all_to_all | solution.py:302
  33.2 1.0 copy-start.1
  34.2 1.3 %copy-start.3 = (bf16[8,8,128,128]{3,2,1,0:T(8,128)(2,1)}, bf16[8,8,128,128]{3,2,1,0:T(8,128)(2,1)S(1)}, u32[]{:S(2)}) copy-start(bf16[8,8,128,128]{3,2,1,0:T(8,128)(2,1)S(1)} %get-tuple-element.22.vt_ref) | copy-start | bytes 6291460
  35.5 0.7 copy-start.6
  36.2 0.7 copy-start.7
  36.9 0.7 copy-start.9
  58.9 6.7 %copy-start.2 = (bf16[8,256,256]{2,1,0:T(8,128)(2,1)S(1)}, bf16[8,256,256]{2,1,0:T(8,128)(2,1)}, u32[]{:S(2)}) copy-start(bf16[8,256,256]{2,1,0:T(8,128)(2,1)} %copy-done.1) | copy-start | bytes 3145732
  58.9 6.7 %copy-start.4 = (bf16[8,8,128,128]{3,2,1,0:T(8,128)(2,1)S(1)}, bf16[8,8,128,128]{3,2,1,0:T(8,128)(2,1)}, u32[]{:S(2)}) copy-start(bf16[8,8,128,128]{3,2,1,0:T(8,128)(2,1)} %copy-done.3) | copy-start | bytes 6291460
  58.9 6.7 %copy-start.8 = (bf16[256,512]{1,0:T(8,128)(2,1)S(1)}, bf16[256,512]{1,0:T(8,128)(2,1)}, u32[]{:S(2)}) copy-start(bf16[256,512]{1,0:T(8,128)(2,1)} %copy-done.7) | copy-start | bytes 786436
  64.3 1.2 %collective-permute-start = (f32[8,128]{1,0:T(8,128)S(1)}, f32[8,128]{1,0:T(8,128)S(1)}, u32[]{:S(2)}, u32[]{:S(2)}) collective-permute-start(f32[8,128]{1,0:T(8,128)S(1)} %density.1.mine_ref), channel_id=1, source_target_pairs={{0,1},{1,0},{2,3},{3,2},{4,5},{5,4},{6,7},{7,6},{8,9},{9,8},{10,11... | collective-permute-start | bytes 12296 | tf_op jit(solution)/shard_map/ppermute | solution.py:379
